TPU v7x, 128 devices: a whole 4x4x4 slice. The times are simulated.
128 devices in a mesh: ctx: 16 (over z, y_lo, core), head: 8 (over x, y_hi).
Axes of the slice: x: 4, y: 4 (y_hi: 2, y_lo: 2; y = y_hi * 2 + y_lo), z: 4, core: 2. Of those that a mesh axis runs over, the one named last changes fastest.
Arguments:
- hidden: bfloat16 [8192, 4096], P('ctx'), may hold values from -6 to 6
- base_ids: int32 [8192], P('ctx'), may hold values from 0 to 4
- norm_gain: float32 [4096], replicated, may hold values from 0.1 to 1.9
- w_gate: bfloat16 [4096, 4096], P(None, 'head'), may hold values from -0.09375 to 0.09375
- w_value: bfloat16 [4096, 4096], P(None, 'head'), may hold values from -0.09375 to 0.09375
- w_bc: bfloat16 [4096, 256], replicated, may hold values from -0.09375 to 0.09375
- w_step: bfloat16 [4096, 64], P(None, 'head'), may hold values from -0.09375 to 0.09375
- conv_value: float32 [4, 4096], P(None, 'head'), may hold values from -3 to 3
- conv_bc: float32 [4, 256], replicated, may hold values from -3 to 3
- step_bias: float32 [64], P('head'), may hold values from -5.5 to -3.5
- decay_rate: float32 [64], P('head'), as said below
- skip_gain: float32 [64], P('head'), may hold values from 0.5 to 1.5
- out_gain: float32 [4096], P('head'), may hold values from 0.1 to 1.9
- w_out: bfloat16 [4096, 4096], P('head'), may hold values from -0.09375 to 0.09375
Outputs:
- mixed_out: bfloat16 [8192, 4096], P('ctx', 'head')
Inputs may be any that keep to these rules, and one draw needn't show every extreme that they name: `base_ids`: 4 marks an unknown base N, 0 to 3 are A, C, G, T. `decay_rate`: positive rates.
All inputs are finite; a program needn't handle non-finite values.
Results may differ from a plain program's by a relative error of at most 0.0059.
Values may be sent and summed in bfloat16 or wider, within the bound.
No kernel may reach another device: no remote copies, remote signals or barrier semaphores. Data moves between devices by JAX's collectives and lax.ppermute only.
A program may use at most 192 MiB of HBM per device.

v0:
```python
import jax
import jax.numpy as jnp
from jax import lax
from jax.sharding import PartitionSpec as P

CONV_WIDTH = 4
BLOCK = 256


EPSILON = 1e-05
PRECISE = lax.Precision.HIGHEST


def swapped(array, axis, stride):
    return lax.ppermute(array, axis, [(i, i ^ 1 << stride) for i in range(lax.axis_size(axis))])


def padded_2(array, sides, width):
    for axis, dim in sides:
        size, length = (lax.axis_size(axis), array.shape[dim])
        up = [(i, (i + 1) % size) for i in range(size - 1)]
        down = [(j, i) for i, j in up]
        last = lax.slice_in_dim(array, length - width, length, axis=dim)
        initial = lax.slice_in_dim(array, 0, width, axis=dim)
        before = lax.ppermute(last, axis, up)
        after = lax.ppermute(initial, axis, down)
        array = jnp.concatenate([before, array, after], axis=dim)
    return array


def prefix(part, axis, combine, identity, reverse):
    count = lax.axis_size(axis)
    place = lax.axis_index(axis)
    ahead = count - 1 - place if reverse else place
    gathered = jax.tree.map(lambda a: lax.all_gather(a, axis), part)
    state = jax.tree.map(lambda a, e: jnp.zeros_like(a) + jnp.asarray(e, a.dtype), part, identity)

    def one(lap, state):
        source = count - 1 - lap if reverse else lap
        return combine(
            state, jax.tree.map(lambda a: lax.dynamic_index_in_dim(a, source, 0, False), gathered)
        )

    return lax.fori_loop(0, ahead, one, state)


def convolve(padded, kernel, kernel_len):
    length = padded.shape[1] - 2 * (kernel_len - 1)
    reach = 2 * (kernel_len - 1)
    forward_sum = kernel[0] * padded[:, 0:length]
    backward_sum = kernel[0] * padded[:, reach : reach + length]
    for offset in range(1, kernel_len):
        forward_sum = forward_sum + kernel[offset] * padded[:, offset : offset + length]
        backward_sum = (
            backward_sum + kernel[offset] * padded[:, reach - offset : reach - offset + length]
        )
    return (forward_sum, backward_sum)


def lane_flip(source_array):
    return jnp.concatenate([source_array[:2], source_array[2:, ::-1]], axis=0)


def local_scan(values, inputs_b, inputs_c, steps, log_decay):
    lane_total, length, heads_dev, head_width = values.shape
    state_dim = inputs_b.shape[-1]
    block_total = length // BLOCK

    def blocked(source_array):
        return source_array.reshape((lane_total, block_total, BLOCK) + source_array.shape[2:])

    value_blocks = blocked(values)
    b_rows = blocked(inputs_b)
    c_rows = blocked(inputs_c)
    step_blocks = blocked(steps)
    cumulative = jnp.cumsum(blocked(log_decay), axis=2)
    scores = jnp.einsum("gbtn,gbsn->gbts", c_rows, b_rows, precision=PRECISE)
    gaps = cumulative[:, :, :, None, :] - cumulative[:, :, None, :, :]
    causal = jnp.arange(BLOCK)[:, None] >= jnp.arange(BLOCK)[None, :]
    weights = (
        jnp.exp(jnp.where(causal[:, :, None], gaps, -jnp.inf))
        * scores[..., None]
        * step_blocks[:, :, None, :, :]
    )
    within = jnp.einsum("gbtsh,gbshp->gbthp", weights, value_blocks, precision=PRECISE)
    tail_weight = jnp.exp(cumulative[:, :, -1:, :] - cumulative) * step_blocks
    block_states = jnp.einsum(
        "gbsh,gbsn,gbshp->gbhpn", tail_weight, b_rows, value_blocks, precision=PRECISE
    )
    block_decay = cumulative[:, :, -1, :]

    def advance(state_carry, block_item):
        return (jnp.exp(block_item[0])[..., None, None] * state_carry + block_item[1], state_carry)

    start_state = jnp.zeros((lane_total, heads_dev, head_width, state_dim), jnp.float32)
    final_state, entering = lax.scan(
        advance, start_state, (jnp.moveaxis(block_decay, 1, 0), jnp.moveaxis(block_states, 1, 0))
    )
    entering = jnp.moveaxis(entering, 0, 1)
    across = jnp.exp(cumulative)[..., None] * jnp.einsum(
        "gbtn,gbhpn->gbthp", c_rows, entering, precision=PRECISE
    )
    local_out = (within + across).reshape(values.shape)
    run_decay = jnp.cumsum(log_decay, axis=1)
    return (local_out, run_decay, jnp.sum(block_decay, axis=1), final_state)


def combine_states(earlier, later):
    return (earlier[0] + later[0], jnp.exp(later[0])[..., None, None] * earlier[1] + later[1])


def shards(
    hidden,
    base_ids,
    norm_gain,
    w_gate,
    w_value,
    w_bc,
    w_step,
    conv_value,
    conv_bc,
    step_bias,
    decay_rate,
    skip_gain,
    out_gain,
    w_out,
):
    keep_own = (base_ids != 4).astype(jnp.float32)
    bit_total = lax.axis_size("ctx").bit_length() - 1
    partner = (hidden, base_ids)
    for bit_pos in range(bit_total):
        partner = swapped((partner[0], partner[1]), "ctx", bit_pos)
    other_rows = partner[0][::-1, ::-1]
    other_keep = (partner[1][::-1] != 4).astype(jnp.float32)
    branches = jnp.stack([hidden, other_rows])
    keep_both = jnp.stack([keep_own, other_keep])
    inv_rms = lax.rsqrt(jnp.mean(jnp.square(branches.astype(jnp.float32)), axis=-1) + EPSILON)
    scaled = (branches * norm_gain).astype(jnp.bfloat16)

    def project(weight):
        return (
            jnp.einsum("btd,dk->btk", scaled, weight, preferred_element_type=jnp.float32)
            * inv_rms[..., None]
        )

    gate_in = project(w_gate)
    value_in = project(w_value)
    bc_in = project(w_bc)
    step_in = project(w_step)
    heads_dev = w_step.shape[1]
    inner_dev = w_gate.shape[1]
    head_width = inner_dev // heads_dev
    state_dim = w_bc.shape[1] // 2
    length = hidden.shape[0]
    mixed_in = jnp.concatenate([value_in, bc_in], axis=-1)
    padded = padded_2(mixed_in, (("ctx", 1),), CONV_WIDTH - 1)
    kernel = jnp.concatenate([conv_value, conv_bc], axis=-1)
    forward_mix, backward_mix = convolve(padded, kernel, CONV_WIDTH)
    lane_mix = jax.nn.silu(jnp.concatenate([forward_mix, backward_mix], axis=0))
    keep_lanes = jnp.concatenate([keep_both, keep_both], axis=0)
    values = (lane_mix[..., :inner_dev] * keep_lanes[..., None]).reshape(
        4, length, heads_dev, head_width
    )
    inputs_b = lane_mix[..., inner_dev : inner_dev + state_dim]
    inputs_c = lane_mix[..., inner_dev + state_dim :]
    steps = jax.nn.softplus(step_in + step_bias)
    log_decay = -decay_rate * steps
    steps_lanes = jnp.concatenate([steps, steps], axis=0)
    decay_lanes = jnp.concatenate([log_decay, log_decay], axis=0)
    values = lane_flip(values)
    inputs_b = lane_flip(inputs_b)
    inputs_c = lane_flip(inputs_c)
    local_out, run_decay, device_decay, final_state = local_scan(
        values, inputs_b, inputs_c, lane_flip(steps_lanes), lane_flip(decay_lanes)
    )
    zero_decay = jnp.zeros((2, heads_dev), jnp.float32)
    zero_state = jnp.zeros((2, heads_dev, head_width, state_dim), jnp.float32)
    upward = prefix(
        (device_decay[:2], final_state[:2]), "ctx", combine_states, (zero_decay, zero_state), False
    )
    downward = prefix(
        (device_decay[2:], final_state[2:]), "ctx", combine_states, (zero_decay, zero_state), True
    )
    incoming = jnp.concatenate([upward[1], downward[1]], axis=0)
    chain_part = jnp.exp(run_decay)[..., None] * jnp.einsum(
        "gtn,ghpn->gthp", inputs_c, incoming, precision=PRECISE
    )
    lane_out = lane_flip(local_out + chain_part + skip_gain[:, None] * values)
    summed = lane_out[:2] + lane_out[2:]
    gated = summed * jax.nn.silu(gate_in).reshape(2, length, heads_dev, head_width)
    normed = (
        gated
        * lax.rsqrt(jnp.mean(jnp.square(gated), axis=-1, keepdims=True) + EPSILON)
        * out_gain.reshape(heads_dev, head_width)
    ).astype(jnp.bfloat16)
    term = jnp.einsum(
        "gtk,kd->gtd",
        normed.reshape(2, length, inner_dev),
        w_out,
        preferred_element_type=jnp.float32,
    )
    own_part, other_part = (
        lax.psum_scatter(term[0], "head", scatter_dimension=1, tiled=True),
        lax.psum_scatter(term[1][::-1, ::-1], "head", scatter_dimension=1, tiled=True),
    )
    for bit_pos in range(bit_total):
        other_part = swapped(other_part, "ctx", bit_pos)
    total = own_part + other_part
    return total.astype(jnp.bfloat16)


def solution(mesh):
    return jax.shard_map(
        shards,
        mesh=mesh,
        in_specs=(
            P("ctx", None),
            P("ctx"),
            P(),
            P(None, "head"),
            P(None, "head"),
            P(),
            P(None, "head"),
            P(None, "head"),
            P(),
            P("head"),
            P("head"),
            P("head"),
            P("head"),
            P("head", None),
        ),
        out_specs=P("ctx", "head"),
        check_vma=False,
    )
```

profile of v0, /device:TPU:0, one launch (start us, length us, event | category | flops | bytes accessed | tf_op | source)
XLA Modules:
  0.0 936.3 jit_solution(7947794349656516027)
XLA Ops:
  6.5 7.4 collective-permute-done
  15.6 91.0 %collective-permute-done.1 = bf16[512,4096]{1,0:T(8,128)(2,1)S(1)} collective-permute-done((bf16[512,4096]{1,0:T(8,128)(2,1)S(1)}, bf16[512,4096]{1,0:T(8,128)(2,1)S(1)}, u32[]{:S(2)}, u32[]{:S(2)}) %collective-permute-start.1) | collective-permute-done | bytes 4194336 | tf_op jit(solution)/shard_map/ppermute | solution.py:15
  108.5 90.1 %collective-permute-done.2 = bf16[512,4096]{1,0:T(8,128)(2,1)} collective-permute-done((bf16[512,4096]{1,0:T(8,128)(2,1)S(1)}, bf16[512,4096]{1,0:T(8,128)(2,1)}, u32[]{:S(2)}, u32[]{:S(2)}) %collective-permute-start.2) | collective-permute-done | bytes 4194336 | tf_op jit(solution)/shard_map/ppermute | solution.py:15
  209.0 83.5 %collective-permute-done.8 = s32[512]{0:T(512)S(1)} collective-permute-done((s32[512]{0:T(512)S(1)}, s32[512]{0:T(512)S(1)}, u32[]{:S(2)}, u32[]{:S(2)}) %collective-permute-start.8) | collective-permute-done | bytes 2080 | tf_op jit(solution)/shard_map/ppermute | solution.py:15
  298.0 63.2 %rev.27 = bf16[512,4096]{1,0:T(8,128)(2,1)} reverse(bf16[512,4096]{1,0:T(8,128)(2,1)} %collective-permute-done.3), dimensions={0,1} | reverse | bytes 8388608 | tf_op jit(solution)/shard_map/rev | solution.py:133
  361.2 5.7 fusion.1
  375.8 5.0 fusion.47
  382.9 4.7 fusion.42
  403.7 4.9 fusion.29
  417.3 4.7 fusion.78
  424.7 5.2 rev.31
  456.9 19.4 %all-gather.4 = f32[16,2,8]{2,1,0:T(2,128)S(1)} all-gather(f32[1,2,8]{2,1,0:T(2,128)S(1)} %get-tuple-element.259), channel_id=2, replica_groups=mesh['ctx'=16,'head'=8] {'ctx'}, dimensions={0}, use_global_device_ids=true | all-gather | bytes 1088 | tf_op jit(solution)/shard_map/all_gather | solution.py:35
  476.2 16.7 %all-gather.5 = f32[16,2,8]{2,1,0:T(2,128)S(1)} all-gather(f32[1,2,8]{2,1,0:T(2,128)S(1)} %get-tuple-element.260), channel_id=4, replica_groups=mesh['ctx'=16,'head'=8] {'ctx'}, dimensions={0}, use_global_device_ids=true | all-gather | bytes 1088 | tf_op jit(solution)/shard_map/all_gather | solution.py:35
  499.2 19.1 %fusion.19 = f32[4,2,8,8,8,256]{5,4,3,2,1,0:T(8,128)S(1)} fusion(f32[4,2,256,8,64]{2,4,3,1,0:T(8,128)S(1)} %fusion.36, f32[4,2,256,8,64]{2,4,3,1,0:T(8,128)S(1)} %copy-done.8, f32[4,2,256,8]{2,3,1,0:T(8,128)S(1)} %bitcast.162, f32[4,2,256,256]{3,2,1,0:T(8,128)S(1)} %fusion.51, f32[4,2,256,8]{2,3,1,0:T(8,128)S(1)} %get-tuple-element.240, ...), kind=kOutput, calls=%fused_computation.40 | convolution fusion | flops 3240099840 | bytes 14942208 | tf_op jit(solution)/shard_map/gbtsh,gbshp->gbthp/dot_general | solution.py:85
  521.0 39.7 %all-gather.11.cloned.1.call-done = f32[32,8,64,128]{3,2,1,0:T(8,128)} async-done(((f32[2,8,64,128]{3,2,1,0:T(8,128)}), f32[32,8,64,128]{3,2,1,0:T(8,128)}) %all-gather.11.cloned.1.call-update) | async-done | bytes 8388624 | tf_op jit(solution)/shard_map/all_gather | solution.py:35
  560.7 18.7 %while.40 = (s32[]{:T(128)}, f32[2,8,64,128]{3,2,1,0:T(8,128)S(1)}, s32[]{:T(128)}, f32[16,2,8]{2,1,0:T(2,128)S(1)}, f32[16,2,8,64,128]{4,3,2,1,0:T(8,128)}, /*index=5*/s32[]{:T(128)}, s32[]{:T(128)}, s32[]{:T(128)}, s32[]{:T(128)}) while((s32[]{:T(128)}, f32[2,8,64,128]{3,2,1,0:T(8,128)S(1)}, s32[]{:T(128)}, f32[16,2,8]{2,1,0:T(2,128)S(1)}, ...), condition=%wide.region_11.12_spmd, body=%wide.region_10.11_spmd.sunk | while | flops 262150 | bytes 1573211 | solution.py:44
  579.5 6.6 fusion.14
  592.4 9.9 %multiply_reduce_fusion = (f32[2,512,8]{1,2,0:T(8,128)S(1)}, f32[2,512,512]{1,2,0:T(8,128)S(1)}) fusion(f32[2,512,8,64]{1,3,2,0:T(8,128)S(1)} %rev.34, f32[4,512,8,64]{1,3,2,0:T(8,128)} %copy-done.3, f32[2,512]{1,0:T(2,128)S(1)} %copy-done.24, bf16[4096,512]{1,0:T(8,128)(2,1)} %param.23, f32[4096]{0:T(1024)S(1)} %copy-done.30, ...), kind=kOutput, calls=%fused_computation.71 | convolution fusion | flops 4316454912 | bytes 18927616 | tf_op jit(solution)/shard_map/btd,dk->btk/dot_general | solution.py:142
  609.2 6.4 slice_bitcast_fusion
  615.6 67.7 %rev.35 = f32[512,4096]{1,0:T(8,128)} reverse(f32[512,4096]{1,0:T(8,128)} %get-tuple-element.241), dimensions={0,1} | reverse | bytes 16777216 | tf_op jit(solution)/shard_map/rev | solution.py:204
  683.9 113.2 %reduce-scatter.5.cloned.1.call-done = f32[512,512]{1,0:T(8,128)} async-done(((f32[512,4096]{1,0:T(8,128)}), f32[512,512]{1,0:T(8,128)}) %reduce-scatter.5.cloned.1.call-update) | async-done | bytes 1048592 | tf_op jit(solution)/shard_map/reduce_scatter | solution.py:204
  800.6 35.9 %collective-permute-done.11 = f32[512,512]{1,0:T(8,128)S(1)} collective-permute-done((f32[512,512]{1,0:T(8,128)S(1)}, f32[512,512]{1,0:T(8,128)S(1)}, u32[]{:S(2)}, u32[]{:S(2)}) %collective-permute-start.11) | collective-permute-done | bytes 1048608 | tf_op jit(solution)/shard_map/ppermute | solution.py:15
  838.0 22.9 %collective-permute-done.12 = f32[512,512]{1,0:T(8,128)} collective-permute-done((f32[512,512]{1,0:T(8,128)S(1)}, f32[512,512]{1,0:T(8,128)}, u32[]{:S(2)}, u32[]{:S(2)}) %collective-permute-start.12) | collective-permute-done | bytes 1048608 | tf_op jit(solution)/shard_map/ppermute | solution.py:15
  864.1 63.3 %reduce-scatter.3.cloned.1.call-done = f32[512,512]{1,0:T(8,128)} async-done(((f32[512,4096]{1,0:T(8,128)}), f32[512,512]{1,0:T(8,128)}) %reduce-scatter.3.cloned.1.call-update) | async-done | bytes 1048592 | tf_op jit(solution)/shard_map/reduce_scatter | solution.py:203
  (199 shorter events, 138.0 us)
Async XLA Ops:
  6.5 369.3 %copy-start = (bf16[4096,256]{1,0:T(8,128)(2,1)S(1)}, bf16[4096,256]{1,0:T(8,128)(2,1)}, u32[]{:S(2)}) copy-start(bf16[4096,256]{1,0:T(8,128)(2,1)} %param.25) | copy-start | bytes 6291460
  6.5 514.4 %all-gather.9.cloned.1.call-start = ((), (), s32[]{:S(2)}) async-start(), calls=%async_computation.4 | async-start | bytes 8912896 | tf_op jit(solution)/shard_map/all_gather | solution.py:35
  6.5 7.4 collective-permute-start
  13.9 92.6 %collective-permute-start.1 = (bf16[512,4096]{1,0:T(8,128)(2,1)S(1)}, bf16[512,4096]{1,0:T(8,128)(2,1)S(1)}, u32[]{:S(2)}, u32[]{:S(2)}) collective-permute-start(bf16[512,4096]{1,0:T(8,128)(2,1)S(1)} %collective-permute-done), channel_id=1, source_target_pairs={{0,16},{8,24},{16,0},{24,8},{32,48},{40,56},{48,32},{56,40},{64,80... | collective-permute-start | bytes 12582920 | tf_op jit(solution)/shard_map/ppermute | solution.py:15
  106.5 92.1 %collective-permute-start.2 = (bf16[512,4096]{1,0:T(8,128)(2,1)S(1)}, bf16[512,4096]{1,0:T(8,128)(2,1)}, u32[]{:S(2)}, u32[]{:S(2)}) collective-permute-start(bf16[512,4096]{1,0:T(8,128)(2,1)S(1)} %collective-permute-done.1), channel_id=1, source_target_pairs={{0,32},{8,40},{16,48},{24,56},{32,0},{40,8},{48,16},{56,24},{64,96... | collective-permute-start | bytes 12582920 | tf_op jit(solution)/shard_map/ppermute | solution.py:15
  198.7 99.3 %collective-permute-start.3 = (bf16[512,4096]{1,0:T(8,128)(2,1)}, bf16[512,4096]{1,0:T(8,128)(2,1)}, u32[]{:S(2)}, u32[]{:S(2)}) collective-permute-start(bf16[512,4096]{1,0:T(8,128)(2,1)} %collective-permute-done.2), channel_id=1, source_target_pairs={{0,64},{8,72},{16,80},{24,88},{32,96},{40,104},{48,112},{56,120},{... | collective-permute-start | bytes 12582920 | tf_op jit(solution)/shard_map/ppermute | solution.py:15
  202.4 1.4 collective-permute-start.6
  203.7 3.6 collective-permute-start.7
  207.3 85.2 %collective-permute-start.8 = (s32[512]{0:T(512)S(1)}, s32[512]{0:T(512)S(1)}, u32[]{:S(2)}, u32[]{:S(2)}) collective-permute-start(s32[512]{0:T(512)S(1)} %collective-permute-done.7), channel_id=1, source_target_pairs={{0,32},{8,40},{16,48},{24,56},{32,0},{40,8},{48,16},{56,24},{64,96... | collective-permute-start | bytes 6152 | tf_op jit(solution)/shard_map/ppermute | solution.py:15
  292.5 5.3 collective-permute-start.9
  297.9 68.9 %copy-start.28 = (bf16[4096,8]{0,1:T(8,128)(2,1)S(1)}, bf16[4096,8]{0,1:T(8,128)(2,1)}, u32[]{:S(2)}) copy-start(bf16[4096,8]{0,1:T(8,128)(2,1)} %param.26) | copy-start | bytes 196612
  297.9 68.9 %copy-start.29 = (f32[4096]{0:T(1024)S(1)}, f32[4096]{0:T(1024)}, u32[]{:S(2)}) copy-start(f32[4096]{0:T(1024)} %param.22) | copy-start | bytes 49156
  391.9 7.2 collective-permute-start.5
  393.2 4.0 collective-permute-start.4
  450.1 43.0 %copy-start.11 = (f32[4,512,128]{1,2,0:T(8,128)S(1)}, f32[4,512,128]{1,2,0:T(8,128)}, u32[]{:S(2)}) copy-start(f32[4,512,128]{1,2,0:T(8,128)} %get-tuple-element.266) | copy-start | bytes 3145732
  450.1 43.7 %copy-start.12 = (f32[4,512,128]{1,2,0:T(8,128)S(1)}, f32[4,512,128]{1,2,0:T(8,128)}, u32[]{:S(2)}) copy-start(f32[4,512,128]{1,2,0:T(8,128)} %get-tuple-element.267) | copy-start | bytes 3145732
  451.2 109.5 %all-gather.11.cloned.1.call-start = ((), (), s32[]{:S(2)}) async-start(), calls=%async_computation.5 | async-start | bytes 8912896 | tf_op jit(solution)/shard_map/all_gather | solution.py:35
  451.9 345.2 %reduce-scatter.5.cloned.1.call-start = ((), (), s32[]{:S(2)}) async-start(), calls=%async_computation.3 | async-start | bytes 9437184 | tf_op jit(solution)/shard_map/reduce_scatter | solution.py:204
  683.3 244.1 %reduce-scatter.3.cloned.1.call-start = ((), (), s32[]{:S(2)}) async-start(), calls=%async_computation.2 | async-start | bytes 9437184 | tf_op jit(solution)/shard_map/reduce_scatter | solution.py:203
  683.4 246.2 %copy-start.1 = (bf16[4096,256]{1,0:T(8,128)(2,1)S(1)}, bf16[4096,256]{1,0:T(8,128)(2,1)}, u32[]{:S(2)}) copy-start(bf16[4096,256]{1,0:T(8,128)(2,1)} %param.25) | copy-start | bytes 6291460
  797.1 2.9 collective-permute-start.10
  800.0 36.4 %collective-permute-start.11 = (f32[512,512]{1,0:T(8,128)S(1)}, f32[512,512]{1,0:T(8,128)S(1)}, u32[]{:S(2)}, u32[]{:S(2)}) collective-permute-start(f32[512,512]{1,0:T(8,128)S(1)} %collective-permute-done.10), channel_id=1, source_target_pairs={{0,16},{8,24},{16,0},{24,8},{32,48},{40,56},{48,32},{56,40},{64,80... | collective-permute-start | bytes 3145736 | tf_op jit(solution)/shard_map/ppermute | solution.py:15
  836.4 24.5 %collective-permute-start.12 = (f32[512,512]{1,0:T(8,128)S(1)}, f32[512,512]{1,0:T(8,128)}, u32[]{:S(2)}, u32[]{:S(2)}) collective-permute-start(f32[512,512]{1,0:T(8,128)S(1)} %collective-permute-done.11), channel_id=1, source_target_pairs={{0,32},{8,40},{16,48},{24,56},{32,0},{40,8},{48,16},{56,24},{64,96... | collective-permute-start | bytes 3145736 | tf_op jit(solution)/shard_map/ppermute | solution.py:15
  860.9 66.5 %collective-permute-start.13 = (f32[512,512]{1,0:T(8,128)}, f32[512,512]{1,0:T(8,128)S(1)}, u32[]{:S(2)}, u32[]{:S(2)}) collective-permute-start(f32[512,512]{1,0:T(8,128)} %collective-permute-done.12), channel_id=1, source_target_pairs={{0,64},{8,72},{16,80},{24,88},{32,96},{40,104},{48,112},{56,120},{... | collective-permute-start | bytes 3145736 | tf_op jit(solution)/shard_map/ppermute | solution.py:15
  (26 other events, 185.7 us)
Sparse Core Ops, SparseCore 0:
  451.3 54.5 all-gather.8
  507.6 53.0 all-gather.10
  683.4 113.6 reduce-scatter.4
  800.9 126.4 reduce-scatter.2
where the time goes:
time: 953 us; the launch traced here: 936 us
  waiting for transfers between devices  556 us (58%)
  local copies, waits for them, and re-layouts  189 us (20%)
  matrix products  61.5 us (6%)
  other arithmetic  57.5 us (6%)
  blocking collectives  36.1 us (4%)
  starting transfers between devices  21.9 us (2%)
  between operations  13.9 us (1%)
    ppermute x12, waiting for transfers between devices, swapped(): lax.ppermute(array, axis, [(i, i ^ 1 << stride) for i in range(lax.axis_s...  338 us
    reduce_scatter x1, waiting for transfers between devices, shards(): lax.psum_scatter(term[1][::-1, ::-1], 'head', scatter_dimension=1, tiled=...  113 us
    rev x1, local copies, waits for them, and re-layouts, shards(): term[1][::-1, ::-1]  67.7 us
    reduce_scatter x1, waiting for transfers between devices, shards(): lax.psum_scatter(term[0], 'head', scatter_dimension=1, tiled=True)  63.3 us
    rev x1, local copies, waits for them, and re-layouts, shards(): other_rows = partner[0][::-1, ::-1]  63.2 us
    all_gather x2, waiting for transfers between devices, prefix(): gathered = jax.tree.map(lambda a: lax.all_gather(a, axis), part)  39.7 us
    all_gather x2, blocking collectives, prefix(): gathered = jax.tree.map(lambda a: lax.all_gather(a, axis), part)  36.1 us
    dot_general x4, matrix products, project(): jnp.einsum('btd,dk->btk', scaled, weight, preferred_element_type=jnp.floa...  21.9 us
  transfers between devices with their start and end apart: 18, of which 13 were waited for; matrix products, arithmetic and copies ran while one was open for 4% of the time, Pallas kernels for 0%

commit v1 on v0

v1 whole, which is shorter than its diff:
```python
import functools

import jax
import jax.numpy as jnp
from jax import lax
from jax.experimental import pallas as pl
from jax.experimental.pallas import tpu as pltpu
from jax.sharding import PartitionSpec as P

EPSILON = 1e-05
HALO = 8
CHUNK = 128
TILE = 128
FLIP = 256
ROWS = 64
BF16 = jnp.bfloat16
F32 = jnp.float32
NT = (((1,), (1,)), ((), ()))
TN = (((0,), (0,)), ((), ()))


def params(megabytes, dims=1):
    return pltpu.CompilerParams(
        dimension_semantics=("arbitrary",) * dims, vmem_limit_bytes=megabytes << 20
    )


def iota(shape, dim):
    return lax.broadcasted_iota(jnp.int32, shape, dim)


def dot(a, b):
    return jnp.dot(a, b, preferred_element_type=F32)


def reversal(width):
    where = iota((width, width), 0) + iota((width, width), 1) == width - 1
    return jnp.where(where, 1.0, 0.0).astype(BF16)


def spreader(heads, width):
    shape = (heads, heads * width)
    return jnp.where(iota(shape, 1) // width == iota(shape, 0), 1.0, 0.0).astype(BF16)


def spread(columns, matrix):
    high = columns.astype(BF16)
    low = (columns - high.astype(F32)).astype(BF16)
    return dot(high, matrix) + dot(low, matrix)


def silu(x):
    return x / (1.0 + jnp.exp(-x))


def scale_rows(source, begin, gain, xs, squares):
    depth = source.shape[1]
    step = min(source.shape[0], TILE)
    for r in range(0, source.shape[0], step):
        x = source[r : r + step, :].astype(F32)
        xs[begin + r : begin + r + step, :] = (x * gain).astype(BF16)
        square = x * x
        partial = square[:, :TILE]
        for c in range(TILE, depth, TILE):
            partial = partial + square[:, c : c + TILE]
        squares[begin + r : begin + r + step, :] += partial


def scale_mirrored(source, begin, gain, xs):
    size, depth = source.shape
    flip = reversal(FLIP)
    for i in range(depth // FLIP):
        at = depth - (i + 1) * FLIP
        lanes = slice(i * FLIP, (i + 1) * FLIP)
        x = dot(source[:, at : at + FLIP], flip)
        xs[begin : begin + size, lanes] = (x * gain[:, lanes]).astype(BF16)


def multiply(xs, accs, weights, splits):
    part = xs.shape[0] // splits

    def body(i, carry):
        at = pl.ds(pl.multiple_of(i * part, 16), part)
        x = xs[at, :]
        for acc, weight in zip(accs, weights):
            if weight.shape[1] == x.shape[1]:
                acc[at, :] += lax.dot_general(x, weight[...], NT, preferred_element_type=F32)
            else:
                acc[at, :] += dot(x, weight[...])
        return carry

    lax.fori_loop(0, splits, body, 0)


def finish_rms(squares, width):
    mean = jnp.sum(squares[...], axis=1, keepdims=True) * (1.0 / width)
    squares[...] = jnp.broadcast_to(lax.rsqrt(mean + EPSILON), squares.shape)


def mix_kernel(
    hid_ref, mir_ref, halo_ref, halo_mir_ref, gain_ref, wv_ref, wbc_ref, wst_ref,
    mix_ref, step_ref, acc_v, acc_b, acc_s, xs, squares,
):
    k = pl.program_id(0)
    tokens, depth = hid_ref.shape
    rows = tokens + 2 * HALO
    inner = wv_ref.shape[1]

    @pl.when(k == 0)
    def _():
        for acc in (acc_v, acc_b, acc_s, squares):
            acc[...] = jnp.zeros_like(acc)

    gain = gain_ref[...]
    scale_rows(hid_ref, 0, gain, xs, squares)
    scale_rows(halo_ref, tokens, gain, xs, squares)
    scale_mirrored(mir_ref, rows, gain, xs)
    scale_mirrored(halo_mir_ref, rows + tokens, gain, xs)
    multiply(xs, (acc_v, acc_b, acc_s), (wv_ref, wbc_ref, wst_ref), 3)

    @pl.when(k == pl.num_programs(0) - 1)
    def _():
        finish_rms(squares, depth * pl.num_programs(0))
        spans = [(r, r + HALO, TILE) for r in range(0, tokens, TILE)]
        for b in range(2):
            for r, out, size in spans:
                here = slice(b * rows + r, b * rows + r + size)
                step_ref[b, r : r + size, :] = (
                    acc_s[here, :] * squares[r : r + size, : step_ref.shape[2]]
                )
            for r, out, size in spans + [(tokens, 0, HALO), (tokens + HALO, tokens + HALO, HALO)]:
                here = slice(b * rows + r, b * rows + r + size)
                scale = squares[r : r + size, :]
                for c in range(0, inner, TILE):
                    mix_ref[b, out : out + size, c : c + TILE] = acc_v[here, c : c + TILE] * scale
                for c in range(0, acc_b.shape[1], TILE):
                    mix_ref[b, out : out + size, inner + c : inner + c + TILE] = (
                        acc_b[here, c : c + TILE] * scale
                    )


def gate_kernel(hid_ref, mir_ref, gain_ref, wg_ref, gate_ref, acc_g, xs, squares):
    k = pl.program_id(0)
    tokens, depth = hid_ref.shape

    @pl.when(k == 0)
    def _():
        for acc in (acc_g, squares):
            acc[...] = jnp.zeros_like(acc)

    gain = gain_ref[...]
    scale_rows(hid_ref, 0, gain, xs, squares)
    scale_mirrored(mir_ref, tokens, gain, xs)
    multiply(xs, (acc_g,), (wg_ref,), 2)

    @pl.when(k == pl.num_programs(0) - 1)
    def _():
        finish_rms(squares, depth * pl.num_programs(0))
        for b in range(2):
            for r in range(0, tokens, TILE):
                scale = squares[r : r + TILE, :]
                for c in range(0, wg_ref.shape[1], TILE):
                    gate_ref[b, r : r + TILE, c : c + TILE] = silu(
                        acc_g[b * tokens + r : b * tokens + r + TILE, c : c + TILE] * scale
                    )


DEPTH = 1024


def project_mix(hidden, halo, norm_gain, w_value, w_bc, w_step):
    tokens, width = hidden.shape
    count = width // DEPTH
    inner, maps, heads = w_value.shape[1], w_bc.shape[1], w_step.shape[1]
    rows = tokens + 2 * HALO
    ahead = lambda k: (0, k)
    back = lambda k: (0, count - 1 - k)
    down = lambda k: (k, 0)
    whole = lambda k: (0, 0, 0)
    return pl.pallas_call(
        mix_kernel,
        grid=(count,),
        in_specs=[
            pl.BlockSpec((tokens, DEPTH), ahead),
            pl.BlockSpec((tokens, DEPTH), back),
            pl.BlockSpec((2 * HALO, DEPTH), ahead),
            pl.BlockSpec((2 * HALO, DEPTH), back),
            pl.BlockSpec((1, DEPTH), ahead),
            pl.BlockSpec((DEPTH, inner), down),
            pl.BlockSpec((DEPTH, maps), down),
            pl.BlockSpec((heads, DEPTH), ahead),
        ],
        out_specs=[
            pl.BlockSpec((2, rows, inner + maps), whole),
            pl.BlockSpec((2, tokens, heads), whole),
        ],
        out_shape=[
            jax.ShapeDtypeStruct((2, rows, inner + maps), F32),
            jax.ShapeDtypeStruct((2, tokens, heads), F32),
        ],
        scratch_shapes=[
            pltpu.VMEM((2 * rows, inner), F32),
            pltpu.VMEM((2 * rows, maps), F32),
            pltpu.VMEM((2 * rows, heads), F32),
            pltpu.VMEM((2 * rows, DEPTH), BF16),
            pltpu.VMEM((rows, TILE), F32),
        ],
        compiler_params=params(40),
        cost_estimate=pl.CostEstimate(
            flops=4 * rows * width * (inner + maps + FLIP), transcendentals=0, bytes_accessed=20 << 20
        ),
        name="project_mix",
    )(hidden, hidden, halo, halo, norm_gain[None], w_value, w_bc, w_step.T)


def project_gate(hidden, norm_gain, w_gate):
    tokens, width = hidden.shape
    count = width // DEPTH
    inner = w_gate.shape[1]
    ahead = lambda k: (0, k)
    back = lambda k: (0, count - 1 - k)
    return pl.pallas_call(
        gate_kernel,
        grid=(count,),
        in_specs=[
            pl.BlockSpec((tokens, DEPTH), ahead),
            pl.BlockSpec((tokens, DEPTH), back),
            pl.BlockSpec((1, DEPTH), ahead),
            pl.BlockSpec((DEPTH, inner), lambda k: (k, 0)),
        ],
        out_specs=pl.BlockSpec((2, tokens, inner), lambda k: (0, 0, 0)),
        out_shape=jax.ShapeDtypeStruct((2, tokens, inner), F32),
        scratch_shapes=[
            pltpu.VMEM((2 * tokens, inner), F32),
            pltpu.VMEM((2 * tokens, DEPTH), BF16),
            pltpu.VMEM((tokens, TILE), F32),
        ],
        compiler_params=params(32),
        cost_estimate=pl.CostEstimate(
            flops=4 * tokens * width * (inner + FLIP),
            transcendentals=2 * tokens * inner,
            bytes_accessed=14 << 20,
        ),
        name="project_gate",
    )(hidden, hidden, norm_gain[None], w_gate)


def conv_kernel(
    mix_ref, step_ref, keep_ref, taps_ref, bias_ref, rate_ref, skip_ref,
    direct_ref, xf_ref, xb_ref, maps_ref, cols_ref, rows_ref, prefix_ref, enter_ref, final_ref,
    dt_sc, wf_sc, wb_sc, vf_sc, vb_sc,
):
    tokens, heads = step_ref.shape[1:]
    inner = direct_ref.shape[2]
    width = inner // heads
    state = maps_ref.shape[3]
    chunks = tokens // CHUNK
    matrix = spreader(heads, width)

    raw = step_ref[0] + bias_ref[...]
    dt = jnp.maximum(raw, 0.0) + jnp.log1p(jnp.exp(-jnp.abs(raw)))
    log_decay = -rate_ref[...] * dt
    square = (CHUNK, CHUNK)
    lower = jnp.where(iota(square, 0) >= iota(square, 1), 1.0, 0.0)
    upper = jnp.where(iota(square, 0) <= iota(square, 1), 1.0, 0.0)
    eye = jnp.where(iota(square, 0) == iota(square, 1), 1.0, 0.0)
    dt_sc[...] = spread(dt, matrix)
    totals = []
    for c in range(chunks):
        at = slice(c * CHUNK, (c + 1) * CHUNK)
        part = log_decay[at]
        inclusive = jnp.dot(lower, part, precision=lax.Precision.HIGHEST, preferred_element_type=F32)
        exclusive = inclusive - part
        last = inclusive[CHUNK - 1 : CHUNK]
        totals.append(last)
        cols_ref[0, 0, at] = inclusive
        cols_ref[0, 1, at] = exclusive
        cols_ref[0, 2, at] = jnp.exp(inclusive)
        cols_ref[0, 3, at] = jnp.exp(last - exclusive)
        for i, array in ((0, inclusive), (1, exclusive)):
            rows_ref[0, i, :, at] = lax.dot_general(
                array, eye, TN, precision=lax.Precision.HIGHEST, preferred_element_type=F32
            )
        wf_sc[at] = spread(jnp.exp(last - inclusive), matrix)
        wb_sc[at] = spread(jnp.exp(exclusive), matrix)
    zero = jnp.zeros_like(totals[0])
    before, after = [zero], [zero]
    for c in range(chunks - 1):
        before.append(before[-1] + totals[c])
        after.append(after[-1] + totals[chunks - 1 - c])
    after = after[::-1]
    everything = before[-1] + totals[-1]
    stack = jnp.concatenate(before + after + totals + [everything] * 4, axis=0)
    spread_rows = spread(jnp.exp(stack), matrix)
    prefix_ref[0] = spread_rows
    lane_totals = jnp.dot(
        jnp.broadcast_to(everything, (8, heads)),
        matrix.astype(F32),
        precision=lax.Precision.HIGHEST,
        preferred_element_type=F32,
    )

    half = CONV - 1

    def block(i, carry):
        r = pl.multiple_of(i * ROWS, ROWS)
        keep = keep_ref[pl.ds(r, ROWS), :]
        here = pl.ds(r, ROWS)
        for c in range(0, inner + 2 * state, TILE):
            lanes = slice(c, c + TILE)
            window = mix_ref[0, pl.ds(r, ROWS + 2 * HALO), lanes]
            moved = [window[HALO + j : HALO + j + ROWS] for j in range(-half, half + 1)]
            forward = taps_ref[0:1, lanes] * moved[0]
            backward = taps_ref[0:1, lanes] * moved[2 * half]
            for o in range(1, CONV):
                forward = forward + taps_ref[o : o + 1, lanes] * moved[o]
                backward = backward + taps_ref[o : o + 1, lanes] * moved[2 * half - o]
            forward = silu(forward)
            backward = silu(backward)
            if c < inner:
                forward = forward * keep
                backward = backward * keep
                direct_ref[0, here, lanes] = skip_ref[:, lanes] * (forward + backward)
                dt_lanes = dt_sc[here, lanes]
                forward = forward * dt_lanes
                backward = backward * dt_lanes
                xf_ref[0, here, lanes] = forward.astype(BF16)
                xb_ref[0, here, lanes] = backward.astype(BF16)
                vf_sc[here, lanes] = (forward * wf_sc[here, lanes]).astype(BF16)
                vb_sc[here, lanes] = (backward * wb_sc[here, lanes]).astype(BF16)
            else:
                which = (c - inner) // TILE
                maps_ref[0, which, here, :] = forward.astype(BF16)
                maps_ref[0, 2 + which, here, :] = backward.astype(BF16)
        return carry

    lax.fori_loop(0, tokens // ROWS, block, 0)

    for direction, moved, order in ((0, vf_sc, range(chunks)), (1, vb_sc, range(chunks - 1, -1, -1))):
        for j in range(0, inner, TILE):
            lanes = slice(j, j + TILE)
            carry = jnp.zeros((state, TILE), F32)
            for c in order:
                at = slice(c * CHUNK, (c + 1) * CHUNK)
                enter_ref[0, direction, c, :, lanes] = carry.astype(BF16)
                gained = lax.dot_general(
                    maps_ref[0, 2 * direction, at, :], moved[at, lanes], TN, preferred_element_type=F32
                )
                carry = carry * prefix_ref[0, 2 * chunks + c : 2 * chunks + c + 1, lanes] + gained
            final_ref[direction, 0, j // TILE, :state] = carry
            final_ref[direction, 0, j // TILE, state:] = lane_totals[:, lanes]


CONV = 4


def convolve(mix, steps, keep, taps, step_bias, decay_rate, skip):
    rows, channels = mix.shape[1:]
    tokens, heads = steps.shape[1:]
    inner = skip.shape[1]
    state = (channels - inner) // 2
    chunks = tokens // CHUNK
    one = lambda b: (b, 0, 0)
    flat = lambda b: (0, 0)
    four = lambda b: (b, 0, 0, 0)
    five = lambda b: (b, 0, 0, 0, 0)
    return pl.pallas_call(
        conv_kernel,
        grid=(2,),
        in_specs=[
            pl.BlockSpec((1, rows, channels), one),
            pl.BlockSpec((1, tokens, heads), one),
            pl.BlockSpec((tokens, 1), flat),
            pl.BlockSpec((CONV, channels), flat),
            pl.BlockSpec((1, heads), flat),
            pl.BlockSpec((1, heads), flat),
            pl.BlockSpec((1, inner), flat),
        ],
        out_specs=[
            pl.BlockSpec((1, tokens, inner), one),
            pl.BlockSpec((1, tokens, inner), one),
            pl.BlockSpec((1, tokens, inner), one),
            pl.BlockSpec((1, 4, tokens, state), four),
            pl.BlockSpec((1, 4, tokens, heads), four),
            pl.BlockSpec((1, 2, heads, tokens), four),
            pl.BlockSpec((1, 4 * chunks, inner), one),
            pl.BlockSpec((1, 2, chunks, state, inner), five),
            pl.BlockSpec((2, 1, inner // TILE, state + 8, TILE), lambda b: (0, b, 0, 0, 0)),
        ],
        out_shape=[
            jax.ShapeDtypeStruct((2, tokens, inner), F32),
            jax.ShapeDtypeStruct((2, tokens, inner), BF16),
            jax.ShapeDtypeStruct((2, tokens, inner), BF16),
            jax.ShapeDtypeStruct((2, 4, tokens, state), BF16),
            jax.ShapeDtypeStruct((2, 4, tokens, heads), F32),
            jax.ShapeDtypeStruct((2, 2, heads, tokens), F32),
            jax.ShapeDtypeStruct((2, 4 * chunks, inner), F32),
            jax.ShapeDtypeStruct((2, 2, chunks, state, inner), BF16),
            jax.ShapeDtypeStruct((2, 2, inner // TILE, state + 8, TILE), F32),
        ],
        scratch_shapes=[
            pltpu.VMEM((tokens, inner), F32),
            pltpu.VMEM((tokens, inner), F32),
            pltpu.VMEM((tokens, inner), F32),
            pltpu.VMEM((tokens, inner), BF16),
            pltpu.VMEM((tokens, inner), BF16),
        ],
        compiler_params=params(40),
        cost_estimate=pl.CostEstimate(flops=1 << 30, transcendentals=1 << 22, bytes_accessed=20 << 20),
        name="convolve",
    )(mix, steps, keep, taps, step_bias[None], decay_rate[None], skip)


def within_kernel(
    direct_ref, xf_ref, xb_ref, maps_ref, cols_ref, rows_ref, wout_ref, local_ref, mirror_ref,
):
    heads = cols_ref.shape[3]
    inner = direct_ref.shape[2]
    width = inner // heads
    square = (CHUNK, CHUNK)
    below = iota(square, 0) >= iota(square, 1)
    above = iota(square, 0) <= iota(square, 1)
    scores_f = lax.dot_general(maps_ref[0, 1], maps_ref[0, 0], NT, preferred_element_type=F32)
    scores_b = lax.dot_general(maps_ref[0, 3], maps_ref[0, 2], NT, preferred_element_type=F32)
    scores_f = jnp.where(below, scores_f, 0.0)
    scores_b = jnp.where(above, scores_b, 0.0)
    left = iota((CHUNK, TILE), 1) < width
    for j in range(0, inner, TILE):
        lanes = slice(j, j + TILE)
        values = jnp.concatenate([xf_ref[0, :, lanes], xb_ref[0, :, lanes]], axis=0)
        parts = []
        for h in range(j // width, (j + TILE) // width):
            gap = jnp.where(
                below,
                cols_ref[0, 0, :, h : h + 1] - rows_ref[0, 0, h : h + 1, :],
                rows_ref[0, 1, h : h + 1, :] - cols_ref[0, 1, :, h : h + 1],
            )
            decay = jnp.exp(gap)
            weights = jnp.concatenate(
                [(decay * scores_f).astype(BF16), (decay * scores_b).astype(BF16)], axis=1
            )
            parts.append(dot(weights, values))
        local_ref[0, :, lanes] = direct_ref[0, :, lanes] + jnp.where(left, parts[0], parts[1])
    flip = reversal(FLIP)
    blocks = wout_ref.shape[1] // FLIP
    for i in range(blocks):
        at = (blocks - 1 - i) * FLIP
        mirror_ref[:, i * FLIP : (i + 1) * FLIP] = dot(wout_ref[:, at : at + FLIP], flip).astype(BF16)


def within(direct, xf, xb, maps, cols, rows, w_out):
    tokens, inner = direct.shape[1:]
    state = maps.shape[3]
    heads = cols.shape[3]
    chunks = tokens // CHUNK
    count = 2 * chunks
    slab = w_out.shape[1] // count
    token = lambda i: (i // chunks, i % chunks, 0)
    inside = lambda i: (i // chunks, 0, i % chunks, 0)
    return pl.pallas_call(
        within_kernel,
        grid=(count,),
        in_specs=[
            pl.BlockSpec((1, CHUNK, inner), token),
            pl.BlockSpec((1, CHUNK, inner), token),
            pl.BlockSpec((1, CHUNK, inner), token),
            pl.BlockSpec((1, 4, CHUNK, state), inside),
            pl.BlockSpec((1, 4, CHUNK, heads), inside),
            pl.BlockSpec((1, 2, heads, CHUNK), lambda i: (i // chunks, 0, 0, i % chunks)),
            pl.BlockSpec((inner, slab), lambda i: (0, count - 1 - i)),
        ],
        out_specs=[
            pl.BlockSpec((1, CHUNK, inner), token),
            pl.BlockSpec((inner, slab), lambda i: (0, i)),
        ],
        out_shape=[
            jax.ShapeDtypeStruct((2, tokens, inner), F32),
            jax.ShapeDtypeStruct(w_out.shape, BF16),
        ],
        compiler_params=params(32),
        cost_estimate=pl.CostEstimate(flops=4 << 30, transcendentals=1 << 22, bytes_accessed=24 << 20),
        name="within",
    )(direct, xf, xb, maps, cols, rows, w_out)


def chain_kernel(states_ref, incoming_ref):
    count = states_ref.shape[0]
    state = incoming_ref.shape[1]
    backward = lax.axis_index("ctx") >= count // 2
    carry = jnp.zeros(incoming_ref.shape[1:], F32)
    for n in range(count):
        at = jnp.where(backward, count - 1 - n, n)
        incoming_ref[at] = carry.astype(incoming_ref.dtype)
        carry = carry * jnp.exp(states_ref[at, state : state + 1, :]) + states_ref[at, :state, :]


def chain(states):
    count, rows, tile = states.shape
    return pl.pallas_call(
        chain_kernel,
        out_shape=jax.ShapeDtypeStruct((count, rows - 8, tile), BF16),
        compiler_params=pltpu.CompilerParams(vmem_limit_bytes=16 << 20),
        cost_estimate=pl.CostEstimate(flops=1 << 20, transcendentals=0, bytes_accessed=2 << 20),
        name="chain",
    )(states)


def output_kernel(
    local_ref, silu_ref, maps_ref, cols_ref, prefix_ref, enter_ref, incoming_ref, gain_ref,
    wout_ref, mirror_ref, out_ref, normed,
):
    i = pl.program_id(0)
    chunks = normed.shape[1] // CHUNK
    heads = cols_ref.shape[3]
    inner = local_ref.shape[2]
    width = inner // heads

    @pl.when(i < 2 * chunks)
    def _():
        chunk = i % chunks
        branch = i // chunks
        matrix = spreader(heads, width)
        scale_f = spread(cols_ref[0, 2], matrix)
        scale_b = spread(cols_ref[0, 3], matrix)
        shape = (FLIP, FLIP)
        group = jnp.where(iota(shape, 0) // width == iota(shape, 1) // width, 1.0, 0.0).astype(BF16)
        ahead = prefix_ref[0, pl.ds(chunk, 1), :]
        behind = prefix_ref[0, pl.ds(chunks + chunk, 1), :]
        for j in range(0, inner, FLIP):
            lanes = slice(j, j + FLIP)
            tiles = range(j // TILE, (j + FLIP) // TILE)
            into_f = jnp.concatenate([incoming_ref[0, 0, t].astype(F32) for t in tiles], axis=1)
            into_b = jnp.concatenate([incoming_ref[1, 0, t].astype(F32) for t in tiles], axis=1)
            into_f = enter_ref[0, 0, 0, :, lanes].astype(F32) + ahead[:, lanes] * into_f
            into_b = enter_ref[0, 1, 0, :, lanes].astype(F32) + behind[:, lanes] * into_b
            y = local_ref[0, :, lanes]
            y = y + scale_f[:, lanes] * dot(maps_ref[0, 1], into_f.astype(BF16))
            y = y + scale_b[:, lanes] * dot(maps_ref[0, 3], into_b.astype(BF16))
            y = y * silu_ref[0, :, lanes]
            square = y * y
            high = square.astype(BF16)
            low = (square - high.astype(F32)).astype(BF16)
            mean = (dot(high, group) + dot(low, group)) * (1.0 / width)
            y = y * lax.rsqrt(mean + EPSILON) * gain_ref[:, lanes]
            at = pl.ds(pl.multiple_of(chunk * CHUNK, CHUNK), CHUNK)
            normed[branch, at, lanes] = y.astype(BF16)

    @pl.when(i >= 2 * chunks)
    def _():
        out_ref[0] = (dot(normed[0], wout_ref[...]) + dot(normed[1], mirror_ref[...])).astype(
            out_ref.dtype
        )


def output(local, gate, maps, cols, prefix, enter, incoming, gain, w_out, mirror, parts):
    tokens, inner = local.shape[1:]
    state = maps.shape[3]
    heads = cols.shape[3]
    chunks = tokens // CHUNK
    pre = 2 * chunks
    slab = w_out.shape[1] // parts
    held = lambda i: jnp.minimum(i, pre - 1)
    token = lambda i: (held(i) // chunks, held(i) % chunks, 0)
    inside = lambda i: (held(i) // chunks, 0, held(i) % chunks, 0)
    column = lambda i: (0, jnp.maximum(i - pre, 0))
    return pl.pallas_call(
        output_kernel,
        grid=(pre + parts,),
        in_specs=[
            pl.BlockSpec((1, CHUNK, inner), token),
            pl.BlockSpec((1, CHUNK, inner), token),
            pl.BlockSpec((1, 4, CHUNK, state), inside),
            pl.BlockSpec((1, 4, CHUNK, heads), inside),
            pl.BlockSpec((1, 4 * chunks, inner), lambda i: (held(i) // chunks, 0, 0)),
            pl.BlockSpec(
                (1, 2, 1, state, inner), lambda i: (held(i) // chunks, 0, held(i) % chunks, 0, 0)
            ),
            pl.BlockSpec(
                (2, 1, inner // TILE, state, TILE), lambda i: (0, held(i) // chunks, 0, 0, 0)
            ),
            pl.BlockSpec((1, inner), lambda i: (0, 0)),
            pl.BlockSpec((inner, slab), column),
            pl.BlockSpec((inner, slab), column),
        ],
        out_specs=pl.BlockSpec((1, tokens, slab), lambda i: (jnp.maximum(i - pre, 0), 0, 0)),
        out_shape=jax.ShapeDtypeStruct((parts, tokens, slab), BF16),
        scratch_shapes=[pltpu.VMEM((2, tokens, inner), BF16)],
        compiler_params=params(32),
        name="output",
    )(local, gate, maps, cols, prefix, enter, incoming, gain, w_out, mirror)


def shards(
    hidden,
    base_ids,
    norm_gain,
    w_gate,
    w_value,
    w_bc,
    w_step,
    conv_value,
    conv_bc,
    step_bias,
    decay_rate,
    skip_gain,
    out_gain,
    w_out,
):
    count = lax.axis_size("ctx")
    up = [(i, i + 1) for i in range(count - 1)]
    down = [(j, i) for i, j in up]
    halo = jnp.concatenate(
        [
            lax.ppermute(hidden[-HALO:], "ctx", up),
            lax.ppermute(hidden[:HALO], "ctx", down),
        ],
        axis=0,
    )
    keep = (base_ids != 4).astype(F32)[:, None]
    mix, steps = project_mix(hidden, halo, norm_gain, w_value, w_bc, w_step)
    inner = w_gate.shape[1]
    heads = w_step.shape[1]
    taps = jnp.concatenate([conv_value, conv_bc], axis=1)
    skip = jnp.repeat(skip_gain, inner // heads)[None]
    direct, xf, xb, maps, cols, rows, prefix, enter, final = convolve(
        mix, steps, keep, taps, step_bias, decay_rate, skip
    )
    state, tile = final.shape[3:]
    sent = lax.all_to_all(final.reshape(count, state, tile), "ctx", 0, 0)
    incoming = lax.all_to_all(chain(sent), "ctx", 0, 0)
    incoming = incoming.reshape(final.shape[:3] + incoming.shape[1:])
    gate = project_gate(hidden, norm_gain, w_gate)
    local, mirror = within(direct, xf, xb, maps, cols, rows, w_out)
    parts = lax.axis_size("head")
    term = output(local, gate, maps, cols, prefix, enter, incoming, out_gain[None], w_out, mirror, parts)
    pieces = lax.all_to_all(term, "head", 0, 0)
    return jnp.sum(pieces.astype(F32), axis=0).astype(BF16)


def solution(mesh):
    return jax.shard_map(
        shards,
        mesh=mesh,
        in_specs=(
            P("ctx", None),
            P("ctx"),
            P(),
            P(None, "head"),
            P(None, "head"),
            P(),
            P(None, "head"),
            P(None, "head"),
            P(),
            P("head"),
            P("head"),
            P("head"),
            P("head"),
            P("head", None),
        ),
        out_specs=P("ctx", "head"),
        check_vma=False,
    )
```

time: 953 us -> 197 us (0.21); the launches traced: 936 us -> 196 us
  waiting for transfers between devices: 556 us -> 1.37 us
  local copies, waits for them, and re-layouts: 189 us -> 34.2 us
  Pallas kernels: 0 us -> 63.9 us
  matrix products: 61.5 us -> 0 us
  other arithmetic: 57.5 us -> 5.14 us
  blocking collectives: 36.1 us -> 84.6 us
  starting transfers between devices: 21.9 us -> 6.16 us
  between operations: 13.9 us -> 0.2 us
    ppermute x14 -> x2, waiting for transfers between devices: 338 us -> 1.37 us  [the longest x1 1.37 us: shards(): lax.ppermute(hidden[:HALO], 'ctx', down)]
    reduce_scatter x2 -> x0, waiting for transfers between devices: 177 us -> none  [the longest x1 113 us: shards(): lax.psum_scatter(term[1][::-1, ::-1], 'head', scatter_dimension=1, tiled=...]
    rev x9 -> x0, local copies, waits for them, and re-layouts: 145 us -> none  [the longest x1 67.7 us: shards(): term[1][::-1, ::-1]]
    all_to_all x0 -> x2, blocking collectives: none -> 84.6 us  [the longest x1 57.8 us: shards(): pieces = lax.all_to_all(term, 'head', 0, 0)]
    pallas_call x0 -> x6, Pallas kernels: none -> 63.9 us  [the longest x1 16.3 us: convolve(): pl.pallas_call(conv_kernel, grid=(2,), in_specs=[pl.BlockSpec((1, rows, c...]
    dot_general x10 -> x0, matrix products: 61.5 us -> none  [the longest x4 21.9 us: project(): jnp.einsum('btd,dk->btk', scaled, weight, preferred_element_type=jnp.floa...]
    all_gather x2 -> x0, waiting for transfers between devices: 39.7 us -> none  [prefix(): gathered = jax.tree.map(lambda a: lax.all_gather(a, axis), part)]
    all_gather x2 -> x0, blocking collectives: 36.1 us -> none  [prefix(): gathered = jax.tree.map(lambda a: lax.all_gather(a, axis), part)]
  transfers between devices with their start and end apart: 18 -> 3, of which waited for: 13 -> 1; matrix products, arithmetic and copies ran while one was open for 4% -> 1% of each run, Pallas kernels for 0% -> 9%
where the time goes in v1:
time: 197 us; the launch traced here: 196 us
  blocking collectives  84.6 us (43%)
  Pallas kernels  63.9 us (32%)
  local copies, waits for them, and re-layouts  34.2 us (17%)
  starting transfers between devices  6.16 us (3%)
  other arithmetic  5.14 us (3%)
    all_to_all x1, blocking collectives, shards(): pieces = lax.all_to_all(term, 'head', 0, 0)  57.8 us
    unnamed x62, local copies, waits for them, and re-layouts  32.4 us
    all_to_all x1, blocking collectives, shards(): sent = lax.all_to_all(final.reshape(count, state, tile), 'ctx', 0, 0)  26.8 us
    pallas_call x1, Pallas kernels, convolve(): pl.pallas_call(conv_kernel, grid=(2,), in_specs=[pl.BlockSpec((1, rows, c...  16.3 us
    pallas_call x1, Pallas kernels, project_mix(): pl.pallas_call(mix_kernel, grid=(count,), in_specs=[pl.BlockSpec((tokens,...  16.3 us
    pallas_call x1, Pallas kernels, output(): pl.pallas_call(output_kernel, grid=(pre + parts,), in_specs=[pl.BlockSpec...  12.5 us
    pallas_call x1, Pallas kernels, project_gate(): pl.pallas_call(gate_kernel, grid=(count,), in_specs=[pl.BlockSpec((tokens...  11 us
    pallas_call x1, Pallas kernels, within(): pl.pallas_call(within_kernel, grid=(count,), in_specs=[pl.BlockSpec((1, C...  6.9 us
  transfers between devices with their start and end apart: 3, of which 1 were waited for; matrix products, arithmetic and copies ran while one was open for 1% of the time, Pallas kernels for 9%

profile of v1, /device:TPU:0, one launch (start us, length us, event | category | flops | bytes accessed | tf_op | source)
XLA Modules:
  0.0 195.7 jit_solution(9871534251445308752)
XLA Ops:
  7.3 2.2 %copy-done.13 = bf16[512,4096]{1,0:T(8,128)(2,1)S(1)} copy-done((bf16[512,4096]{1,0:T(8,128)(2,1)S(1)}, bf16[512,4096]{1,0:T(8,128)(2,1)}, u32[]{:S(2)}) %copy-start.13) | copy-done | bytes 4194328
  9.4 2.2 %copy-done.16 = bf16[4096,512]{1,0:T(8,128)(2,1)S(1)} copy-done((bf16[4096,512]{1,0:T(8,128)(2,1)S(1)}, bf16[4096,512]{1,0:T(8,128)(2,1)}, u32[]{:S(2)}) %copy-start.16) | copy-done | bytes 4194328
  11.6 1.6 copy-done.18
  14.8 16.3 %project_mix.1 = (f32[2,528,768]{2,1,0:T(8,128)S(1)}, f32[2,512,8]{2,1,0:T(8,128)S(1)}) custom-call(bf16[512,4096]{1,0:T(8,128)(2,1)S(1)} %copy-done.13, bf16[512,4096]{1,0:T(8,128)(2,1)S(1)} %copy-done.13, bf16[16,4096]{1,0:T(8,128)(2,1)S(1)} %pad_maximum_fusion.halo_ref.halo_mir_ref, bf16[16,4096]{1,0:T(8,128)(2,1)S(1)} %pad_maximum_fusion.halo_ref.halo_mir_ref, ...), custom_call_target="tpu_custom_call" | custom-call | flops 8858370048 | bytes 20971520 | tf_op jit(solution)/shard_map/project_mix/pallas_call | solution.py:180
  31.1 1.7 copy-done.24
  32.8 16.3 %convolve.1 = (f32[2,512,512]{2,1,0:T(8,128)S(1)}, bf16[2,512,512]{2,1,0:T(8,128)(2,1)S(1)}, bf16[2,512,512]{2,1,0:T(8,128)(2,1)S(1)}, bf16[2,4,512,128]{3,2,1,0...) custom-call(f32[2,528,768]{2,1,0:T(8,128)} %copy-done.24, ...), custom_call_target="tpu_custom_call" | custom-call | flops 1073741824 | bytes 20971520 | tf_op jit(solution)/shard_map/convolve/pallas_call | solution.py:367
  49.1 1.4 copy-done.4
  52.8 26.8 %all_to_all.15.states_ref = f32[16,136,128]{2,1,0:T(8,128)S(1)} all-to-all(f32[16,136,128]{2,1,0:T(8,128)S(1)} %bitcast.9), channel_id=1, replica_groups=mesh['ctx'=16,'head'=8] {'ctx'}, dimensions={0} | all-to-all | bytes 2228224 | tf_op jit(solution)/shard_map/all_to_all | solution.py:629
  80.5 3.6 %all-to-all-start.1 = ((bf16[16,128,128]{2,1,0:T(8,128)(2,1)}), bf16[16,128,128]{2,1,0:T(8,128)(2,1)S(1)}, u32[]{:S(2)}, u32[]{:S(2)}) async-start(bf16[16,128,128]{2,1,0:T(8,128)(2,1)} %chain.1), calls=%async_computation.1 | async-start | bytes 1048576 | tf_op jit(solution)/shard_map/all_to_all | solution.py:630
  84.1 2.2 %copy-done.14 = bf16[512,4096]{1,0:T(8,128)(2,1)S(1)} copy-done((bf16[512,4096]{1,0:T(8,128)(2,1)S(1)}, bf16[512,4096]{1,0:T(8,128)(2,1)}, u32[]{:S(2)}) %copy-start.14) | copy-done | bytes 4194328
  86.3 2.2 %copy-done.17 = bf16[4096,512]{1,0:T(8,128)(2,1)S(1)} copy-done((bf16[4096,512]{1,0:T(8,128)(2,1)S(1)}, bf16[4096,512]{1,0:T(8,128)(2,1)}, u32[]{:S(2)}) %copy-start.17) | copy-done | bytes 4194328
  88.5 11.0 %project_gate.1.silu_ref = f32[2,512,512]{2,1,0:T(8,128)S(1)} custom-call(bf16[512,4096]{1,0:T(8,128)(2,1)S(1)} %copy-done.14, bf16[512,4096]{1,0:T(8,128)(2,1)S(1)} %copy-done.14, f32[1,4096]{1,0:T(1,128)S(1)} %bitcast.13, bf16[4096,512]{1,0:T(8,128)(2,1)S(1)} %copy-done.17), custom_call_target="tpu_custom_call" | custom-call | flops 6442450944 | bytes 14680064 | tf_op jit(solution)/shard_map/project_gate/pallas_call | solution.py:222
  99.5 1.4 copy-done.6
  100.9 6.9 %within.1 = (f32[2,512,512]{2,1,0:T(8,128)S(1)}, bf16[512,4096]{1,0:T(8,128)(2,1)S(1)}) custom-call(f32[2,512,512]{2,1,0:T(8,128)S(1)} %copy-done.26, bf16[2,512,512]{2,1,0:T(8,128)(2,1)S(1)} %copy-done.28, bf16[2,512,512]{2,1,0:T(8,128)(2,1)S(1)} %copy-done.30, bf16[2,4,512,128]{3,2,1,0:T(8,128)(2,1)S(1)} %copy-done.11, ...), custom_call_target="tpu_custom_call" | custom-call | flops 4294967296 | bytes 25165824 | tf_op jit(solution)/shard_map/within/pallas_call | solution.py:460
  107.8 2.0 copy-done.2
  109.8 1.4 copy-done.8
  111.2 2.2 %copy-done.1 = bf16[512,4096]{1,0:T(8,128)(2,1)S(1)} copy-done((bf16[512,4096]{1,0:T(8,128)(2,1)S(1)}, bf16[512,4096]{1,0:T(8,128)(2,1)}, u32[]{:S(2)}) %copy-start.1) | copy-done | bytes 4194328
  113.4 2.2 %copy-done.3 = bf16[512,4096]{1,0:T(8,128)(2,1)S(1)} copy-done((bf16[512,4096]{1,0:T(8,128)(2,1)S(1)}, bf16[512,4096]{1,0:T(8,128)(2,1)}, u32[]{:S(2)}) %copy-start.3) | copy-done | bytes 4194328
  115.6 1.6 copy-done.5
  117.1 1.6 copy-done.7
  118.7 1.6 copy-done.9
  121.5 12.5 %output.1 = bf16[8,512,512]{2,1,0:T(8,128)(2,1)S(1)} custom-call(f32[2,512,512]{2,1,0:T(8,128)S(1)} %copy-done.9, f32[2,512,512]{2,1,0:T(8,128)S(1)} %copy-done.7, bf16[2,4,512,128]{3,2,1,0:T(8,128)(2,1)S(1)} %copy-done.12, f32[2,4,512,8]{3,2,1,0:T(8,128)S(1)} %get-tuple-element.24.cols_ref, f32[2,16,512]{2,1,0:T(8,128)S(1)} %get-tuple-element.27.prefix_ref, ...), custom_call_target="tpu_custom_call" | custom-call | tf_op jit(solution)/shard_map/output/pallas_call | solution.py:566
  134.1 57.8 %all_to_all.16 = bf16[8,512,512]{2,1,0:T(8,128)(2,1)} all-to-all(bf16[8,512,512]{2,1,0:T(8,128)(2,1)S(1)} %output.1), channel_id=1, replica_groups=mesh['ctx'=16,'head'=8] {'head'}, dimensions={0} | all-to-all | bytes 8388608 | tf_op jit(solution)/shard_map/all_to_all | solution.py:636
  191.9 3.7 %reduce_sum.12 = bf16[512,512]{1,0:T(8,128)(2,1)} reduce(bf16[8,512,512]{2,1,0:T(8,128)(2,1)} %all_to_all.16, bf16[]{:T(256)} %constant.4.clone.1), dimensions={0}, to_apply=%region_0.0 | reduce | flops 1835008 | bytes 4718594 | tf_op jit(solution)/shard_map/reduce_sum | solution.py:637
  (60 shorter events, 13.3 us)
Async XLA Ops:
  0.9 5.0 %collective-permute-start = (bf16[8,4096]{1,0:T(8,128)(2,1)S(1)}, bf16[8,4096]{1,0:T(8,128)(2,1)S(1)}, u32[]{:S(2)}, u32[]{:S(2)}) collective-permute-start(bf16[8,4096]{1,0:T(8,128)(2,1)S(1)} %get-tuple-element.31), channel_id=1, source_target_pairs={{0,8},{8,16},{16,24},{24,32},{32,40},{40,48},{48,56},{56,64},{64,7... | collective-permute-start | bytes 196616 | tf_op jit(solution)/shard_map/ppermute | solution.py:614
  2.2 5.0 %collective-permute-start.1 = (bf16[8,4096]{1,0:T(8,128)(2,1)S(1)}, bf16[8,4096]{1,0:T(8,128)(2,1)S(1)}, u32[]{:S(2)}, u32[]{:S(2)}) collective-permute-start(bf16[8,4096]{1,0:T(8,128)(2,1)S(1)} %get-tuple-element.32), channel_id=1, source_target_pairs={{8,0},{16,8},{24,16},{32,24},{40,32},{48,40},{56,48},{64,56},{72,6... | collective-permute-start | bytes 196616 | tf_op jit(solution)/shard_map/ppermute | solution.py:615
  7.2 2.2 %copy-start.13 = (bf16[512,4096]{1,0:T(8,128)(2,1)S(1)}, bf16[512,4096]{1,0:T(8,128)(2,1)}, u32[]{:S(2)}) copy-start(bf16[512,4096]{1,0:T(8,128)(2,1)} %mir_ref.3) | copy-start | bytes 12582916
  9.4 2.2 %copy-start.16 = (bf16[4096,512]{1,0:T(8,128)(2,1)S(1)}, bf16[4096,512]{1,0:T(8,128)(2,1)}, u32[]{:S(2)}) copy-start(bf16[4096,512]{1,0:T(8,128)(2,1)} %wv_ref.1) | copy-start | bytes 12582916
  11.6 1.6 copy-start.18
  14.8 18.0 %copy-start.22 = (f32[8]{0:T(128)S(1)}, f32[8]{0:T(128)}, u32[]{:S(2)}) copy-start(f32[8]{0:T(128)} %param.23) | copy-start | bytes 100
  14.8 18.0 %copy-start.23 = (f32[8]{0:T(128)S(1)}, f32[8]{0:T(128)}, u32[]{:S(2)}) copy-start(f32[8]{0:T(128)} %param.24) | copy-start | bytes 100
  31.1 1.7 copy-start.24
  52.8 26.8 %copy-start.10 = (bf16[2,4,512,128]{3,2,1,0:T(8,128)(2,1)}, bf16[2,4,512,128]{3,2,1,0:T(8,128)(2,1)S(1)}, u32[]{:S(2)}) copy-start(bf16[2,4,512,128]{3,2,1,0:T(8,128)(2,1)S(1)} %get-tuple-element.23.maps_ref) | copy-start | bytes 3145732
  52.8 26.8 %copy-start.27 = (bf16[2,512,512]{2,1,0:T(8,128)(2,1)}, bf16[2,512,512]{2,1,0:T(8,128)(2,1)S(1)}, u32[]{:S(2)}) copy-start(bf16[2,512,512]{2,1,0:T(8,128)(2,1)S(1)} %get-tuple-element.21.xf_ref) | copy-start | bytes 3145732
  52.8 31.3 %copy-start.21 = (f32[4096]{0:T(1024)S(1)}, f32[4096]{0:T(1024)}, u32[]{:S(2)}) copy-start(f32[4096]{0:T(1024)} %param.16) | copy-start | bytes 49156
  80.5 30.7 %all-to-all-start.1 = ((bf16[16,128,128]{2,1,0:T(8,128)(2,1)}), bf16[16,128,128]{2,1,0:T(8,128)(2,1)S(1)}, u32[]{:S(2)}, u32[]{:S(2)}) async-start(bf16[16,128,128]{2,1,0:T(8,128)(2,1)} %chain.1), calls=%async_computation.1 | async-start | bytes 1048576 | tf_op jit(solution)/shard_map/all_to_all | solution.py:630
  84.1 2.2 %copy-start.14 = (bf16[512,4096]{1,0:T(8,128)(2,1)S(1)}, bf16[512,4096]{1,0:T(8,128)(2,1)}, u32[]{:S(2)}) copy-start(bf16[512,4096]{1,0:T(8,128)(2,1)} %mir_ref.3) | copy-start | bytes 12582916
  86.3 2.2 %copy-start.17 = (bf16[4096,512]{1,0:T(8,128)(2,1)S(1)}, bf16[4096,512]{1,0:T(8,128)(2,1)}, u32[]{:S(2)}) copy-start(bf16[4096,512]{1,0:T(8,128)(2,1)} %wg_ref.1) | copy-start | bytes 12582916
  88.5 12.4 %copy-start = (bf16[512,4096]{1,0:T(8,128)(2,1)S(1)}, bf16[512,4096]{1,0:T(8,128)(2,1)}, u32[]{:S(2)}) copy-start(bf16[512,4096]{1,0:T(8,128)(2,1)} %wout_ref.3) | copy-start | bytes 12582916
  88.5 12.4 %copy-start.11 = (bf16[2,4,512,128]{3,2,1,0:T(8,128)(2,1)S(1)}, bf16[2,4,512,128]{3,2,1,0:T(8,128)(2,1)}, u32[]{:S(2)}) copy-start(bf16[2,4,512,128]{3,2,1,0:T(8,128)(2,1)} %copy-done.10) | copy-start | bytes 3145732
  88.5 12.4 %copy-start.26 = (f32[2,512,512]{2,1,0:T(8,128)S(1)}, f32[2,512,512]{2,1,0:T(8,128)}, u32[]{:S(2)}) copy-start(f32[2,512,512]{2,1,0:T(8,128)} %copy-done.25) | copy-start | bytes 6291460
  88.5 12.4 %copy-start.28 = (bf16[2,512,512]{2,1,0:T(8,128)(2,1)S(1)}, bf16[2,512,512]{2,1,0:T(8,128)(2,1)}, u32[]{:S(2)}) copy-start(bf16[2,512,512]{2,1,0:T(8,128)(2,1)} %copy-done.27) | copy-start | bytes 3145732
  88.5 12.4 %copy-start.30 = (bf16[2,512,512]{2,1,0:T(8,128)(2,1)S(1)}, bf16[2,512,512]{2,1,0:T(8,128)(2,1)}, u32[]{:S(2)}) copy-start(bf16[2,512,512]{2,1,0:T(8,128)(2,1)} %copy-done.29) | copy-start | bytes 3145732
  100.9 10.3 %copy-start.15 = (f32[512]{0:T(512)S(1)}, f32[512]{0:T(512)}, u32[]{:S(2)}) copy-start(f32[512]{0:T(512)} %param.26) | copy-start | bytes 6148
  107.8 2.0 %copy-start.2 = (bf16[512,4096]{1,0:T(8,128)(2,1)}, bf16[512,4096]{1,0:T(8,128)(2,1)S(1)}, u32[]{:S(2)}) copy-start(bf16[512,4096]{1,0:T(8,128)(2,1)S(1)} %get-tuple-element.30.mirror_ref) | copy-start | bytes 12582916
  111.2 2.2 %copy-start.1 = (bf16[512,4096]{1,0:T(8,128)(2,1)S(1)}, bf16[512,4096]{1,0:T(8,128)(2,1)}, u32[]{:S(2)}) copy-start(bf16[512,4096]{1,0:T(8,128)(2,1)} %wout_ref.3) | copy-start | bytes 12582916
  113.4 2.2 %copy-start.3 = (bf16[512,4096]{1,0:T(8,128)(2,1)S(1)}, bf16[512,4096]{1,0:T(8,128)(2,1)}, u32[]{:S(2)}) copy-start(bf16[512,4096]{1,0:T(8,128)(2,1)} %copy-done.2) | copy-start | bytes 12582916
  115.5 1.6 copy-start.5
  (10 other events, 12.5 us)

commit v2 on v1

v2 whole, which is shorter than its diff:
```python
import functools

import jax
import jax.numpy as jnp
from jax import lax
from jax.experimental import pallas as pl
from jax.experimental.pallas import tpu as pltpu
from jax.sharding import PartitionSpec as P

EPSILON = 1e-05
HALO = 8
CHUNK = 128
TILE = 128
FLIP = 256
ROWS = 64
GRANT = 56
BF16 = jnp.bfloat16
F32 = jnp.float32
NT = (((1,), (1,)), ((), ()))
TN = (((0,), (0,)), ((), ()))


def params(megabytes, dims=1):
    return pltpu.CompilerParams(
        dimension_semantics=("arbitrary",) * dims, vmem_limit_bytes=megabytes << 20
    )


def iota(shape, dim):
    return lax.broadcasted_iota(jnp.int32, shape, dim)


def dot(a, b):
    return jnp.dot(a, b, preferred_element_type=F32)


def reversal(width):
    where = iota((width, width), 0) + iota((width, width), 1) == width - 1
    return jnp.where(where, 1.0, 0.0).astype(BF16)


def spreader(heads, width):
    shape = (heads, heads * width)
    return jnp.where(iota(shape, 1) // width == iota(shape, 0), 1.0, 0.0).astype(BF16)


def spread(columns, matrix):
    high = columns.astype(BF16)
    low = (columns - high.astype(F32)).astype(BF16)
    return dot(high, matrix) + dot(low, matrix)


def silu(x):
    half = 0.5 * x
    return half + half * jnp.tanh(half)


def scale_rows(source, begin, gain, xs, squares):
    depth = source.shape[1]
    step = min(source.shape[0], TILE)
    for r in range(0, source.shape[0], step):
        x = source[r : r + step, :].astype(F32)
        xs[begin + r : begin + r + step, :] = (x * gain).astype(BF16)
        square = x * x
        partial = square[:, :TILE]
        for c in range(TILE, depth, TILE):
            partial = partial + square[:, c : c + TILE]
        squares[begin + r : begin + r + step, :] += partial


def scale_mirrored(source, begin, gain, xs):
    size, depth = source.shape
    flip = reversal(FLIP)
    for i in range(depth // FLIP):
        at = depth - (i + 1) * FLIP
        lanes = slice(i * FLIP, (i + 1) * FLIP)
        x = dot(source[:, at : at + FLIP], flip)
        xs[begin : begin + size, lanes] = (x * gain[:, lanes]).astype(BF16)


def accumulate(xs, accs, weights, splits):
    part = xs.shape[0] // splits
    for i in range(splits):
        at = slice(i * part, (i + 1) * part)
        x = xs[at, :]
        for acc, weight in zip(accs, weights):
            acc[at, :] += dot(x, weight[...])


def finish_rms(squares, width):
    mean = jnp.sum(squares[...], axis=1, keepdims=True) * (1.0 / width)
    squares[...] = jnp.broadcast_to(lax.rsqrt(mean + EPSILON), squares.shape)


def scale_all(hid, mir, halo, halo_mir, gain, xs, squares):
    tokens, depth = hid.shape
    rows = tokens + 2 * HALO
    scale_rows(hid, 0, gain, xs, squares)
    scale_rows(halo, tokens, gain, xs, squares)
    scale_mirrored(mir, rows, gain, xs)
    scale_mirrored(halo_mir, rows + tokens, gain, xs)


def placed(tokens):
    spans = [(r, r + HALO, TILE) for r in range(0, tokens, TILE)]
    return spans + [(tokens, 0, HALO), (tokens + HALO, tokens + HALO, HALO)]


def mix_kernel(
    hid_ref, mir_ref, before_ref, after_ref, before_mir_ref, after_mir_ref, gain_ref,
    wv_ref, wb_ref, wst_ref, mix_ref, step_ref, acc_v, acc_b, xs, squares, weights,
):
    k = pl.program_id(0)
    tokens, depth = hid_ref.shape
    rows = tokens + 2 * HALO
    inner = wv_ref.shape[1]
    heads = wst_ref.shape[0]
    state = wb_ref.shape[1]

    @pl.when(k == 0)
    def _():
        for acc in (acc_v, acc_b, squares):
            acc[...] = jnp.zeros_like(acc)

    halo = jnp.concatenate([before_ref[...].astype(F32), after_ref[...].astype(F32)], axis=0)
    halo_mir = jnp.concatenate(
        [before_mir_ref[...].astype(F32), after_mir_ref[...].astype(F32)], axis=0
    ).astype(BF16)
    scale_all(hid_ref, mir_ref, halo, halo_mir, gain_ref[...], xs, squares)
    weights[:, :state] = wb_ref[...]
    turned = jnp.concatenate(
        [wst_ref[...].astype(F32), jnp.zeros((TILE - heads, depth), F32)], axis=0
    )
    for c in range(0, depth, TILE):
        weights[c : c + TILE, state:] = turned[:, c : c + TILE].T.astype(BF16)
    accumulate(xs, (acc_v, acc_b), (wv_ref, weights), 3)

    @pl.when(k == pl.num_programs(0) - 1)
    def _():
        finish_rms(squares, depth * pl.num_programs(0))
        for b in range(2):
            for r in range(0, tokens, CHUNK):
                at = r // CHUNK * heads
                step_ref[b, :, at : at + heads] = (
                    acc_b[b * rows + r : b * rows + r + CHUNK, state : state + heads]
                    * squares[r : r + CHUNK, :heads]
                )
            for r, out, size in placed(tokens):
                here = slice(b * rows + r, b * rows + r + size)
                scale = squares[r : r + size, :]
                for c in range(0, inner, TILE):
                    mix_ref[b, c // TILE, out : out + size, :] = acc_v[here, c : c + TILE] * scale
                mix_ref[b, inner // TILE, out : out + size, :] = acc_b[here, :state] * scale


def gate_kernel(
    hid_ref, mir_ref, before_ref, after_ref, before_mir_ref, after_mir_ref, gain_ref,
    wg_ref, wc_ref, taps_ref, gate_ref, maps_ref, acc_g, acc_c, xs, squares, padded,
):
    k = pl.program_id(0)
    tokens, depth = hid_ref.shape
    rows = tokens + 2 * HALO

    @pl.when(k == 0)
    def _():
        for acc in (acc_g, acc_c, squares):
            acc[...] = jnp.zeros_like(acc)

    halo = jnp.concatenate([before_ref[...].astype(F32), after_ref[...].astype(F32)], axis=0)
    halo_mir = jnp.concatenate(
        [before_mir_ref[...].astype(F32), after_mir_ref[...].astype(F32)], axis=0
    ).astype(BF16)
    scale_all(hid_ref, mir_ref, halo, halo_mir, gain_ref[...], xs, squares)
    accumulate(xs, (acc_g, acc_c), (wg_ref, wc_ref), 3)

    @pl.when(k == pl.num_programs(0) - 1)
    def _():
        finish_rms(squares, depth * pl.num_programs(0))
        for b in range(2):
            for r in range(0, tokens, TILE):
                scale = squares[r : r + TILE, :]
                for c in range(0, wg_ref.shape[1], TILE):
                    gate_ref[b, r : r + TILE, c : c + TILE] = silu(
                        acc_g[b * rows + r : b * rows + r + TILE, c : c + TILE] * scale
                    )
            for r, out, size in placed(tokens):
                padded[out : out + size, :] = (
                    acc_c[b * rows + r : b * rows + r + size, :] * squares[r : r + size, :]
                )
            for r in range(0, tokens, ROWS):
                forward, backward = convolved(padded, r, taps_ref[...])
                maps_ref[b, 0, r : r + ROWS, :] = forward.astype(BF16)
                maps_ref[b, 1, r : r + ROWS, :] = backward.astype(BF16)


def convolved(source, row, taps):
    half = CONV - 1
    moved = [source[pl.ds(row + HALO + j, ROWS), :] for j in range(-half, half + 1)]
    forward = taps[0:1] * moved[0]
    backward = taps[0:1] * moved[2 * half]
    for o in range(1, CONV):
        forward = forward + taps[o : o + 1] * moved[o]
        backward = backward + taps[o : o + 1] * moved[2 * half - o]
    return silu(forward), silu(backward)


CONV = 4
DEPTH = 1024


def token_specs(tokens, count):
    ahead = lambda k: (0, k)
    back = lambda k: (0, count - 1 - k)
    return [
        pl.BlockSpec((tokens, DEPTH), ahead),
        pl.BlockSpec((tokens, DEPTH), back),
        pl.BlockSpec((HALO, DEPTH), ahead),
        pl.BlockSpec((HALO, DEPTH), ahead),
        pl.BlockSpec((HALO, DEPTH), back),
        pl.BlockSpec((HALO, DEPTH), back),
        pl.BlockSpec((1, DEPTH), ahead),
    ]


def project_mix(hidden, before, after, norm_gain, w_value, w_bc, w_step):
    tokens, width = hidden.shape
    count = width // DEPTH
    inner, state, heads = w_value.shape[1], w_bc.shape[1] // 2, w_step.shape[1]
    rows = tokens + 2 * HALO
    planes = (inner + state) // TILE
    return pl.pallas_call(
        mix_kernel,
        grid=(count,),
        in_specs=token_specs(tokens, count)
        + [
            pl.BlockSpec((DEPTH, inner), lambda k: (k, 0)),
            pl.BlockSpec((DEPTH, state), lambda k: (k, 0)),
            pl.BlockSpec((heads, DEPTH), lambda k: (0, k)),
        ],
        out_specs=[
            pl.BlockSpec((2, planes, rows, TILE), lambda k: (0, 0, 0, 0)),
            pl.BlockSpec((2, CHUNK, heads * tokens // CHUNK), lambda k: (0, 0, 0)),
        ],
        out_shape=[
            jax.ShapeDtypeStruct((2, planes, rows, TILE), F32),
            jax.ShapeDtypeStruct((2, CHUNK, heads * tokens // CHUNK), F32),
        ],
        scratch_shapes=[
            pltpu.VMEM((2 * rows, inner), F32),
            pltpu.VMEM((2 * rows, state + TILE), F32),
            pltpu.VMEM((2 * rows, DEPTH), BF16),
            pltpu.VMEM((rows, TILE), F32),
            pltpu.VMEM((DEPTH, state + TILE), BF16),
        ],
        compiler_params=params(GRANT),
        cost_estimate=pl.CostEstimate(
            flops=4 * rows * width * (inner + 2 * state + FLIP), transcendentals=0, bytes_accessed=20 << 20
        ),
        name="project_mix",
    )(
        hidden, hidden, before, after, before, after, norm_gain[None], w_value, w_bc, w_step.T
    )


def project_gate(hidden, before, after, norm_gain, w_gate, w_bc, taps):
    tokens, width = hidden.shape
    count = width // DEPTH
    inner, state = w_gate.shape[1], w_bc.shape[1] // 2
    rows = tokens + 2 * HALO
    return pl.pallas_call(
        gate_kernel,
        grid=(count,),
        in_specs=token_specs(tokens, count)
        + [
            pl.BlockSpec((DEPTH, inner), lambda k: (k, 0)),
            pl.BlockSpec((DEPTH, state), lambda k: (k, 1)),
            pl.BlockSpec((CONV, state), lambda k: (0, 1)),
        ],
        out_specs=[
            pl.BlockSpec((2, tokens, inner), lambda k: (0, 0, 0)),
            pl.BlockSpec((2, 2, tokens, state), lambda k: (0, 0, 0, 0)),
        ],
        out_shape=[
            jax.ShapeDtypeStruct((2, tokens, inner), F32),
            jax.ShapeDtypeStruct((2, 2, tokens, state), BF16),
        ],
        scratch_shapes=[
            pltpu.VMEM((2 * rows, inner), F32),
            pltpu.VMEM((2 * rows, state), F32),
            pltpu.VMEM((2 * rows, DEPTH), BF16),
            pltpu.VMEM((rows, TILE), F32),
            pltpu.VMEM((rows, TILE), F32),
        ],
        compiler_params=params(GRANT),
        cost_estimate=pl.CostEstimate(
            flops=4 * rows * width * (inner + state + FLIP),
            transcendentals=2 * tokens * inner,
            bytes_accessed=14 << 20,
        ),
        name="project_gate",
    )(hidden, hidden, before, after, before, after, norm_gain[None], w_gate, w_bc, taps)


def thirds(x):
    high = x.astype(BF16)
    rest = x - high.astype(F32)
    middle = rest.astype(BF16)
    return high, middle, (rest - middle.astype(F32)).astype(BF16)


def exact(matrix, x):
    high, middle, low = thirds(x)
    return dot(matrix, high) + dot(matrix, middle) + dot(matrix, low)


def conv_kernel(
    mix_ref, step_ref, base_ref, tapv_ref, tapb_ref, bias_ref, rate_ref, skip_ref,
    direct_ref, xf_ref, xb_ref, maps_ref, cols_ref, rows_ref, prefix_ref, enter_ref, final_ref,
    dt_sc, wf_sc, wb_sc, keep_sc, vf_sc, vb_sc, carry_sc,
):
    tokens, inner = direct_ref.shape[1:]
    heads = bias_ref.shape[1]
    width = inner // heads
    state = maps_ref.shape[3]
    chunks = tokens // CHUNK
    matrix = spreader(heads, width)

    def lanes_of(x):
        return jnp.concatenate([x] * chunks, axis=1)

    raw = step_ref[0] + lanes_of(bias_ref[...])
    dt = jnp.maximum(raw, 0.0) + jnp.log1p(jnp.exp(-jnp.abs(raw)))
    log_decay = -lanes_of(rate_ref[...]) * dt
    square = (CHUNK, CHUNK)
    lower = jnp.where(iota(square, 0) >= iota(square, 1), 1.0, 0.0).astype(BF16)
    inclusive = exact(lower, log_decay)
    exclusive = inclusive - log_decay
    last = inclusive[CHUNK - 1 : CHUNK]
    columns = (inclusive, exclusive, jnp.exp(inclusive), jnp.exp(last - exclusive))
    pad = jnp.zeros((CHUNK, TILE - chunks * heads), F32)
    turned = [jnp.concatenate([x, pad], axis=1).T for x in (inclusive, exclusive)]
    shape = (chunks * heads, inner)
    for c in range(chunks):
        mine = slice(c * heads, (c + 1) * heads)
        for q, x in enumerate(columns):
            cols_ref[0, c, q] = x[:, mine]
        for q, x in enumerate(turned):
            rows_ref[0, c, q] = x[mine, :]
        select = jnp.where(iota(shape, 1) // width + c * heads == iota(shape, 0), 1.0, 0.0)
        select = select.astype(BF16)
        at = slice(c * CHUNK, (c + 1) * CHUNK)
        dt_sc[at] = spread(dt, select)
        wf_sc[at] = spread(jnp.exp(last - inclusive), select)
        wb_sc[at] = spread(jnp.exp(exclusive), select)
    totals = [last[:, c * heads : (c + 1) * heads] for c in range(chunks)]
    zero = jnp.zeros_like(totals[0])
    before, after = [zero], [zero]
    for c in range(chunks - 1):
        before.append(before[-1] + totals[c])
        after.append(after[-1] + totals[chunks - 1 - c])
    after = after[::-1]
    everything = before[-1] + totals[-1]
    stack = jnp.concatenate(before + after + totals + [everything] * chunks, axis=0)
    prefix_ref[0] = spread(jnp.exp(stack), matrix)
    sent_totals = jnp.concatenate(
        [dot(x, matrix) for x in thirds(everything)] + [jnp.zeros((16 - 3, inner), F32)], axis=0
    ).astype(BF16)

    keep = jnp.where(base_ref[...] != 4, 1.0, 0.0)
    keep = jnp.concatenate([keep, jnp.zeros((CHUNK - chunks, CHUNK), F32)], axis=0).T
    for c in range(chunks):
        keep_sc[c * CHUNK : (c + 1) * CHUNK] = jnp.broadcast_to(keep[:, c : c + 1], square)
    skip = spread(skip_ref[...], matrix)

    def block(i, carry):
        r = pl.multiple_of(i * ROWS, ROWS)
        here = pl.ds(r, ROWS)
        kept = keep_sc[here, :]
        for c in range(0, inner, TILE):
            lanes = slice(c, c + TILE)
            forward, backward = convolved(mix_ref.at[0, c // TILE], r, tapv_ref[:, lanes])
            forward = forward * kept
            backward = backward * kept
            direct_ref[0, here, lanes] = skip[:, lanes] * (forward + backward)
            dt_lanes = dt_sc[here, lanes]
            forward = forward * dt_lanes
            backward = backward * dt_lanes
            xf_ref[0, here, lanes] = forward.astype(BF16)
            xb_ref[0, here, lanes] = backward.astype(BF16)
            vf_sc[here, lanes] = (forward * wf_sc[here, lanes]).astype(BF16)
            vb_sc[here, lanes] = (backward * wb_sc[here, lanes]).astype(BF16)
        forward, backward = convolved(mix_ref.at[0, inner // TILE], r, tapb_ref[...])
        maps_ref[0, 0, here, :] = forward.astype(BF16)
        maps_ref[0, 1, here, :] = backward.astype(BF16)
        return carry

    lax.fori_loop(0, tokens // ROWS, block, 0)

    for direction, moved, order in ((0, vf_sc, range(chunks)), (1, vb_sc, range(chunks - 1, -1, -1))):
        for n, c in enumerate(order):
            at = slice(c * CHUNK, (c + 1) * CHUNK)
            gained = lax.dot_general(
                maps_ref[0, direction, at, :], moved[at, :], TN, preferred_element_type=F32
            )
            if n == 0:
                enter_ref[0, direction, c] = jnp.zeros(enter_ref.shape[3:], BF16)
                carry_sc[...] = gained
            else:
                enter_ref[0, direction, c] = carry_sc[...].astype(BF16)
                total = prefix_ref[0, 2 * chunks + c : 2 * chunks + c + 1, :]
                carry_sc[...] = carry_sc[...] * total + gained
        for j in range(0, inner, TILE):
            final_ref[direction, 0, j // TILE, :state] = carry_sc[:, j : j + TILE].astype(BF16)
            final_ref[direction, 0, j // TILE, state:] = sent_totals[:, j : j + TILE]


def convolve(mix, steps, base_ids, conv_value, conv_bc, step_bias, decay_rate, skip_gain):
    planes, rows = mix.shape[1:3]
    tokens = rows - 2 * HALO
    inner = conv_value.shape[1]
    heads = step_bias.shape[1]
    state = conv_bc.shape[1] // 2
    chunks = tokens // CHUNK
    one = lambda b: (b, 0, 0)
    flat = lambda b: (0, 0)
    four = lambda b: (b, 0, 0, 0)
    five = lambda b: (b, 0, 0, 0, 0)
    return pl.pallas_call(
        conv_kernel,
        grid=(2,),
        in_specs=[
            pl.BlockSpec((1, planes, rows, TILE), four),
            pl.BlockSpec((1, CHUNK, heads * chunks), one),
            pl.BlockSpec((chunks, CHUNK), flat),
            pl.BlockSpec((CONV, inner), flat),
            pl.BlockSpec((CONV, state), flat),
            pl.BlockSpec((1, heads), flat),
            pl.BlockSpec((1, heads), flat),
            pl.BlockSpec((1, heads), flat),
        ],
        out_specs=[
            pl.BlockSpec((1, tokens, inner), one),
            pl.BlockSpec((1, tokens, inner), one),
            pl.BlockSpec((1, tokens, inner), one),
            pl.BlockSpec((1, 2, tokens, state), four),
            pl.BlockSpec((1, chunks, 4, CHUNK, heads), five),
            pl.BlockSpec((1, chunks, 2, heads, CHUNK), five),
            pl.BlockSpec((1, 4 * chunks, inner), one),
            pl.BlockSpec((1, 2, chunks, state, inner), five),
            pl.BlockSpec((2, 1, inner // TILE, state + 16, TILE), lambda b: (0, b, 0, 0, 0)),
        ],
        out_shape=[
            jax.ShapeDtypeStruct((2, tokens, inner), F32),
            jax.ShapeDtypeStruct((2, tokens, inner), BF16),
            jax.ShapeDtypeStruct((2, tokens, inner), BF16),
            jax.ShapeDtypeStruct((2, 2, tokens, state), BF16),
            jax.ShapeDtypeStruct((2, chunks, 4, CHUNK, heads), F32),
            jax.ShapeDtypeStruct((2, chunks, 2, heads, CHUNK), F32),
            jax.ShapeDtypeStruct((2, 4 * chunks, inner), F32),
            jax.ShapeDtypeStruct((2, 2, chunks, state, inner), BF16),
            jax.ShapeDtypeStruct((2, 2, inner // TILE, state + 16, TILE), BF16),
        ],
        scratch_shapes=[
            pltpu.VMEM((tokens, inner), F32),
            pltpu.VMEM((tokens, inner), F32),
            pltpu.VMEM((tokens, inner), F32),
            pltpu.VMEM((tokens, TILE), F32),
            pltpu.VMEM((tokens, inner), BF16),
            pltpu.VMEM((tokens, inner), BF16),
            pltpu.VMEM((state, inner), F32),
        ],
        compiler_params=params(GRANT),
        cost_estimate=pl.CostEstimate(flops=1 << 30, transcendentals=1 << 22, bytes_accessed=20 << 20),
        name="convolve",
    )(mix, steps, base_ids, conv_value, conv_bc, step_bias, decay_rate, skip_gain)


def within_kernel(
    direct_ref, xf_ref, xb_ref, b_ref, c_ref, cols_ref, rows_ref, wout_ref, local_ref, mirror_ref
):
    heads = cols_ref.shape[4]
    inner = direct_ref.shape[2]
    width = inner // heads
    square = (CHUNK, CHUNK)
    below = iota(square, 0) >= iota(square, 1)
    above = iota(square, 0) <= iota(square, 1)
    scores_f = lax.dot_general(c_ref[0, 0], b_ref[0, 0], NT, preferred_element_type=F32)
    scores_b = lax.dot_general(c_ref[0, 1], b_ref[0, 1], NT, preferred_element_type=F32)
    scores_f = jnp.where(below, scores_f, 0.0)
    scores_b = jnp.where(above, scores_b, 0.0)
    left = iota((CHUNK, TILE), 1) < width
    for j in range(0, inner, TILE):
        lanes = slice(j, j + TILE)
        values = jnp.concatenate([xf_ref[0, :, lanes], xb_ref[0, :, lanes]], axis=0)
        parts = []
        for h in range(j // width, (j + TILE) // width):
            gap = jnp.where(
                below,
                cols_ref[0, 0, 0, :, h : h + 1] - rows_ref[0, 0, 0, h : h + 1, :],
                rows_ref[0, 0, 1, h : h + 1, :] - cols_ref[0, 0, 1, :, h : h + 1],
            )
            decay = jnp.exp(gap)
            weights = jnp.concatenate(
                [(decay * scores_f).astype(BF16), (decay * scores_b).astype(BF16)], axis=1
            )
            parts.append(dot(weights, values))
        local_ref[0, :, lanes] = direct_ref[0, :, lanes] + jnp.where(left, parts[0], parts[1])
    flip = reversal(FLIP)
    blocks = wout_ref.shape[1] // FLIP
    for i in range(blocks):
        at = (blocks - 1 - i) * FLIP
        mirror_ref[:, i * FLIP : (i + 1) * FLIP] = dot(wout_ref[:, at : at + FLIP], flip).astype(BF16)


def within(direct, xf, xb, b_maps, c_maps, cols, rows, w_out):
    tokens, inner = direct.shape[1:]
    state = b_maps.shape[3]
    heads = cols.shape[4]
    chunks = tokens // CHUNK
    count = 2 * chunks
    slab = w_out.shape[1] // count
    token = lambda i: (i // chunks, i % chunks, 0)
    inside = lambda i: (i // chunks, 0, i % chunks, 0)
    five = lambda i: (i // chunks, i % chunks, 0, 0, 0)
    return pl.pallas_call(
        within_kernel,
        grid=(count,),
        in_specs=[
            pl.BlockSpec((1, CHUNK, inner), token),
            pl.BlockSpec((1, CHUNK, inner), token),
            pl.BlockSpec((1, CHUNK, inner), token),
            pl.BlockSpec((1, 2, CHUNK, state), inside),
            pl.BlockSpec((1, 2, CHUNK, state), inside),
            pl.BlockSpec((1, 1, 4, CHUNK, heads), five),
            pl.BlockSpec((1, 1, 2, heads, CHUNK), five),
            pl.BlockSpec((inner, slab), lambda i: (0, count - 1 - i)),
        ],
        out_specs=[
            pl.BlockSpec((1, CHUNK, inner), token),
            pl.BlockSpec((inner, slab), lambda i: (0, i)),
        ],
        out_shape=[
            jax.ShapeDtypeStruct((2, tokens, inner), F32),
            jax.ShapeDtypeStruct(w_out.shape, BF16),
        ],
        compiler_params=params(GRANT),
        cost_estimate=pl.CostEstimate(flops=4 << 30, transcendentals=1 << 22, bytes_accessed=24 << 20),
        name="within",
    )(direct, xf, xb, b_maps, c_maps, cols, rows, w_out)


def chain_kernel(states_ref, incoming_ref):
    count = states_ref.shape[0]
    state = incoming_ref.shape[1]
    backward = lax.axis_index("ctx") >= count // 2
    carry = jnp.zeros(incoming_ref.shape[1:], F32)
    for n in range(count):
        at = jnp.where(backward, count - 1 - n, n)
        incoming_ref[at] = carry.astype(incoming_ref.dtype)
        total = jnp.sum(states_ref[at, state:, :].astype(F32), axis=0, keepdims=True)
        carry = carry * jnp.exp(total) + states_ref[at, :state, :].astype(F32)


def chain(states):
    count, rows, tile = states.shape
    return pl.pallas_call(
        chain_kernel,
        out_shape=jax.ShapeDtypeStruct((count, rows - 16, tile), BF16),
        compiler_params=pltpu.CompilerParams(vmem_limit_bytes=16 << 20),
        cost_estimate=pl.CostEstimate(flops=1 << 20, transcendentals=0, bytes_accessed=2 << 20),
        name="chain",
    )(states)


def normalise(
    branch, chunk, local_ref, silu_ref, c_ref, cols_ref, prefix_ref, enter_ref, incoming_ref,
    gain_ref, normed,
):
    chunks = normed.shape[1] // CHUNK
    heads = cols_ref.shape[4]
    inner = local_ref.shape[2]
    width = inner // heads
    matrix = spreader(heads, width)
    scale_f = spread(cols_ref[0, 0, 2], matrix)
    scale_b = spread(cols_ref[0, 0, 3], matrix)
    shape = (FLIP, FLIP)
    group = jnp.where(iota(shape, 0) // width == iota(shape, 1) // width, 1.0, 0.0).astype(BF16)
    ahead = prefix_ref[0, pl.ds(chunk, 1), :]
    behind = prefix_ref[0, pl.ds(chunks + chunk, 1), :]
    for j in range(0, inner, FLIP):
        lanes = slice(j, j + FLIP)
        tiles = range(j // TILE, (j + FLIP) // TILE)
        into_f = jnp.concatenate([incoming_ref[0, 0, t].astype(F32) for t in tiles], axis=1)
        into_b = jnp.concatenate([incoming_ref[1, 0, t].astype(F32) for t in tiles], axis=1)
        into_f = enter_ref[0, 0, 0, :, lanes].astype(F32) + ahead[:, lanes] * into_f
        into_b = enter_ref[0, 1, 0, :, lanes].astype(F32) + behind[:, lanes] * into_b
        y = local_ref[0, :, lanes]
        y = y + scale_f[:, lanes] * dot(c_ref[0, 0], into_f.astype(BF16))
        y = y + scale_b[:, lanes] * dot(c_ref[0, 1], into_b.astype(BF16))
        y = y * silu_ref[0, :, lanes]
        square = y * y
        high = square.astype(BF16)
        low = (square - high.astype(F32)).astype(BF16)
        mean = (dot(high, group) + dot(low, group)) * (1.0 / width)
        y = y * lax.rsqrt(mean + EPSILON) * gain_ref[:, lanes]
        at = pl.ds(pl.multiple_of(chunk * CHUNK, CHUNK), CHUNK)
        normed[branch, at, lanes] = y.astype(BF16)


def multiply_out(n, row, normed, wout_ref, mirror_ref, send_ref, keep_ref):
    rows = send_ref.shape[1]
    half = 4

    def product():
        at = slice(row, row + rows)
        return (dot(normed[0, at], wout_ref[...]) + dot(normed[1, at], mirror_ref[...])).astype(BF16)

    @pl.when(n < half)
    def _():
        send_ref[0] = product()

    @pl.when(n >= half)
    def _():
        keep_ref[0] = product()


def first_kernel(
    blocks_ref, local_ref, silu_ref, c_ref, cols_ref, prefix_ref, enter_ref, incoming_ref, gain_ref,
    wout_ref, mirror_ref, send_ref, keep_ref, normed,
):
    i = pl.program_id(0)
    chunks = normed.shape[1] // CHUNK

    @pl.when(i < 2 * chunks)
    def _():
        normalise(
            i // chunks, i % chunks, local_ref, silu_ref, c_ref, cols_ref, prefix_ref, enter_ref,
            incoming_ref, gain_ref, normed,
        )

    @pl.when(i >= 2 * chunks)
    def _():
        multiply_out(i - 2 * chunks, 0, normed, wout_ref, mirror_ref, send_ref, keep_ref)


def first_output(blocks, local, gate, c_maps, cols, prefix, enter, incoming, gain, w_out, mirror, rows):
    tokens, inner = local.shape[1:]
    state = c_maps.shape[3]
    heads = cols.shape[4]
    chunks = tokens // CHUNK
    parts = 8
    pre = 2 * chunks
    slab = w_out.shape[1] // parts
    held = lambda i: jnp.minimum(i, pre - 1)
    token = lambda i, n: (held(i) // chunks, held(i) % chunks, 0)
    inside = lambda i, n: (held(i) // chunks, 0, held(i) % chunks, 0)
    column = lambda i, n: (0, n[jnp.maximum(i - pre, 0)])
    return pl.pallas_call(
        first_kernel,
        grid_spec=pltpu.PrefetchScalarGridSpec(
            num_scalar_prefetch=1,
            grid=(pre + parts,),
            in_specs=[
                pl.BlockSpec((1, CHUNK, inner), token),
                pl.BlockSpec((1, CHUNK, inner), token),
                pl.BlockSpec((1, 2, CHUNK, state), inside),
                pl.BlockSpec(
                    (1, 1, 4, CHUNK, heads), lambda i, n: (held(i) // chunks, held(i) % chunks, 0, 0, 0)
                ),
                pl.BlockSpec((1, 4 * chunks, inner), lambda i, n: (held(i) // chunks, 0, 0)),
                pl.BlockSpec(
                    (1, 2, 1, state, inner),
                    lambda i, n: (held(i) // chunks, 0, held(i) % chunks, 0, 0),
                ),
                pl.BlockSpec(
                    (2, 1, inner // TILE, state, TILE), lambda i, n: (0, held(i) // chunks, 0, 0, 0)
                ),
                pl.BlockSpec((1, inner), lambda i, n: (0, 0)),
                pl.BlockSpec((inner, slab), column),
                pl.BlockSpec((inner, slab), column),
            ],
            out_specs=[
                pl.BlockSpec((1, rows, slab), lambda i, n: (jnp.clip(i - pre, 0, 3), 0, 0)),
                pl.BlockSpec((1, rows, slab), lambda i, n: (jnp.maximum(i - pre - 4, 0), 0, 0)),
                pl.BlockSpec((2, tokens, inner), lambda i, n: (0, 0, 0)),
            ],
        ),
        out_shape=[
            jax.ShapeDtypeStruct((4, rows, slab), BF16),
            jax.ShapeDtypeStruct((4, rows, slab), BF16),
            jax.ShapeDtypeStruct((2, tokens, inner), BF16),
        ],
        compiler_params=params(GRANT),
        cost_estimate=pl.CostEstimate(flops=3 << 30, transcendentals=1 << 20, bytes_accessed=24 << 20),
        name="first_output",
    )(blocks, local, gate, c_maps, cols, prefix, enter, incoming, gain, w_out, mirror)


def next_output(blocks, normed, w_out, mirror, row, rows):
    tokens, inner = normed.shape[1:]
    parts = 8
    slab = w_out.shape[1] // parts
    column = lambda i, n: (0, n[i])

    def kernel(blocks_ref, normed_ref, wout_ref, mirror_ref, send_ref, keep_ref):
        multiply_out(pl.program_id(0), row, normed_ref, wout_ref, mirror_ref, send_ref, keep_ref)

    return pl.pallas_call(
        kernel,
        grid_spec=pltpu.PrefetchScalarGridSpec(
            num_scalar_prefetch=1,
            grid=(parts,),
            in_specs=[
                pl.BlockSpec((2, tokens, inner), lambda i, n: (0, 0, 0)),
                pl.BlockSpec((inner, slab), column),
                pl.BlockSpec((inner, slab), column),
            ],
            out_specs=[
                pl.BlockSpec((1, rows, slab), lambda i, n: (jnp.minimum(i, 3), 0, 0)),
                pl.BlockSpec((1, rows, slab), lambda i, n: (jnp.maximum(i - 4, 0), 0, 0)),
            ],
        ),
        out_shape=[jax.ShapeDtypeStruct((4, rows, slab), BF16)] * 2,
        compiler_params=params(GRANT),
        cost_estimate=pl.CostEstimate(flops=2 << 30, transcendentals=0, bytes_accessed=12 << 20),
        name="next_output",
    )(blocks, normed, w_out, mirror)


ORDERS = ((2, 6, 1), (6, 1, 2), (1, 2, 6))
GROUPS = ((0, 176), (176, 176), (352, 160))


def block_order(order):
    kept = [0]
    for partner in order[:0:-1]:
        kept = [k ^ partner for k in kept] + kept
    return [k ^ order[0] for k in kept] + kept


def reduced(send, keep, order):
    for partner in order:
        pairs = [(i, i ^ partner) for i in range(lax.axis_size("head"))]
        arrived = lax.ppermute(send, "head", pairs)
        half = keep.shape[0] // 2
        total = (keep.astype(F32) + arrived.astype(F32)).astype(BF16)
        send, keep = total[:half], total[half:]
    return total[0]


def shards(
    hidden,
    base_ids,
    norm_gain,
    w_gate,
    w_value,
    w_bc,
    w_step,
    conv_value,
    conv_bc,
    step_bias,
    decay_rate,
    skip_gain,
    out_gain,
    w_out,
):
    count = lax.axis_size("ctx")
    up = [(i, i + 1) for i in range(count - 1)]
    down = [(j, i) for i, j in up]
    before = lax.ppermute(hidden[-HALO:], "ctx", up)
    after = lax.ppermute(hidden[:HALO], "ctx", down)
    mix, steps = project_mix(hidden, before, after, norm_gain, w_value, w_bc, w_step)
    direct, xf, xb, b_maps, cols, rows, prefix, enter, final = convolve(
        mix,
        steps,
        base_ids.reshape(-1, CHUNK),
        conv_value,
        conv_bc,
        step_bias[None],
        decay_rate[None],
        skip_gain[None],
    )
    state, tile = final.shape[3:]
    sent = lax.all_to_all(final.reshape(count, state, tile), "ctx", 0, 0)
    gate, c_maps = project_gate(hidden, before, after, norm_gain, w_gate, w_bc, conv_bc)
    sent, gate, c_maps = lax.optimization_barrier((sent, gate, c_maps))
    incoming = lax.all_to_all(chain(sent), "ctx", 0, 0)
    incoming = incoming.reshape(final.shape[:3] + incoming.shape[1:])
    local, mirror = within(direct, xf, xb, b_maps, c_maps, cols, rows, w_out)
    blocks = jnp.array([block_order(o) for o in ORDERS], jnp.int32) ^ lax.axis_index("head")
    send, keep, normed = first_output(
        blocks[0], local, gate, c_maps, cols, prefix, enter, incoming, out_gain[None], w_out, mirror,
        GROUPS[0][1],
    )
    groups = [(send, keep)]
    for i in (1, 2):
        groups.append(next_output(blocks[i], normed, w_out, mirror, *GROUPS[i]))
    return jnp.concatenate([reduced(*g, o) for g, o in zip(groups, ORDERS)], axis=0)


def solution(mesh):
    return jax.shard_map(
        shards,
        mesh=mesh,
        in_specs=(
            P("ctx", None),
            P("ctx"),
            P(),
            P(None, "head"),
            P(None, "head"),
            P(),
            P(None, "head"),
            P(None, "head"),
            P(),
            P("head"),
            P("head"),
            P("head"),
            P("head"),
            P("head", None),
        ),
        out_specs=P("ctx", "head"),
        check_vma=False,
    )
```

time: 197 us -> 152 us (0.77)
  blocking collectives: 84.6 us -> 0 us
  local copies, waits for them, and re-layouts: 34.2 us -> 3 us
  starting transfers between devices: 6.16 us -> 34.2 us
  waiting for transfers between devices: 1.37 us -> 25 us
  Pallas kernels: 63.9 us -> 85.3 us
  other arithmetic: 5.14 us -> 2.47 us
    all_to_all x2 -> x0, blocking collectives: 84.6 us -> none  [the longest x1 57.8 us: shards(): pieces = lax.all_to_all(term, 'head', 0, 0)]
    unnamed x62 -> x14, local copies, waits for them, and re-layouts: 32.4 us -> 1.43 us
    ppermute x2 -> x11, waiting for transfers between devices: 1.37 us -> 25 us  [the longest x9 24.8 us: reduced(): arrived = lax.ppermute(send, 'head', pairs)]
    pallas_call x4 -> x6, Pallas kernels: 56.1 us -> 73.4 us  [the longest x2 18.3 us: next_output(): pl.pallas_call(kernel, grid_spec=pltpu.PrefetchScalarGridSpec(num_scalar_...]
    ppermute x2 -> x11, starting transfers between devices: 2.59 us -> 19 us  [the longest x9 14.7 us: reduced(): arrived = lax.ppermute(send, 'head', pairs)]
    all_to_all x0 -> x1, starting transfers between devices: none -> 9.55 us  [shards(): sent = lax.all_to_all(final.reshape(count, state, tile), 'ctx', 0, 0)]
    pallas_call x1, Pallas kernels: 6.9 us -> 11 us  [within(): pl.pallas_call(within_kernel, grid=(count,), in_specs=[pl.BlockSpec((1, C...]
    reduce_sum x1 -> x0, other arithmetic: 3.72 us -> none  [shards(): return jnp.sum(pieces.astype(F32), axis=0).astype(BF16)]
  transfers between devices with their start and end apart: 3 -> 13, of which waited for: 1 -> 8; matrix products, arithmetic and copies ran while one was open for 1% -> 2% of each run, Pallas kernels for 9% -> 23%
where the time goes in v2:
time: 152 us; the launch traced here: 150 us
  Pallas kernels  85.3 us (56%)
  starting transfers between devices  34.2 us (23%)
  waiting for transfers between devices  25 us (16%)
  local copies, waits for them, and re-layouts  3 us (2%)
  other arithmetic  2.47 us (2%)
    ppermute x9, waiting for transfers between devices, reduced(): arrived = lax.ppermute(send, 'head', pairs)  24.8 us
    pallas_call x2, Pallas kernels, next_output(): pl.pallas_call(kernel, grid_spec=pltpu.PrefetchScalarGridSpec(num_scalar_...  18.3 us
    pallas_call x1, Pallas kernels, first_output(): pl.pallas_call(first_kernel, grid_spec=pltpu.PrefetchScalarGridSpec(num_s...  17.6 us
    ppermute x9, starting transfers between devices, reduced(): arrived = lax.ppermute(send, 'head', pairs)  14.7 us
    pallas_call x1, Pallas kernels, project_gate(): pl.pallas_call(gate_kernel, grid=(count,), in_specs=token_specs(tokens, c...  14.6 us
    pallas_call x1, Pallas kernels, project_mix(): pl.pallas_call(mix_kernel, grid=(count,), in_specs=token_specs(tokens, co...  13.2 us
    pallas_call x1, Pallas kernels, within(): pl.pallas_call(within_kernel, grid=(count,), in_specs=[pl.BlockSpec((1, C...  11 us
    pallas_call x1, Pallas kernels, convolve(): pl.pallas_call(conv_kernel, grid=(2,), in_specs=[pl.BlockSpec((1, planes,...  9.73 us
  transfers between devices with their start and end apart: 13, of which 8 were waited for; matrix products, arithmetic and copies ran while one was open for 2% of the time, Pallas kernels for 23%

profile of v2, /device:TPU:0, one launch (start us, length us, event | category | flops | bytes accessed | tf_op | source)
XLA Modules:
  0.0 150.2 jit_solution(10156458305454840458)
XLA Ops:
  0.0 0.9 fusion.3
  0.9 1.3 collective-permute-start.1
  2.2 3.0 %collective-permute-start = (bf16[8,4096]{1,0:T(8,128)(2,1)S(1)}, bf16[8,4096]{1,0:T(8,128)(2,1)S(1)}, u32[]{:S(2)}, u32[]{:S(2)}) collective-permute-start(bf16[8,4096]{1,0:T(8,128)(2,1)S(1)} %get-tuple-element.56), channel_id=1, source_target_pairs={{0,8},{8,16},{16,24},{24,32},{32,40},{40,48},{48,56},{56,64},{64,7... | collective-permute-start | bytes 196616 | tf_op jit(solution)/shard_map/ppermute | solution.py:770
  6.7 13.2 %project_mix.1 = (f32[2,5,528,128]{3,2,1,0:T(8,128)}, f32[2,128,32]{2,1,0:T(8,128)}) custom-call(bf16[512,4096]{1,0:T(8,128)(2,1)} %mir_ref.3, bf16[512,4096]{1,0:T(8,128)(2,1)} %mir_ref.3, bf16[8,4096]{1,0:T(8,128)(2,1)} %copy-done.6, bf16[8,4096]{1,0:T(8,128)(2,1)} %copy-done.5, bf16[8,4096]{1,0:T(8,128)(2,1)} %copy-done.6, bf16[8,4096]{1,0:T(8,128)(2,1)} %copy-done.5, ...), custom_call_target="tpu_custom_call" | custom-call | flops 8858370048 | bytes 20971520 | tf_op jit(solution)/shard_map/project_mix/pallas_call | solution.py:231
  19.9 9.7 %convolve.1 = (f32[2,512,512]{2,1,0:T(8,128)}, bf16[2,512,512]{2,1,0:T(8,128)(2,1)}, bf16[2,512,512]{2,1,0:T(8,128)(2,1)}, bf16[2,2,512,128]{3,2,1,0:T(8,128)(2,...) custom-call(f32[2,5,528,128]{3,2,1,0:T(8,128)} %get-tuple-element.30, ...), custom_call_target="tpu_custom_call" | custom-call | flops 1073741824 | bytes 20971520 | tf_op jit(solution)/shard_map/convolve/pallas_call | solution.py:428
  29.7 9.5 %all-to-all-start = ((bf16[16,144,128]{2,1,0:T(8,128)(2,1)}), bf16[16,144,128]{2,1,0:T(8,128)(2,1)S(1)}, u32[]{:S(2)}, u32[]{:S(2)}) async-start(bf16[16,144,128]{2,1,0:T(8,128)(2,1)} %bitcast.22), calls=%async_computation | async-start | bytes 1179648 | tf_op jit(solution)/shard_map/all_to_all | solution.py:784
  39.2 14.6 %project_gate.1 = (f32[2,512,512]{2,1,0:T(8,128)}, bf16[2,2,512,128]{3,2,1,0:T(8,128)(2,1)}) custom-call(bf16[512,4096]{1,0:T(8,128)(2,1)} %mir_ref.3, bf16[512,4096]{1,0:T(8,128)(2,1)} %mir_ref.3, bf16[8,4096]{1,0:T(8,128)(2,1)} %copy-done.6, bf16[8,4096]{1,0:T(8,128)(2,1)} %copy-done.5, bf16[8,4096]{1,0:T(8,128)(2,1)} %copy-done.6, ...), custom_call_target="tpu_custom_call" | custom-call | flops 7751073792 | bytes 14680064 | tf_op jit(solution)/shard_map/project_gate/pallas_call | solution.py:270
  53.8 1.0 chain.1
  54.8 5.7 %all-to-all-start.1 = ((bf16[16,128,128]{2,1,0:T(8,128)(2,1)}), bf16[16,128,128]{2,1,0:T(8,128)(2,1)S(1)}, u32[]{:S(2)}, u32[]{:S(2)}) async-start(bf16[16,128,128]{2,1,0:T(8,128)(2,1)} %chain.1), calls=%async_computation.1 | async-start | bytes 1048576 | tf_op jit(solution)/shard_map/all_to_all | solution.py:787
  61.0 11.0 %within.1 = (f32[2,512,512]{2,1,0:T(8,128)}, bf16[512,4096]{1,0:T(8,128)(2,1)}) custom-call(f32[2,512,512]{2,1,0:T(8,128)} %get-tuple-element.32.direct_ref, bf16[2,512,512]{2,1,0:T(8,128)(2,1)} %get-tuple-element.33.xf_ref, bf16[2,512,512]{2,1,0:T(8,128)(2,1)} %get-tuple-element.34.xb_ref, bf16[2,2,512,128]{3,2,1,0:T(8,128)(2,1)} %get-tuple-element.35.b_ref, ...), custom_call_target="tpu_custom_call" | custom-call | flops 4294967296 | bytes 25165824 | tf_op jit(solution)/shard_map/within/pallas_call | solution.py:525
  72.8 17.6 %first_output.1 = (bf16[4,176,512]{2,1,0:T(8,128)(2,1)}, bf16[4,176,512]{2,1,0:T(8,128)(2,1)}, bf16[2,512,512]{2,1,0:T(8,128)(2,1)}) custom-call(s32[8]{0:T(128)} %get-tuple-element.59.blocks_ref, f32[2,512,512]{2,1,0:T(8,128)} %get-tuple-element.42.local_ref, f32[2,512,512]{2,1,0:T(8,128)} %get-tuple-element.43.silu_ref, ...), custom_call_target="tpu_custom_call" | custom-call | flops 3221225472 | bytes 25165824 | tf_op jit(solution)/shard_map/first_output/pallas_call | solution.py:658
  90.4 9.1 %next_output.3 = (bf16[4,160,512]{2,1,0:T(8,128)(2,1)}, bf16[4,160,512]{2,1,0:T(8,128)(2,1)}) custom-call(s32[8]{0:T(128)} %get-tuple-element.58.blocks_ref, bf16[2,512,512]{2,1,0:T(8,128)(2,1)} %get-tuple-element.50.normed_ref, bf16[512,4096]{1,0:T(8,128)(2,1)} %wout_ref.7, bf16[512,4096]{1,0:T(8,128)(2,1)} %get-tuple-element.47.mirror_ref), custom_call_target="tpu_custom_call" | custom-call | flops 2147483648 | bytes 12582912 | tf_op jit(solution)/shard_map/next_output/pallas_call | solution.py:708
  99.5 2.9 %collective-permute-start.8 = (bf16[4,160,512]{2,1,0:T(8,128)(2,1)}, bf16[4,160,512]{2,1,0:T(8,128)(2,1)S(1)}, u32[]{:S(2)}, u32[]{:S(2)}) collective-permute-start(bf16[4,160,512]{2,1,0:T(8,128)(2,1)} %get-tuple-element.54), channel_id=1, source_target_pairs={{0,1},{1,0},{2,3},{3,2},{4,5},{5,4},{6,7},{7,6},{8,9},{9,8},{10,11... | collective-permute-start | bytes 1966088 | tf_op jit(solution)/shard_map/ppermute | solution.py:744
  102.4 1.5 collective-permute-start.2
  103.9 9.2 %next_output.2 = (bf16[4,176,512]{2,1,0:T(8,128)(2,1)}, bf16[4,176,512]{2,1,0:T(8,128)(2,1)}) custom-call(s32[8]{0:T(128)} %get-tuple-element.57.blocks_ref, bf16[2,512,512]{2,1,0:T(8,128)(2,1)} %get-tuple-element.50.normed_ref, bf16[512,4096]{1,0:T(8,128)(2,1)} %wout_ref.7, bf16[512,4096]{1,0:T(8,128)(2,1)} %get-tuple-element.47.mirror_ref), custom_call_target="tpu_custom_call" | custom-call | flops 2147483648 | bytes 12582912 | tf_op jit(solution)/shard_map/next_output/pallas_call | solution.py:708
  113.1 2.1 %collective-permute-start.5 = (bf16[4,176,512]{2,1,0:T(8,128)(2,1)}, bf16[4,176,512]{2,1,0:T(8,128)(2,1)S(1)}, u32[]{:S(2)}, u32[]{:S(2)}) collective-permute-start(bf16[4,176,512]{2,1,0:T(8,128)(2,1)} %get-tuple-element.52), channel_id=1, source_target_pairs={{0,6},{1,7},{2,4},{3,5},{4,2},{5,3},{6,0},{7,1},{8,14},{9,15},{10,... | collective-permute-start | bytes 2162696 | tf_op jit(solution)/shard_map/ppermute | solution.py:744
  115.2 3.1 %collective-permute-done.8 = bf16[4,160,512]{2,1,0:T(8,128)(2,1)S(1)} collective-permute-done((bf16[4,160,512]{2,1,0:T(8,128)(2,1)}, bf16[4,160,512]{2,1,0:T(8,128)(2,1)S(1)}, u32[]{:S(2)}, u32[]{:S(2)}) %collective-permute-start.8) | collective-permute-done | bytes 655392 | tf_op jit(solution)/shard_map/ppermute | solution.py:744
  118.5 1.6 %collective-permute-start.9 = (bf16[2,160,512]{2,1,0:T(8,128)(2,1)S(1)}, bf16[2,160,512]{2,1,0:T(8,128)(2,1)S(1)}, u32[]{:S(2)}, u32[]{:S(2)}) collective-permute-start(bf16[2,160,512]{2,1,0:T(8,128)(2,1)S(1)} %slice.77), channel_id=1, source_target_pairs={{0,2},{1,3},{2,0},{3,1},{4,6},{5,7},{6,4},{7,5},{8,10},{9,11},{10,... | collective-permute-start | bytes 983048 | tf_op jit(solution)/shard_map/ppermute | solution.py:744
  120.9 2.8 %collective-permute-start.3 = (bf16[2,176,512]{2,1,0:T(8,128)(2,1)S(1)}, bf16[2,176,512]{2,1,0:T(8,128)(2,1)S(1)}, u32[]{:S(2)}, u32[]{:S(2)}) collective-permute-start(bf16[2,176,512]{2,1,0:T(8,128)(2,1)S(1)} %slice.69), channel_id=1, source_target_pairs={{0,6},{1,7},{2,4},{3,5},{4,2},{5,3},{6,0},{7,1},{8,14},{9,15},{10,... | collective-permute-start | bytes 1081352 | tf_op jit(solution)/shard_map/ppermute | solution.py:744
  123.7 9.9 %collective-permute-done.5 = bf16[4,176,512]{2,1,0:T(8,128)(2,1)S(1)} collective-permute-done((bf16[4,176,512]{2,1,0:T(8,128)(2,1)}, bf16[4,176,512]{2,1,0:T(8,128)(2,1)S(1)}, u32[]{:S(2)}, u32[]{:S(2)}) %collective-permute-start.5) | collective-permute-done | bytes 720928 | tf_op jit(solution)/shard_map/ppermute | solution.py:744
  134.6 2.2 %collective-permute-start.10 = (bf16[1,160,512]{2,1,0:T(8,128)(2,1)S(1)}, bf16[1,160,512]{2,1,0:T(8,128)(2,1)S(1)}, u32[]{:S(2)}, u32[]{:S(2)}) collective-permute-start(bf16[1,160,512]{2,1,0:T(8,128)(2,1)S(1)} %slice.79), channel_id=1, source_target_pairs={{0,6},{1,7},{2,4},{3,5},{4,2},{5,3},{6,0},{7,1},{8,14},{9,15},{10,... | collective-permute-start | bytes 491528 | tf_op jit(solution)/shard_map/ppermute | solution.py:744
  136.8 4.5 %collective-permute-done.3 = bf16[2,176,512]{2,1,0:T(8,128)(2,1)S(1)} collective-permute-done((bf16[2,176,512]{2,1,0:T(8,128)(2,1)S(1)}, bf16[2,176,512]{2,1,0:T(8,128)(2,1)S(1)}, u32[]{:S(2)}, u32[]{:S(2)}) %collective-permute-start.3) | collective-permute-done | bytes 360480 | tf_op jit(solution)/shard_map/ppermute | solution.py:744
  142.1 1.5 %collective-permute-done.6 = bf16[2,176,512]{2,1,0:T(8,128)(2,1)S(1)} collective-permute-done((bf16[2,176,512]{2,1,0:T(8,128)(2,1)S(1)}, bf16[2,176,512]{2,1,0:T(8,128)(2,1)S(1)}, u32[]{:S(2)}, u32[]{:S(2)}) %collective-permute-start.6) | collective-permute-done | bytes 360480 | tf_op jit(solution)/shard_map/ppermute | solution.py:744
  144.0 4.5 %collective-permute-done.4 = bf16[1,176,512]{2,1,0:T(8,128)(2,1)S(1)} collective-permute-done((bf16[1,176,512]{2,1,0:T(8,128)(2,1)S(1)}, bf16[1,176,512]{2,1,0:T(8,128)(2,1)S(1)}, u32[]{:S(2)}, u32[]{:S(2)}) %collective-permute-start.4) | collective-permute-done | bytes 180256 | tf_op jit(solution)/shard_map/ppermute | solution.py:744
  (43 shorter events, 7.7 us)
Async XLA Ops:
  0.9 5.0 %collective-permute-start.1 = (bf16[8,4096]{1,0:T(8,128)(2,1)S(1)}, bf16[8,4096]{1,0:T(8,128)(2,1)S(1)}, u32[]{:S(2)}, u32[]{:S(2)}) collective-permute-start(bf16[8,4096]{1,0:T(8,128)(2,1)S(1)} %get-tuple-element.55), channel_id=1, source_target_pairs={{8,0},{16,8},{24,16},{32,24},{40,32},{48,40},{56,48},{64,56},{72,6... | collective-permute-start | bytes 196616 | tf_op jit(solution)/shard_map/ppermute | solution.py:771
  2.2 3.9 %collective-permute-start = (bf16[8,4096]{1,0:T(8,128)(2,1)S(1)}, bf16[8,4096]{1,0:T(8,128)(2,1)S(1)}, u32[]{:S(2)}, u32[]{:S(2)}) collective-permute-start(bf16[8,4096]{1,0:T(8,128)(2,1)S(1)} %get-tuple-element.56), channel_id=1, source_target_pairs={{0,8},{8,16},{16,24},{24,32},{32,40},{40,48},{48,56},{56,64},{64,7... | collective-permute-start | bytes 196616 | tf_op jit(solution)/shard_map/ppermute | solution.py:770
  5.9 0.6 copy-start.5
  6.1 0.6 copy-start.6
  29.7 24.1 %all-to-all-start = ((bf16[16,144,128]{2,1,0:T(8,128)(2,1)}), bf16[16,144,128]{2,1,0:T(8,128)(2,1)S(1)}, u32[]{:S(2)}, u32[]{:S(2)}) async-start(bf16[16,144,128]{2,1,0:T(8,128)(2,1)} %bitcast.22), calls=%async_computation | async-start | bytes 1179648 | tf_op jit(solution)/shard_map/all_to_all | solution.py:784
  54.8 17.3 %all-to-all-start.1 = ((bf16[16,128,128]{2,1,0:T(8,128)(2,1)}), bf16[16,128,128]{2,1,0:T(8,128)(2,1)S(1)}, u32[]{:S(2)}, u32[]{:S(2)}) async-start(bf16[16,128,128]{2,1,0:T(8,128)(2,1)} %chain.1), calls=%async_computation.1 | async-start | bytes 1048576 | tf_op jit(solution)/shard_map/all_to_all | solution.py:787
  72.0 0.8 copy-start
  90.4 12.0 %copy-start.4 = (bf16[4,176,512]{2,1,0:T(8,128)(2,1)S(1)}, bf16[4,176,512]{2,1,0:T(8,128)(2,1)}, u32[]{:S(2)}) copy-start(bf16[4,176,512]{2,1,0:T(8,128)(2,1)} %get-tuple-element.49) | copy-start | bytes 2162692
  99.5 18.8 %collective-permute-start.8 = (bf16[4,160,512]{2,1,0:T(8,128)(2,1)}, bf16[4,160,512]{2,1,0:T(8,128)(2,1)S(1)}, u32[]{:S(2)}, u32[]{:S(2)}) collective-permute-start(bf16[4,160,512]{2,1,0:T(8,128)(2,1)} %get-tuple-element.54), channel_id=1, source_target_pairs={{0,1},{1,0},{2,3},{3,2},{4,5},{5,4},{6,7},{7,6},{8,9},{9,8},{10,11... | collective-permute-start | bytes 1966088 | tf_op jit(solution)/shard_map/ppermute | solution.py:744
  102.4 18.2 %collective-permute-start.2 = (bf16[4,176,512]{2,1,0:T(8,128)(2,1)S(1)}, bf16[4,176,512]{2,1,0:T(8,128)(2,1)S(1)}, u32[]{:S(2)}, u32[]{:S(2)}) collective-permute-start(bf16[4,176,512]{2,1,0:T(8,128)(2,1)S(1)} %copy-done.4), channel_id=1, source_target_pairs={{0,2},{1,3},{2,0},{3,1},{4,6},{5,7},{6,4},{7,5},{8,10},{9,11},{10,... | collective-permute-start | bytes 2162696 | tf_op jit(solution)/shard_map/ppermute | solution.py:744
  103.9 14.4 %copy-start.3 = (bf16[4,160,512]{2,1,0:T(8,128)(2,1)S(1)}, bf16[4,160,512]{2,1,0:T(8,128)(2,1)}, u32[]{:S(2)}) copy-start(bf16[4,160,512]{2,1,0:T(8,128)(2,1)} %get-tuple-element.53) | copy-start | bytes 1966084
  113.1 7.5 %copy-start.1 = (bf16[4,176,512]{2,1,0:T(8,128)(2,1)S(1)}, bf16[4,176,512]{2,1,0:T(8,128)(2,1)}, u32[]{:S(2)}) copy-start(bf16[4,176,512]{2,1,0:T(8,128)(2,1)} %get-tuple-element.48) | copy-start | bytes 2162692
  113.1 20.4 %collective-permute-start.5 = (bf16[4,176,512]{2,1,0:T(8,128)(2,1)}, bf16[4,176,512]{2,1,0:T(8,128)(2,1)S(1)}, u32[]{:S(2)}, u32[]{:S(2)}) collective-permute-start(bf16[4,176,512]{2,1,0:T(8,128)(2,1)} %get-tuple-element.52), channel_id=1, source_target_pairs={{0,6},{1,7},{2,4},{3,5},{4,2},{5,3},{6,0},{7,1},{8,14},{9,15},{10,... | collective-permute-start | bytes 2162696 | tf_op jit(solution)/shard_map/ppermute | solution.py:744
  118.5 15.1 %copy-start.2 = (bf16[4,176,512]{2,1,0:T(8,128)(2,1)S(1)}, bf16[4,176,512]{2,1,0:T(8,128)(2,1)}, u32[]{:S(2)}) copy-start(bf16[4,176,512]{2,1,0:T(8,128)(2,1)} %get-tuple-element.51) | copy-start | bytes 2162692
  118.5 16.0 %collective-permute-start.9 = (bf16[2,160,512]{2,1,0:T(8,128)(2,1)S(1)}, bf16[2,160,512]{2,1,0:T(8,128)(2,1)S(1)}, u32[]{:S(2)}, u32[]{:S(2)}) collective-permute-start(bf16[2,160,512]{2,1,0:T(8,128)(2,1)S(1)} %slice.77), channel_id=1, source_target_pairs={{0,2},{1,3},{2,0},{3,1},{4,6},{5,7},{6,4},{7,5},{8,10},{9,11},{10,... | collective-permute-start | bytes 983048 | tf_op jit(solution)/shard_map/ppermute | solution.py:744
  120.9 20.4 %collective-permute-start.3 = (bf16[2,176,512]{2,1,0:T(8,128)(2,1)S(1)}, bf16[2,176,512]{2,1,0:T(8,128)(2,1)S(1)}, u32[]{:S(2)}, u32[]{:S(2)}) collective-permute-start(bf16[2,176,512]{2,1,0:T(8,128)(2,1)S(1)} %slice.69), channel_id=1, source_target_pairs={{0,6},{1,7},{2,4},{3,5},{4,2},{5,3},{6,0},{7,1},{8,14},{9,15},{10,... | collective-permute-start | bytes 1081352 | tf_op jit(solution)/shard_map/ppermute | solution.py:744
  133.8 9.9 %collective-permute-start.6 = (bf16[2,176,512]{2,1,0:T(8,128)(2,1)S(1)}, bf16[2,176,512]{2,1,0:T(8,128)(2,1)S(1)}, u32[]{:S(2)}, u32[]{:S(2)}) collective-permute-start(bf16[2,176,512]{2,1,0:T(8,128)(2,1)S(1)} %slice.73), channel_id=1, source_target_pairs={{0,1},{1,0},{2,3},{3,2},{4,5},{5,4},{6,7},{7,6},{8,9},{9,8},{10,11... | collective-permute-start | bytes 1081352 | tf_op jit(solution)/shard_map/ppermute | solution.py:744
  134.6 9.3 %collective-permute-start.10 = (bf16[1,160,512]{2,1,0:T(8,128)(2,1)S(1)}, bf16[1,160,512]{2,1,0:T(8,128)(2,1)S(1)}, u32[]{:S(2)}, u32[]{:S(2)}) collective-permute-start(bf16[1,160,512]{2,1,0:T(8,128)(2,1)S(1)} %slice.79), channel_id=1, source_target_pairs={{0,6},{1,7},{2,4},{3,5},{4,2},{5,3},{6,0},{7,1},{8,14},{9,15},{10,... | collective-permute-start | bytes 491528 | tf_op jit(solution)/shard_map/ppermute | solution.py:744
  141.4 7.1 %collective-permute-start.4 = (bf16[1,176,512]{2,1,0:T(8,128)(2,1)S(1)}, bf16[1,176,512]{2,1,0:T(8,128)(2,1)S(1)}, u32[]{:S(2)}, u32[]{:S(2)}) collective-permute-start(bf16[1,176,512]{2,1,0:T(8,128)(2,1)S(1)} %slice.71), channel_id=1, source_target_pairs={{0,1},{1,0},{2,3},{3,2},{4,5},{5,4},{6,7},{7,6},{8,9},{9,8},{10,11... | collective-permute-start | bytes 540680 | tf_op jit(solution)/shard_map/ppermute | solution.py:744
  143.8 5.6 %collective-permute-start.7 = (bf16[1,176,512]{2,1,0:T(8,128)(2,1)S(1)}, bf16[1,176,512]{2,1,0:T(8,128)(2,1)S(1)}, u32[]{:S(2)}, u32[]{:S(2)}) collective-permute-start(bf16[1,176,512]{2,1,0:T(8,128)(2,1)S(1)} %slice.75), channel_id=1, source_target_pairs={{0,2},{1,3},{2,0},{3,1},{4,6},{5,7},{6,4},{7,5},{8,10},{9,11},{10,... | collective-permute-start | bytes 540680 | tf_op jit(solution)/shard_map/ppermute | solution.py:744

commit v3 on v2

v3 whole, which is shorter than its diff:
```python
import functools

import jax
import jax.numpy as jnp
from jax import lax
from jax.experimental import pallas as pl
from jax.experimental.pallas import tpu as pltpu
from jax.sharding import PartitionSpec as P

EPSILON = 1e-05
HALO = 8
CHUNK = 128
TILE = 128
FLIP = 256
ROWS = 64
GRANT = 56
BF16 = jnp.bfloat16
F32 = jnp.float32
NT = (((1,), (1,)), ((), ()))
TN = (((0,), (0,)), ((), ()))


def params(megabytes, dims=1):
    return pltpu.CompilerParams(
        dimension_semantics=("arbitrary",) * dims, vmem_limit_bytes=megabytes << 20
    )


def iota(shape, dim):
    return lax.broadcasted_iota(jnp.int32, shape, dim)


def dot(a, b):
    return jnp.dot(a, b, preferred_element_type=F32)


def reversal(width):
    where = iota((width, width), 0) + iota((width, width), 1) == width - 1
    return jnp.where(where, 1.0, 0.0).astype(BF16)


def spreader(heads, width):
    shape = (heads, heads * width)
    return jnp.where(iota(shape, 1) // width == iota(shape, 0), 1.0, 0.0).astype(BF16)


def selector(group, heads, columns, inner):
    shape = (columns, inner)
    where = iota(shape, 1) // (inner // heads) + group * heads == iota(shape, 0)
    return jnp.where(where, 1.0, 0.0).astype(BF16)


def spread(columns, matrix):
    high = columns.astype(BF16)
    low = (columns - high.astype(F32)).astype(BF16)
    return dot(high, matrix) + dot(low, matrix)


def silu(x):
    half = 0.5 * x
    return half + half * jnp.tanh(half)


def scale_rows(source, begin, gain, xs, squares):
    depth = source.shape[1]
    step = min(source.shape[0], TILE)
    for r in range(0, source.shape[0], step):
        x = source[r : r + step, :].astype(F32)
        xs[begin + r : begin + r + step, :] = (x * gain).astype(BF16)
        square = x * x
        partial = square[:, :TILE]
        for c in range(TILE, depth, TILE):
            partial = partial + square[:, c : c + TILE]
        squares[begin + r : begin + r + step, :] += partial


def scale_mirrored(source, begin, gain, xs):
    size, depth = source.shape
    flip = reversal(FLIP)
    for i in range(depth // FLIP):
        at = depth - (i + 1) * FLIP
        lanes = slice(i * FLIP, (i + 1) * FLIP)
        x = dot(source[:, at : at + FLIP], flip)
        xs[begin : begin + size, lanes] = (x * gain[:, lanes]).astype(BF16)


def accumulate(xs, acc, weights, splits):
    part = xs.shape[0] // splits
    depth = weights[0].shape[0]
    for i in range(splits):
        at = slice(i * part, (i + 1) * part)
        total = dot(xs[at, :depth], weights[0][...])
        for j in range(1, len(weights)):
            total = total + dot(xs[at, j * depth : (j + 1) * depth], weights[j][...])
        acc[at, :] += total


def finish_rms(squares, width):
    mean = jnp.sum(squares[...], axis=1, keepdims=True) * (1.0 / width)
    squares[...] = jnp.broadcast_to(lax.rsqrt(mean + EPSILON), squares.shape)


def scale_all(hid, before, after, gain, xs, squares):
    tokens, depth = hid[0].shape
    rows = tokens + 2 * HALO
    for i in range(2):
        lanes = pl.ds(i * depth, depth)
        halo = jnp.concatenate([before[i][...].astype(F32), after[i][...].astype(F32)], axis=0)
        own, other = gain[i][...], gain[1 - i][...]
        scale_rows(hid[i], 0, own, xs.at[:, lanes], squares)
        scale_rows(halo, tokens, own, xs.at[:, lanes], squares)
        lanes = pl.ds((1 - i) * depth, depth)
        scale_mirrored(hid[i], rows, other, xs.at[:, lanes])
        scale_mirrored(halo.astype(BF16), rows + tokens, other, xs.at[:, lanes])


def placed(tokens):
    spans = [(r, r + HALO, TILE) for r in range(0, tokens, TILE)]
    return spans + [(tokens, 0, HALO), (tokens + HALO, tokens + HALO, HALO)]


def mix_step(hid, before, after, gain, wv, wb, wst, mix, steps, acc_v, acc_b, xs, squares, weights, last):
    tokens, depth = hid[0].shape
    rows = tokens + 2 * HALO
    inner = wv[0].shape[1]
    heads = wst[0].shape[0]
    state = wb[0].shape[1]
    scale_all(hid, before, after, gain, xs, squares)
    for i in range(2):
        weights[i * depth : (i + 1) * depth, :state] = wb[i][...]
        turned = jnp.concatenate(
            [wst[i][...].astype(F32), jnp.zeros((TILE - heads, depth), F32)], axis=0
        )
        for c in range(0, depth, TILE):
            weights[i * depth + c : i * depth + c + TILE, state:] = (
                turned[:, c : c + TILE].T.astype(BF16)
            )
    accumulate(xs, acc_v, wv, 3)
    accumulate(xs, acc_b, (weights,), 3)

    @pl.when(last)
    def _():
        finish_rms(squares, WIDTH)
        for b in range(2):
            for r in range(0, tokens, CHUNK):
                at = r // CHUNK * heads
                steps[b, :, at : at + heads] = (
                    acc_b[b * rows + r : b * rows + r + CHUNK, state : state + heads]
                    * squares[r : r + CHUNK, :heads]
                )
            for r, out, size in placed(tokens):
                here = slice(b * rows + r, b * rows + r + size)
                scale = squares[r : r + size, :]
                for c in range(0, inner, TILE):
                    mix[b, c // TILE, out : out + size, :] = acc_v[here, c : c + TILE] * scale
                mix[b, inner // TILE, out : out + size, :] = acc_b[here, :state] * scale


def gate_kernel(*refs):
    hid, before, after, gain, wg, wc = (refs[2 * i : 2 * i + 2] for i in range(6))
    taps_ref, gate_ref, maps_ref, acc_g, acc_c, xs, squares, padded = refs[12:]
    k = pl.program_id(0)
    tokens = hid[0].shape[0]
    rows = tokens + 2 * HALO

    @pl.when(k == 0)
    def _():
        for acc in (acc_g, acc_c, squares):
            acc[...] = jnp.zeros_like(acc)

    scale_all(hid, before, after, gain, xs, squares)
    accumulate(xs, acc_g, wg, 3)
    accumulate(xs, acc_c, wc, 3)

    @pl.when(k == pl.num_programs(0) - 1)
    def _():
        finish_rms(squares, WIDTH)
        for b in range(2):
            for r in range(0, tokens, TILE):
                scale = squares[r : r + TILE, :]
                for c in range(0, gate_ref.shape[2], TILE):
                    gate_ref[b, r : r + TILE, c : c + TILE] = silu(
                        acc_g[b * rows + r : b * rows + r + TILE, c : c + TILE] * scale
                    )
            for r, out, size in placed(tokens):
                padded[out : out + size, :] = (
                    acc_c[b * rows + r : b * rows + r + size, :] * squares[r : r + size, :]
                )
            for r in range(0, tokens, ROWS):
                forward, backward = convolved(padded, r, taps_ref[...])
                maps_ref[b, 0, r : r + ROWS, :] = forward.astype(BF16)
                maps_ref[b, 1, r : r + ROWS, :] = backward.astype(BF16)


def convolved(source, row, taps):
    half = CONV - 1
    moved = [source[pl.ds(row + HALO + j, ROWS), :] for j in range(-half, half + 1)]
    forward = taps[0:1] * moved[0]
    backward = taps[0:1] * moved[2 * half]
    for o in range(1, CONV):
        forward = forward + taps[o : o + 1] * moved[o]
        backward = backward + taps[o : o + 1] * moved[2 * half - o]
    return silu(forward), silu(backward)


CONV = 4
DEPTH = 512
WIDTH = 4096


PAIRS = 4


def paired(block, index):
    held = lambda k: jnp.minimum(k, PAIRS - 1)
    return [
        pl.BlockSpec(block, lambda k: index(held(k))),
        pl.BlockSpec(block, lambda k: index(2 * PAIRS - 1 - held(k))),
    ]


def token_specs(tokens):
    across = lambda k: (0, k)
    return (
        paired((tokens, DEPTH), across)
        + paired((HALO, DEPTH), across)
        + paired((HALO, DEPTH), across)
        + paired((1, DEPTH), across)
    )


def project_gate(hidden, before, after, norm_gain, w_gate, w_bc, taps):
    tokens, width = hidden.shape
    inner, state = w_gate.shape[1], w_bc.shape[1] // 2
    rows = tokens + 2 * HALO
    return pl.pallas_call(
        gate_kernel,
        grid=(PAIRS,),
        in_specs=token_specs(tokens)
        + paired((DEPTH, inner), lambda k: (k, 0))
        + paired((DEPTH, state), lambda k: (k, 1))
        + [pl.BlockSpec((CONV, state), lambda k: (0, 1))],
        out_specs=[
            pl.BlockSpec((2, tokens, inner), lambda k: (0, 0, 0)),
            pl.BlockSpec((2, 2, tokens, state), lambda k: (0, 0, 0, 0)),
        ],
        out_shape=[
            jax.ShapeDtypeStruct((2, tokens, inner), F32),
            jax.ShapeDtypeStruct((2, 2, tokens, state), BF16),
        ],
        scratch_shapes=[
            pltpu.VMEM((2 * rows, inner), F32),
            pltpu.VMEM((2 * rows, state), F32),
            pltpu.VMEM((2 * rows, 2 * DEPTH), BF16),
            pltpu.VMEM((rows, TILE), F32),
            pltpu.VMEM((rows, TILE), F32),
        ],
        compiler_params=params(GRANT),
        cost_estimate=pl.CostEstimate(
            flops=4 * rows * width * (inner + state + FLIP),
            transcendentals=2 * tokens * inner,
            bytes_accessed=14 << 20,
        ),
        name="project_gate",
    )(*twice(hidden, before, after, norm_gain[None], w_gate, w_bc), taps)


def twice(*arrays):
    return [x for x in arrays for _ in range(2)]


def thirds(x):
    high = x.astype(BF16)
    rest = x - high.astype(F32)
    middle = rest.astype(BF16)
    return high, middle, (rest - middle.astype(F32)).astype(BF16)


def exact(matrix, x):
    high, middle, low = thirds(x)
    return dot(matrix, high) + dot(matrix, middle) + dot(matrix, low)


def conv_step(
    mix, steps, base_ref, tapv_ref, tapb_ref, bias_ref, rate_ref, skip_ref,
    direct_ref, xf_ref, xb_ref, maps_ref, cols_ref, rows_ref, enter_ref, final_ref,
    dt_sc, wf_sc, wb_sc, keep_sc, vf_sc, vb_sc, carry_sc,
):
    tokens, inner = direct_ref.shape[1:]
    heads = bias_ref.shape[1]
    width = inner // heads
    state = maps_ref.shape[3]
    chunks = tokens // CHUNK
    matrix = spreader(heads, width)

    def lanes_of(x):
        return jnp.concatenate([x] * chunks, axis=1)

    raw = steps[...] + lanes_of(bias_ref[...])
    dt = jnp.maximum(raw, 0.0) + jnp.log1p(jnp.exp(-jnp.abs(raw)))
    log_decay = -lanes_of(rate_ref[...]) * dt
    square = (CHUNK, CHUNK)
    lower = jnp.where(iota(square, 0) >= iota(square, 1), 1.0, 0.0).astype(BF16)
    inclusive = exact(lower, log_decay)
    exclusive = inclusive - log_decay
    last = inclusive[CHUNK - 1 : CHUNK]
    pad = jnp.zeros((CHUNK, TILE - chunks * heads), F32)
    turned = [jnp.concatenate([x, pad], axis=1).T for x in (inclusive, exclusive)]
    for c in range(chunks):
        mine = slice(c * heads, (c + 1) * heads)
        for q, x in enumerate(turned):
            rows_ref[0, c, q] = x[mine, :]
        select = selector(c, heads, chunks * heads, inner)
        at = slice(c * CHUNK, (c + 1) * CHUNK)
        dt_sc[at] = spread(dt, select)
        wf_sc[at] = spread(jnp.exp(last - inclusive), select)
        wb_sc[at] = spread(jnp.exp(exclusive), select)
    totals = [last[:, c * heads : (c + 1) * heads] for c in range(chunks)]
    zero = jnp.zeros_like(totals[0])
    before, after = [zero], [zero]
    for c in range(chunks - 1):
        before.append(before[-1] + totals[c])
        after.append(after[-1] + totals[chunks - 1 - c])
    after = after[::-1]
    everything = before[-1] + totals[-1]
    leaving = last - exclusive
    columns = (
        inclusive,
        exclusive,
        jnp.exp(inclusive),
        jnp.exp(leaving),
        jnp.exp(inclusive + jnp.concatenate(before, axis=1)),
        jnp.exp(leaving + jnp.concatenate(after, axis=1)),
    )
    for c in range(chunks):
        mine = slice(c * heads, (c + 1) * heads)
        cols_ref[0, c] = jnp.concatenate([x[:, mine] for x in columns], axis=1)
    chunk_decay = spread(jnp.exp(jnp.concatenate(totals + [zero] * (8 - chunks), axis=0)), matrix)
    sent_totals = jnp.concatenate(
        [dot(x, matrix) for x in thirds(everything)] + [jnp.zeros((16 - 3, inner), F32)], axis=0
    ).astype(BF16)

    keep = jnp.where(base_ref[...] != 4, 1.0, 0.0)
    keep = jnp.concatenate([keep, jnp.zeros((CHUNK - chunks, CHUNK), F32)], axis=0).T
    for c in range(chunks):
        keep_sc[c * CHUNK : (c + 1) * CHUNK] = jnp.broadcast_to(keep[:, c : c + 1], square)
    skip = spread(skip_ref[...], matrix)

    def block(i, carry):
        r = pl.multiple_of(i * ROWS, ROWS)
        here = pl.ds(r, ROWS)
        kept = keep_sc[here, :]
        for c in range(0, inner, TILE):
            lanes = slice(c, c + TILE)
            forward, backward = convolved(mix.at[c // TILE], r, tapv_ref[:, lanes])
            forward = forward * kept
            backward = backward * kept
            direct_ref[0, here, lanes] = skip[:, lanes] * (forward + backward)
            dt_lanes = dt_sc[here, lanes]
            forward = forward * dt_lanes
            backward = backward * dt_lanes
            xf_ref[0, here, lanes] = forward.astype(BF16)
            xb_ref[0, here, lanes] = backward.astype(BF16)
            vf_sc[here, lanes] = (forward * wf_sc[here, lanes]).astype(BF16)
            vb_sc[here, lanes] = (backward * wb_sc[here, lanes]).astype(BF16)
        forward, backward = convolved(mix.at[inner // TILE], r, tapb_ref[...])
        maps_ref[0, 0, here, :] = forward.astype(BF16)
        maps_ref[0, 1, here, :] = backward.astype(BF16)
        return carry

    lax.fori_loop(0, tokens // ROWS, block, 0)

    for direction, moved, order in ((0, vf_sc, range(chunks)), (1, vb_sc, range(chunks - 1, -1, -1))):
        for n, c in enumerate(order):
            at = slice(c * CHUNK, (c + 1) * CHUNK)
            gained = lax.dot_general(
                maps_ref[0, direction, at, :], moved[at, :], TN, preferred_element_type=F32
            )
            if n == 0:
                enter_ref[0, direction, c] = jnp.zeros(enter_ref.shape[3:], BF16)
                carry_sc[...] = gained
            else:
                enter_ref[0, direction, c] = carry_sc[...].astype(BF16)
                carry_sc[...] = carry_sc[...] * chunk_decay[c : c + 1, :] + gained
        for j in range(0, inner, TILE):
            final_ref[direction, 0, j // TILE, :state] = carry_sc[:, j : j + TILE].astype(BF16)
            final_ref[direction, 0, j // TILE, state:] = sent_totals[:, j : j + TILE]


COLUMNS = 6


def front_kernel(*refs):
    hid, before, after, gain, wv, wb, wst = (refs[2 * i : 2 * i + 2] for i in range(7))
    small, outs, scratch = refs[14:20], refs[20:28], refs[28:]
    acc_v, acc_b, xs, squares, weights, mix, steps = scratch[:7]
    i = pl.program_id(0)

    @pl.when(i == 0)
    def _():
        for acc in (acc_v, acc_b, squares):
            acc[...] = jnp.zeros_like(acc)

    @pl.when(i < PAIRS)
    def _():
        mix_step(
            hid, before, after, gain, wv, wb, wst, mix, steps, acc_v, acc_b, xs, squares, weights,
            i == PAIRS - 1,
        )

    @pl.when(i >= PAIRS)
    def _():
        b = i - PAIRS
        conv_step(mix.at[b], steps.at[b], *small, *outs, *scratch[7:])


def front(
    hidden, before, after, norm_gain, w_value, w_bc, w_step,
    base_ids, conv_value, conv_bc, step_bias, decay_rate, skip_gain,
):
    tokens, width = hidden.shape
    inner, state, heads = w_value.shape[1], w_bc.shape[1] // 2, w_step.shape[1]
    rows = tokens + 2 * HALO
    chunks = tokens // CHUNK
    branch = lambda k: jnp.maximum(k - PAIRS, 0)
    one = lambda k: (branch(k), 0, 0)
    flat = lambda k: (0, 0)
    four = lambda k: (branch(k), 0, 0, 0)
    five = lambda k: (branch(k), 0, 0, 0, 0)
    return pl.pallas_call(
        front_kernel,
        grid=(PAIRS + 2,),
        in_specs=token_specs(tokens)
        + paired((DEPTH, inner), lambda k: (k, 0))
        + paired((DEPTH, state), lambda k: (k, 0))
        + paired((heads, DEPTH), lambda k: (0, k))
        + [
            pl.BlockSpec((chunks, CHUNK), flat),
            pl.BlockSpec((CONV, inner), flat),
            pl.BlockSpec((CONV, state), flat),
            pl.BlockSpec((1, heads), flat),
            pl.BlockSpec((1, heads), flat),
            pl.BlockSpec((1, heads), flat),
        ],
        out_specs=[
            pl.BlockSpec((1, tokens, inner), one),
            pl.BlockSpec((1, tokens, inner), one),
            pl.BlockSpec((1, tokens, inner), one),
            pl.BlockSpec((1, 2, tokens, state), four),
            pl.BlockSpec((1, chunks, CHUNK, COLUMNS * heads), four),
            pl.BlockSpec((1, chunks, 2, heads, CHUNK), five),
            pl.BlockSpec((1, 2, chunks, state, inner), five),
            pl.BlockSpec((2, 1, inner // TILE, state + 16, TILE), lambda k: (0, branch(k), 0, 0, 0)),
        ],
        out_shape=[
            jax.ShapeDtypeStruct((2, tokens, inner), F32),
            jax.ShapeDtypeStruct((2, tokens, inner), BF16),
            jax.ShapeDtypeStruct((2, tokens, inner), BF16),
            jax.ShapeDtypeStruct((2, 2, tokens, state), BF16),
            jax.ShapeDtypeStruct((2, chunks, CHUNK, COLUMNS * heads), F32),
            jax.ShapeDtypeStruct((2, chunks, 2, heads, CHUNK), F32),
            jax.ShapeDtypeStruct((2, 2, chunks, state, inner), BF16),
            jax.ShapeDtypeStruct((2, 2, inner // TILE, state + 16, TILE), BF16),
        ],
        scratch_shapes=[
            pltpu.VMEM((2 * rows, inner), F32),
            pltpu.VMEM((2 * rows, state + TILE), F32),
            pltpu.VMEM((2 * rows, 2 * DEPTH), BF16),
            pltpu.VMEM((rows, TILE), F32),
            pltpu.VMEM((2 * DEPTH, state + TILE), BF16),
            pltpu.VMEM((2, (inner + state) // TILE, rows, TILE), F32),
            pltpu.VMEM((2, CHUNK, heads * chunks), F32),
            pltpu.VMEM((tokens, inner), F32),
            pltpu.VMEM((tokens, inner), F32),
            pltpu.VMEM((tokens, inner), F32),
            pltpu.VMEM((tokens, TILE), F32),
            pltpu.VMEM((tokens, inner), BF16),
            pltpu.VMEM((tokens, inner), BF16),
            pltpu.VMEM((state, inner), F32),
        ],
        compiler_params=params(GRANT),
        cost_estimate=pl.CostEstimate(
            flops=4 * rows * width * (inner + 2 * state + FLIP),
            transcendentals=1 << 22,
            bytes_accessed=24 << 20,
        ),
        name="front",
    )(
        *twice(hidden, before, after, norm_gain[None], w_value, w_bc, w_step.T),
        base_ids, conv_value, conv_bc, step_bias, decay_rate, skip_gain,
    )


def within_kernel(direct_ref, xf_ref, xb_ref, b_ref, c_ref, cols_ref, rows_ref, enter_ref, local_ref):
    heads = rows_ref.shape[3]
    inner = direct_ref.shape[2]
    width = inner // heads
    square = (CHUNK, CHUNK)
    below = iota(square, 0) >= iota(square, 1)
    above = iota(square, 0) <= iota(square, 1)
    scores_f = lax.dot_general(c_ref[0, 0], b_ref[0, 0], NT, preferred_element_type=F32)
    scores_b = lax.dot_general(c_ref[0, 1], b_ref[0, 1], NT, preferred_element_type=F32)
    scores_f = jnp.where(below, scores_f, 0.0)
    scores_b = jnp.where(above, scores_b, 0.0)
    left = iota((CHUNK, TILE), 1) < width
    cols = cols_ref[0, 0]
    across_f = dot(c_ref[0, 0], enter_ref[0, 0, 0]) * spread(
        cols, selector(2, heads, cols.shape[1], inner)
    )
    across_b = dot(c_ref[0, 1], enter_ref[0, 1, 0]) * spread(
        cols, selector(3, heads, cols.shape[1], inner)
    )
    local_ref[0] = direct_ref[0] + across_f + across_b
    for j in range(0, inner, TILE):
        lanes = slice(j, j + TILE)
        values = jnp.concatenate([xf_ref[0, :, lanes], xb_ref[0, :, lanes]], axis=0)
        parts = []
        for h in range(j // width, (j + TILE) // width):
            gap = jnp.where(
                below,
                cols[:, h : h + 1] - rows_ref[0, 0, 0, h : h + 1, :],
                rows_ref[0, 0, 1, h : h + 1, :] - cols[:, heads + h : heads + h + 1],
            )
            decay = jnp.exp(gap)
            weights = jnp.concatenate(
                [(decay * scores_f).astype(BF16), (decay * scores_b).astype(BF16)], axis=1
            )
            parts.append(dot(weights, values))
        local_ref[0, :, lanes] += jnp.where(left, parts[0], parts[1])


def within(direct, xf, xb, b_maps, c_maps, cols, rows, enter):
    tokens, inner = direct.shape[1:]
    state = b_maps.shape[3]
    heads = rows.shape[3]
    chunks = tokens // CHUNK
    token = lambda i: (i // chunks, i % chunks, 0)
    inside = lambda i: (i // chunks, 0, i % chunks, 0)
    return pl.pallas_call(
        within_kernel,
        grid=(2 * chunks,),
        in_specs=[
            pl.BlockSpec((1, CHUNK, inner), token),
            pl.BlockSpec((1, CHUNK, inner), token),
            pl.BlockSpec((1, CHUNK, inner), token),
            pl.BlockSpec((1, 2, CHUNK, state), inside),
            pl.BlockSpec((1, 2, CHUNK, state), inside),
            pl.BlockSpec((1, 1, CHUNK, cols.shape[3]), lambda i: (i // chunks, i % chunks, 0, 0)),
            pl.BlockSpec((1, 1, 2, heads, CHUNK), lambda i: (i // chunks, i % chunks, 0, 0, 0)),
            pl.BlockSpec((1, 2, 1, state, inner), lambda i: (i // chunks, 0, i % chunks, 0, 0)),
        ],
        out_specs=pl.BlockSpec((1, CHUNK, inner), token),
        out_shape=jax.ShapeDtypeStruct((2, tokens, inner), F32),
        compiler_params=params(GRANT),
        cost_estimate=pl.CostEstimate(flops=4 << 30, transcendentals=1 << 22, bytes_accessed=16 << 20),
        name="within",
    )(direct, xf, xb, b_maps, c_maps, cols, rows, enter)


def chain_kernel(states_ref, incoming_ref):
    count = states_ref.shape[0]
    state = incoming_ref.shape[1]
    backward = lax.axis_index("ctx") >= count // 2
    carry = jnp.zeros(incoming_ref.shape[1:], F32)
    for n in range(count):
        at = jnp.where(backward, count - 1 - n, n)
        incoming_ref[at] = carry.astype(incoming_ref.dtype)
        total = jnp.sum(states_ref[at, state:, :].astype(F32), axis=0, keepdims=True)
        carry = carry * jnp.exp(total) + states_ref[at, :state, :].astype(F32)


def chain(states):
    count, rows, tile = states.shape
    return pl.pallas_call(
        chain_kernel,
        out_shape=jax.ShapeDtypeStruct((count, rows - 16, tile), BF16),
        compiler_params=pltpu.CompilerParams(vmem_limit_bytes=16 << 20),
        cost_estimate=pl.CostEstimate(flops=1 << 20, transcendentals=0, bytes_accessed=2 << 20),
        name="chain",
    )(states)


ORDERS = ((2, 6, 1), (6, 1, 2), (1, 2, 6))
GROUPS = ((0, 176), (176, 176), (352, 160))
STEPS = (2, 3, 0, 1)
PARTS = 8


def kept_blocks(order):
    kept = {0}
    for partner in order[1:]:
        kept |= {k ^ partner for k in kept}
    return kept


def slots(order):
    kept = kept_blocks(order)
    given = [r for s in STEPS for r in (s, PARTS - 1 - s)]
    return [r for r in given if r not in kept], [r for r in given if r in kept]


def normalise(row, b, local_ref, silu_ref, c_ref, cols_ref, incoming_ref, gain_ref, normed):
    size, inner = local_ref.shape[1:]
    columns = cols_ref.shape[3]
    heads = columns // COLUMNS
    width = inner // heads
    cols = cols_ref[0].reshape(size, columns)
    shape = (FLIP, FLIP)
    group = jnp.where(iota(shape, 0) // width == iota(shape, 1) // width, 1.0, 0.0).astype(BF16)
    scale_f = spread(cols, selector(4, heads, columns, inner))
    scale_b = spread(cols, selector(5, heads, columns, inner))
    for j in range(0, inner, FLIP):
        lanes = slice(j, j + FLIP)
        tiles = range(j // TILE, (j + FLIP) // TILE)
        into_f = jnp.concatenate([incoming_ref[0, 0, t] for t in tiles], axis=1)
        into_b = jnp.concatenate([incoming_ref[1, 0, t] for t in tiles], axis=1)
        y = local_ref[0, :, lanes]
        y = y + scale_f[:, lanes] * dot(c_ref[0, 0], into_f)
        y = y + scale_b[:, lanes] * dot(c_ref[0, 1], into_b)
        y = y * silu_ref[0, :, lanes]
        square = y * y
        high = square.astype(BF16)
        low = (square - high.astype(F32)).astype(BF16)
        mean = (dot(high, group) + dot(low, group)) * (1.0 / width)
        y = y * lax.rsqrt(mean + EPSILON) * gain_ref[:, lanes]
        normed[b, pl.ds(pl.multiple_of(row, size), size), lanes] = y.astype(BF16)


def output_kernel(
    place_ref, local_ref, silu_ref, c_ref, cols_ref, incoming_ref, gain_ref, wout_ref, wmir_ref, *rest
):
    outs, (normed, mirrored, product) = rest[:-3], rest[-3:]
    i = pl.program_id(0)
    size = local_ref.shape[1]
    halves = normed.shape[1] // size
    pre = 2 * halves
    slab = wout_ref.shape[1]

    @pl.when(i < pre)
    def _():
        normalise(
            (i % halves) * size, i // halves, local_ref, silu_ref, c_ref, cols_ref, incoming_ref,
            gain_ref, normed,
        )

    @pl.when(i >= pre)
    def _():
        flip = reversal(FLIP)
        straight = (wout_ref, wmir_ref)
        for n in range(2):
            source = straight[1 - n]
            for c in range(0, slab, FLIP):
                at = slab - FLIP - c
                mirrored[:, c : c + FLIP] = dot(source[:, at : at + FLIP], flip).astype(BF16)
            product[n] = dot(normed[0], straight[n][...]) + dot(normed[1], mirrored[...])

    for t, step in enumerate(STEPS):

        @pl.when(i == pre + t)
        def _():
            for g, (order, (row, rows)) in enumerate(zip(ORDERS, GROUPS)):
                sent, kept = slots(order)
                for n, block in enumerate((step, PARTS - 1 - step)):
                    ref, held = (outs[2 * g], sent) if block in sent else (outs[2 * g + 1], kept)
                    at = held.index(block) % ref.shape[0]
                    ref[at] = product[n, row : row + rows, :].astype(ref.dtype)


def output(local, gate, c_maps, cols, incoming, gain, w_out):
    tokens, inner = local.shape[1:]
    state = c_maps.shape[3]
    chunks = tokens // CHUNK
    size = 2 * CHUNK
    halves = tokens // size
    pre = 2 * halves
    slab = w_out.shape[1] // PARTS
    held = lambda i: jnp.minimum(i, pre - 1)
    token = lambda i, n: (held(i) // halves, held(i) % halves, 0)
    block = lambda i, n: n[0] ^ (jnp.maximum(i - pre, 0) ^ STEPS[0])
    late = lambda i: jnp.maximum(i - pre, 0)
    out_specs, out_shape = [], []
    for order, (_, rows) in zip(ORDERS, GROUPS):
        sent, _ = slots(order)
        if {STEPS[0], PARTS - 1 - STEPS[0]} <= set(sent):
            per, places = 2, (lambda i, n: (jnp.minimum(late(i), 1), 0, 0), lambda i, n: (jnp.maximum(late(i) - 2, 0), 0, 0))
        else:
            per, places = 1, (lambda i, n: (late(i), 0, 0),) * 2
        for place, dtype in zip(places, (BF16, F32)):
            out_specs.append(pl.BlockSpec((per, rows, slab), place))
            out_shape.append(jax.ShapeDtypeStruct((PARTS // 2, rows, slab), dtype))
    return pl.pallas_call(
        output_kernel,
        grid_spec=pltpu.PrefetchScalarGridSpec(
            num_scalar_prefetch=1,
            grid=(pre + len(STEPS),),
            in_specs=[
                pl.BlockSpec((1, size, inner), token),
                pl.BlockSpec((1, size, inner), token),
                pl.BlockSpec((1, 2, size, state), lambda i, n: (held(i) // halves, 0, held(i) % halves, 0)),
                pl.BlockSpec(
                    (1, size // CHUNK, CHUNK, cols.shape[3]),
                    lambda i, n: (held(i) // halves, held(i) % halves, 0, 0),
                ),
                pl.BlockSpec(
                    (2, 1, inner // TILE, state, TILE), lambda i, n: (0, held(i) // halves, 0, 0, 0)
                ),
                pl.BlockSpec((1, inner), lambda i, n: (0, 0)),
                pl.BlockSpec((inner, slab), lambda i, n: (0, block(i, n))),
                pl.BlockSpec((inner, slab), lambda i, n: (0, PARTS - 1 - block(i, n))),
            ],
            out_specs=out_specs,
            scratch_shapes=[
                pltpu.VMEM((2, tokens, inner), BF16),
                pltpu.VMEM((inner, slab), BF16),
                pltpu.VMEM((2, tokens, slab), F32),
            ],
        ),
        out_shape=out_shape,
        compiler_params=params(GRANT),
        cost_estimate=pl.CostEstimate(flops=6 << 30, transcendentals=1 << 20, bytes_accessed=20 << 20),
        name="output",
    )(lax.axis_index("head")[None], local, gate, c_maps, cols, incoming, gain, w_out, w_out)


def reduced(send, keep, order):
    sent, kept = slots(order)
    for n, partner in enumerate(order):
        pairs = [(i, i ^ partner) for i in range(PARTS)]
        arrived = lax.ppermute(send, "head", pairs)
        arrived_as = [r ^ partner for r in sent]

        def total(block):
            return keep[kept.index(block)] + arrived[arrived_as.index(block)].astype(F32)

        if n == len(order) - 1:
            return total(0).astype(BF16)
        following = order[n + 1]
        rest = {0}
        for other in order[n + 2 :]:
            rest |= {k ^ other for k in rest}
        new_kept = [r for r in kept if r in rest]
        new_sent = [r ^ following for r in new_kept]
        send = jnp.stack([total(r).astype(BF16) for r in new_sent])
        keep = jnp.stack([total(r) for r in new_kept])
        sent, kept = new_sent, new_kept


def shards(
    hidden,
    base_ids,
    norm_gain,
    w_gate,
    w_value,
    w_bc,
    w_step,
    conv_value,
    conv_bc,
    step_bias,
    decay_rate,
    skip_gain,
    out_gain,
    w_out,
):
    count = lax.axis_size("ctx")
    up = [(i, i + 1) for i in range(count - 1)]
    down = [(j, i) for i, j in up]
    before = lax.ppermute(hidden[-HALO:], "ctx", up)
    after = lax.ppermute(hidden[:HALO], "ctx", down)
    direct, xf, xb, b_maps, cols, rows, enter, final = front(
        hidden, before, after, norm_gain, w_value, w_bc, w_step,
        base_ids.reshape(-1, CHUNK),
        conv_value,
        conv_bc,
        step_bias[None],
        decay_rate[None],
        skip_gain[None],
    )
    state, tile = final.shape[3:]
    sent = lax.all_to_all(final.reshape(count, state, tile), "ctx", 0, 0)
    gate, c_maps = project_gate(hidden, before, after, norm_gain, w_gate, w_bc, conv_bc)
    sent, gate, c_maps = lax.optimization_barrier((sent, gate, c_maps))
    incoming = lax.all_to_all(chain(sent), "ctx", 0, 0)
    incoming = incoming.reshape(final.shape[:3] + incoming.shape[1:])
    local = within(direct, xf, xb, b_maps, c_maps, cols, rows, enter)
    outs = output(local, gate, c_maps, cols, incoming, out_gain[None], w_out)
    return jnp.concatenate(
        [reduced(outs[2 * g], outs[2 * g + 1], order) for g, order in enumerate(ORDERS)], axis=0
    )


def solution(mesh):
    return jax.shard_map(
        shards,
        mesh=mesh,
        in_specs=(
            P("ctx", None),
            P("ctx"),
            P(),
            P(None, "head"),
            P(None, "head"),
            P(),
            P(None, "head"),
            P(None, "head"),
            P(),
            P("head"),
            P("head"),
            P("head"),
            P("head"),
            P("head", None),
        ),
        out_specs=P("ctx", "head"),
        check_vma=False,
    )
```

time: 152 us -> 128 us (0.84)
  Pallas kernels: 85.3 us -> 59.9 us
  starting transfers between devices: 34.2 us -> 38 us
    pallas_call x7 -> x4, Pallas kernels: 84.4 us -> 58.9 us  [the longest x1 20.4 us: front(): pl.pallas_call(front_kernel, grid=(PAIRS + 2,), in_specs=token_specs(toke...]
    ppermute x9, waiting for transfers between devices: 24.8 us -> 19.3 us  [reduced(): arrived = lax.ppermute(send, 'head', pairs)]
    ppermute x9, starting transfers between devices: 14.7 us -> 20.1 us  [reduced(): arrived = lax.ppermute(send, 'head', pairs)]
    ppermute x1, waiting for transfers between devices: 0.01 us -> 3.72 us  [shards(): after = lax.ppermute(hidden[:HALO], 'ctx', down)]
    ppermute x1, starting transfers between devices: 3.03 us -> 1.29 us  [shards(): before = lax.ppermute(hidden[-HALO:], 'ctx', up)]
  transfers between devices with their start and end apart: 13 -> 13, of which waited for: 8 -> 8; matrix products, arithmetic and copies ran while one was open for 2% -> 1% of each run, Pallas kernels for 23% -> 18%
where the time goes in v3:
time: 128 us
  Pallas kernels  59.9 us (47%)
  starting transfers between devices  38 us (30%)
  waiting for transfers between devices  24.5 us (19%)
  other arithmetic  2.76 us (2%)
  local copies, waits for them, and re-layouts  2.3 us (2%)
    pallas_call x1, Pallas kernels, front(): pl.pallas_call(front_kernel, grid=(PAIRS + 2,), in_specs=token_specs(toke...  20.4 us
    ppermute x9, starting transfers between devices, reduced(): arrived = lax.ppermute(send, 'head', pairs)  20.1 us
    ppermute x9, waiting for transfers between devices, reduced(): arrived = lax.ppermute(send, 'head', pairs)  19.3 us
    pallas_call x1, Pallas kernels, output(): pl.pallas_call(output_kernel, grid_spec=pltpu.PrefetchScalarGridSpec(num_...  15.3 us
    pallas_call x1, Pallas kernels, project_gate(): pl.pallas_call(gate_kernel, grid=(PAIRS,), in_specs=token_specs(tokens) +...  13.8 us
    all_to_all x1, starting transfers between devices, shards(): sent = lax.all_to_all(final.reshape(count, state, tile), 'ctx', 0, 0)  9.64 us
    pallas_call x1, Pallas kernels, within(): pl.pallas_call(within_kernel, grid=(2 * chunks,), in_specs=[pl.BlockSpec(...  9.4 us
    all_to_all x1, starting transfers between devices, shards(): incoming = lax.all_to_all(chain(sent), 'ctx', 0, 0)  5.68 us
  transfers between devices with their start and end apart: 13, of which 8 were waited for; matrix products, arithmetic and copies ran while one was open for 1% of the time, Pallas kernels for 18%

profile of v3, /device:TPU:0, one launch (start us, length us, event | category | flops | bytes accessed | tf_op | source)
XLA Modules:
  0.0 127.6 jit_solution(4278413394120292644)
XLA Ops:
  0.9 1.3 %collective-permute-start = (bf16[8,4096]{1,0:T(8,128)(2,1)S(1)}, bf16[8,4096]{1,0:T(8,128)(2,1)S(1)}, u32[]{:S(2)}, u32[]{:S(2)}) collective-permute-start(bf16[8,4096]{1,0:T(8,128)(2,1)S(1)} %get-tuple-element.44), channel_id=1, source_target_pairs={{0,8},{8,16},{16,24},{24,32},{32,40},{40,48},{48,56},{56,64},{64,7... | collective-permute-start | bytes 196616 | tf_op jit(solution)/shard_map/ppermute | solution.py:767
  2.2 1.3 %collective-permute-start.1 = (bf16[8,4096]{1,0:T(8,128)(2,1)S(1)}, bf16[8,4096]{1,0:T(8,128)(2,1)S(1)}, u32[]{:S(2)}, u32[]{:S(2)}) collective-permute-start(bf16[8,4096]{1,0:T(8,128)(2,1)S(1)} %get-tuple-element.43), channel_id=1, source_target_pairs={{8,0},{16,8},{24,16},{32,24},{40,32},{48,40},{56,48},{64,56},{72,6... | collective-permute-start | bytes 196616 | tf_op jit(solution)/shard_map/ppermute | solution.py:768
  3.5 3.7 %collective-permute-done.1.refs_4_.refs_5_ = bf16[8,4096]{1,0:T(8,128)(2,1)S(1)} collective-permute-done((bf16[8,4096]{1,0:T(8,128)(2,1)S(1)}, bf16[8,4096]{1,0:T(8,128)(2,1)S(1)}, u32[]{:S(2)}, u32[]{:S(2)}) %collective-permute-start.1) | collective-permute-done | bytes 65568 | tf_op jit(solution)/shard_map/ppermute | solution.py:768
  7.8 20.4 %front.1 = (f32[2,512,512]{2,1,0:T(8,128)}, bf16[2,512,512]{2,1,0:T(8,128)(2,1)}, bf16[2,512,512]{2,1,0:T(8,128)(2,1)}, bf16[2,2,512,128]{3,2,1,0:T(8,128)(2,1)}...) custom-call(bf16[512,4096]{1,0:T(8,128)(2,1)} %refs_1_.3, ...), custom_call_target="tpu_custom_call" | custom-call | flops 8858370048 | bytes 25165824 | tf_op jit(solution)/shard_map/front/pallas_call | solution.py:430
  28.3 9.6 %all-to-all-start = ((bf16[16,144,128]{2,1,0:T(8,128)(2,1)}), bf16[16,144,128]{2,1,0:T(8,128)(2,1)S(1)}, u32[]{:S(2)}, u32[]{:S(2)}) async-start(bf16[16,144,128]{2,1,0:T(8,128)(2,1)} %bitcast.16), calls=%async_computation | async-start | bytes 1179648 | tf_op jit(solution)/shard_map/all_to_all | solution.py:779
  37.9 13.8 %project_gate.1 = (f32[2,512,512]{2,1,0:T(8,128)}, bf16[2,2,512,128]{3,2,1,0:T(8,128)(2,1)}) custom-call(bf16[512,4096]{1,0:T(8,128)(2,1)} %refs_1_.3, bf16[512,4096]{1,0:T(8,128)(2,1)} %refs_1_.3, bf16[8,4096]{1,0:T(8,128)(2,1)} %copy-done.4, bf16[8,4096]{1,0:T(8,128)(2,1)} %copy-done.4, bf16[8,4096]{1,0:T(8,128)(2,1)} %copy-done.5, ...), custom_call_target="tpu_custom_call" | custom-call | flops 7751073792 | bytes 14680064 | tf_op jit(solution)/shard_map/project_gate/pallas_call | solution.py:236
  52.7 5.7 %all-to-all-start.1 = ((bf16[16,128,128]{2,1,0:T(8,128)(2,1)}), bf16[16,128,128]{2,1,0:T(8,128)(2,1)S(1)}, u32[]{:S(2)}, u32[]{:S(2)}) async-start(bf16[16,128,128]{2,1,0:T(8,128)(2,1)} %chain.1), calls=%async_computation.1 | async-start | bytes 1048576 | tf_op jit(solution)/shard_map/all_to_all | solution.py:782
  58.4 9.4 %within.1.local_ref = f32[2,512,512]{2,1,0:T(8,128)} custom-call(f32[2,512,512]{2,1,0:T(8,128)} %get-tuple-element.24.direct_ref, bf16[2,512,512]{2,1,0:T(8,128)(2,1)} %get-tuple-element.25.xf_ref, bf16[2,512,512]{2,1,0:T(8,128)(2,1)} %get-tuple-element.26.xb_ref, bf16[2,2,512,128]{3,2,1,0:T(8,128)(2,1)} %get-tuple-element.27.b_ref, ...), custom_call_target="tpu_custom_call" | custom-call | flops 4294967296 | bytes 16777216 | tf_op jit(solution)/shard_map/within/pallas_call | solution.py:539
  67.8 1.5 %all-to-all-done.1 = bf16[16,128,128]{2,1,0:T(8,128)(2,1)S(1)} async-done(((bf16[16,128,128]{2,1,0:T(8,128)(2,1)}), bf16[16,128,128]{2,1,0:T(8,128)(2,1)S(1)}, u32[]{:S(2)}, u32[]{:S(2)}) %all-to-all-start.1) | async-done | bytes 524320 | tf_op jit(solution)/shard_map/all_to_all | solution.py:782
  70.0 15.3 %output.1 = (bf16[4,176,512]{2,1,0:T(8,128)(2,1)}, f32[4,176,512]{2,1,0:T(8,128)}, bf16[4,176,512]{2,1,0:T(8,128)(2,1)}, f32[4,176,512]{2,1,0:T(8,128)}, bf16[4,...) custom-call(s32[1]{0:T(128)} %bitcast.place_ref, f32[2,512,512]{2,1,0:T(8,128)} %within.1.local_ref, ...), custom_call_target="tpu_custom_call" | custom-call | flops 6442450944 | bytes 20971520 | tf_op jit(solution)/shard_map/output/pallas_call | solution.py:691
  85.4 3.3 %collective-permute-start.8 = (bf16[4,160,512]{2,1,0:T(8,128)(2,1)}, bf16[4,160,512]{2,1,0:T(8,128)(2,1)S(1)}, u32[]{:S(2)}, u32[]{:S(2)}) collective-permute-start(bf16[4,160,512]{2,1,0:T(8,128)(2,1)} %get-tuple-element.42), channel_id=1, source_target_pairs={{0,1},{1,0},{2,3},{3,2},{4,5},{5,4},{6,7},{7,6},{8,9},{9,8},{10,11... | collective-permute-start | bytes 1966088 | tf_op jit(solution)/shard_map/ppermute | solution.py:729
  88.6 1.5 %collective-permute-start.2 = (bf16[4,176,512]{2,1,0:T(8,128)(2,1)}, bf16[4,176,512]{2,1,0:T(8,128)(2,1)S(1)}, u32[]{:S(2)}, u32[]{:S(2)}) collective-permute-start(bf16[4,176,512]{2,1,0:T(8,128)(2,1)} %get-tuple-element.38), channel_id=1, source_target_pairs={{0,2},{1,3},{2,0},{3,1},{4,6},{5,7},{6,4},{7,5},{8,10},{9,11},{10,... | collective-permute-start | bytes 2162696 | tf_op jit(solution)/shard_map/ppermute | solution.py:729
  90.1 2.1 %collective-permute-start.5 = (bf16[4,176,512]{2,1,0:T(8,128)(2,1)}, bf16[4,176,512]{2,1,0:T(8,128)(2,1)S(1)}, u32[]{:S(2)}, u32[]{:S(2)}) collective-permute-start(bf16[4,176,512]{2,1,0:T(8,128)(2,1)} %get-tuple-element.40), channel_id=1, source_target_pairs={{0,6},{1,7},{2,4},{3,5},{4,2},{5,3},{6,0},{7,1},{8,14},{9,15},{10,... | collective-permute-start | bytes 2162696 | tf_op jit(solution)/shard_map/ppermute | solution.py:729
  92.2 10.9 %collective-permute-done.8 = bf16[4,160,512]{2,1,0:T(8,128)(2,1)S(1)} collective-permute-done((bf16[4,160,512]{2,1,0:T(8,128)(2,1)}, bf16[4,160,512]{2,1,0:T(8,128)(2,1)S(1)}, u32[]{:S(2)}, u32[]{:S(2)}) %collective-permute-start.8) | collective-permute-done | bytes 655392 | tf_op jit(solution)/shard_map/ppermute | solution.py:729
  103.2 1.2 add_convert_fusion.11
  104.4 1.6 %collective-permute-start.9 = (bf16[2,160,512]{2,1,0:T(8,128)(2,1)S(1)}, bf16[2,160,512]{2,1,0:T(8,128)(2,1)S(1)}, u32[]{:S(2)}, u32[]{:S(2)}) collective-permute-start(bf16[2,160,512]{2,1,0:T(8,128)(2,1)S(1)} %pad_maximum_fusion.3), channel_id=1, source_target_pairs={{0,2},{1,3},{2,0},{3,1},{4,6},{5,7},{6,4},{7,5},{8,10},{9,11},{10,... | collective-permute-start | bytes 983048 | tf_op jit(solution)/shard_map/ppermute | solution.py:729
  106.6 2.8 %collective-permute-start.3 = (bf16[2,176,512]{2,1,0:T(8,128)(2,1)S(1)}, bf16[2,176,512]{2,1,0:T(8,128)(2,1)S(1)}, u32[]{:S(2)}, u32[]{:S(2)}) collective-permute-start(bf16[2,176,512]{2,1,0:T(8,128)(2,1)S(1)} %pad_maximum_fusion.1), channel_id=1, source_target_pairs={{0,6},{1,7},{2,4},{3,5},{4,2},{5,3},{6,0},{7,1},{8,14},{9,15},{10,... | collective-permute-start | bytes 1081352 | tf_op jit(solution)/shard_map/ppermute | solution.py:729
  109.6 2.2 %collective-permute-start.6 = (bf16[2,176,512]{2,1,0:T(8,128)(2,1)S(1)}, bf16[2,176,512]{2,1,0:T(8,128)(2,1)S(1)}, u32[]{:S(2)}, u32[]{:S(2)}) collective-permute-start(bf16[2,176,512]{2,1,0:T(8,128)(2,1)S(1)} %pad_maximum_fusion.2), channel_id=1, source_target_pairs={{0,1},{1,0},{2,3},{3,2},{4,5},{5,4},{6,7},{7,6},{8,9},{9,8},{10,11... | collective-permute-start | bytes 1081352 | tf_op jit(solution)/shard_map/ppermute | solution.py:729
  111.7 1.3 %collective-permute-done.9 = bf16[2,160,512]{2,1,0:T(8,128)(2,1)S(1)} collective-permute-done((bf16[2,160,512]{2,1,0:T(8,128)(2,1)S(1)}, bf16[2,160,512]{2,1,0:T(8,128)(2,1)S(1)}, u32[]{:S(2)}, u32[]{:S(2)}) %collective-permute-start.9) | collective-permute-done | bytes 327712 | tf_op jit(solution)/shard_map/ppermute | solution.py:729
  113.1 2.8 %collective-permute-start.10 = (bf16[1,160,512]{2,1,0:T(8,128)(2,1)S(1)}, bf16[1,160,512]{2,1,0:T(8,128)(2,1)S(1)}, u32[]{:S(2)}, u32[]{:S(2)}) collective-permute-start(bf16[1,160,512]{2,1,0:T(8,128)(2,1)S(1)} %add_convert_fusion.9), channel_id=1, source_target_pairs={{0,6},{1,7},{2,4},{3,5},{4,2},{5,3},{6,0},{7,1},{8,14},{9,15},{10,... | collective-permute-start | bytes 491528 | tf_op jit(solution)/shard_map/ppermute | solution.py:729
  115.9 1.3 %collective-permute-done.3 = bf16[2,176,512]{2,1,0:T(8,128)(2,1)S(1)} collective-permute-done((bf16[2,176,512]{2,1,0:T(8,128)(2,1)S(1)}, bf16[2,176,512]{2,1,0:T(8,128)(2,1)S(1)}, u32[]{:S(2)}, u32[]{:S(2)}) %collective-permute-start.3) | collective-permute-done | bytes 360480 | tf_op jit(solution)/shard_map/ppermute | solution.py:729
  117.3 3.7 %collective-permute-start.4 = (bf16[1,176,512]{2,1,0:T(8,128)(2,1)S(1)}, bf16[1,176,512]{2,1,0:T(8,128)(2,1)S(1)}, u32[]{:S(2)}, u32[]{:S(2)}) collective-permute-start(bf16[1,176,512]{2,1,0:T(8,128)(2,1)S(1)} %add_convert_fusion.5), channel_id=1, source_target_pairs={{0,1},{1,0},{2,3},{3,2},{4,5},{5,4},{6,7},{7,6},{8,9},{9,8},{10,11... | collective-permute-start | bytes 540680 | tf_op jit(solution)/shard_map/ppermute | solution.py:729
  121.2 3.2 %collective-permute-done.4 = bf16[1,176,512]{2,1,0:T(8,128)(2,1)S(1)} collective-permute-done((bf16[1,176,512]{2,1,0:T(8,128)(2,1)S(1)}, bf16[1,176,512]{2,1,0:T(8,128)(2,1)S(1)}, u32[]{:S(2)}, u32[]{:S(2)}) %collective-permute-start.4) | collective-permute-done | bytes 180256 | tf_op jit(solution)/shard_map/ppermute | solution.py:729
  124.5 2.1 %collective-permute-done.7 = bf16[1,176,512]{2,1,0:T(8,128)(2,1)S(1)} collective-permute-done((bf16[1,176,512]{2,1,0:T(8,128)(2,1)S(1)}, bf16[1,176,512]{2,1,0:T(8,128)(2,1)S(1)}, u32[]{:S(2)}, u32[]{:S(2)}) %collective-permute-start.7) | collective-permute-done | bytes 180256 | tf_op jit(solution)/shard_map/ppermute | solution.py:729
  (33 shorter events, 5.4 us)
Async XLA Ops:
  0.9 2.6 %collective-permute-start = (bf16[8,4096]{1,0:T(8,128)(2,1)S(1)}, bf16[8,4096]{1,0:T(8,128)(2,1)S(1)}, u32[]{:S(2)}, u32[]{:S(2)}) collective-permute-start(bf16[8,4096]{1,0:T(8,128)(2,1)S(1)} %get-tuple-element.44), channel_id=1, source_target_pairs={{0,8},{8,16},{16,24},{24,32},{32,40},{40,48},{48,56},{56,64},{64,7... | collective-permute-start | bytes 196616 | tf_op jit(solution)/shard_map/ppermute | solution.py:767
  2.2 5.0 %collective-permute-start.1 = (bf16[8,4096]{1,0:T(8,128)(2,1)S(1)}, bf16[8,4096]{1,0:T(8,128)(2,1)S(1)}, u32[]{:S(2)}, u32[]{:S(2)}) collective-permute-start(bf16[8,4096]{1,0:T(8,128)(2,1)S(1)} %get-tuple-element.43), channel_id=1, source_target_pairs={{8,0},{16,8},{24,16},{32,24},{40,32},{48,40},{56,48},{64,56},{72,6... | collective-permute-start | bytes 196616 | tf_op jit(solution)/shard_map/ppermute | solution.py:768
  3.5 3.7 %copy-start.4 = (bf16[8,4096]{1,0:T(8,128)(2,1)}, bf16[8,4096]{1,0:T(8,128)(2,1)S(1)}, u32[]{:S(2)}) copy-start(bf16[8,4096]{1,0:T(8,128)(2,1)S(1)} %collective-permute-done.refs_2_.refs_3_) | copy-start | bytes 196612
  7.2 0.6 copy-start.5
  28.3 23.5 %all-to-all-start = ((bf16[16,144,128]{2,1,0:T(8,128)(2,1)}), bf16[16,144,128]{2,1,0:T(8,128)(2,1)S(1)}, u32[]{:S(2)}, u32[]{:S(2)}) async-start(bf16[16,144,128]{2,1,0:T(8,128)(2,1)} %bitcast.16), calls=%async_computation | async-start | bytes 1179648 | tf_op jit(solution)/shard_map/all_to_all | solution.py:779
  52.7 16.6 %all-to-all-start.1 = ((bf16[16,128,128]{2,1,0:T(8,128)(2,1)}), bf16[16,128,128]{2,1,0:T(8,128)(2,1)S(1)}, u32[]{:S(2)}, u32[]{:S(2)}) async-start(bf16[16,128,128]{2,1,0:T(8,128)(2,1)} %chain.1), calls=%async_computation.1 | async-start | bytes 1048576 | tf_op jit(solution)/shard_map/all_to_all | solution.py:782
  69.2 0.8 copy-start.3
  85.4 21.1 %copy-start.1 = (f32[4,176,512]{2,1,0:T(8,128)S(1)}, f32[4,176,512]{2,1,0:T(8,128)}, u32[]{:S(2)}) copy-start(f32[4,176,512]{2,1,0:T(8,128)} %get-tuple-element.37) | copy-start | bytes 4325380
  85.4 17.8 %collective-permute-start.8 = (bf16[4,160,512]{2,1,0:T(8,128)(2,1)}, bf16[4,160,512]{2,1,0:T(8,128)(2,1)S(1)}, u32[]{:S(2)}, u32[]{:S(2)}) collective-permute-start(bf16[4,160,512]{2,1,0:T(8,128)(2,1)} %get-tuple-element.42), channel_id=1, source_target_pairs={{0,1},{1,0},{2,3},{3,2},{4,5},{5,4},{6,7},{7,6},{8,9},{9,8},{10,11... | collective-permute-start | bytes 1966088 | tf_op jit(solution)/shard_map/ppermute | solution.py:729
  88.6 17.8 %collective-permute-start.2 = (bf16[4,176,512]{2,1,0:T(8,128)(2,1)}, bf16[4,176,512]{2,1,0:T(8,128)(2,1)S(1)}, u32[]{:S(2)}, u32[]{:S(2)}) collective-permute-start(bf16[4,176,512]{2,1,0:T(8,128)(2,1)} %get-tuple-element.38), channel_id=1, source_target_pairs={{0,2},{1,3},{2,0},{3,1},{4,6},{5,7},{6,4},{7,5},{8,10},{9,11},{10,... | collective-permute-start | bytes 2162696 | tf_op jit(solution)/shard_map/ppermute | solution.py:729
  90.1 19.3 %collective-permute-start.5 = (bf16[4,176,512]{2,1,0:T(8,128)(2,1)}, bf16[4,176,512]{2,1,0:T(8,128)(2,1)S(1)}, u32[]{:S(2)}, u32[]{:S(2)}) collective-permute-start(bf16[4,176,512]{2,1,0:T(8,128)(2,1)} %get-tuple-element.40), channel_id=1, source_target_pairs={{0,6},{1,7},{2,4},{3,5},{4,2},{5,3},{6,0},{7,1},{8,14},{9,15},{10,... | collective-permute-start | bytes 2162696 | tf_op jit(solution)/shard_map/ppermute | solution.py:729
  104.3 5.1 %copy-start = (f32[4,176,512]{2,1,0:T(8,128)S(1)}, f32[4,176,512]{2,1,0:T(8,128)}, u32[]{:S(2)}) copy-start(f32[4,176,512]{2,1,0:T(8,128)} %get-tuple-element.39) | copy-start | bytes 4325380
  104.4 8.6 %collective-permute-start.9 = (bf16[2,160,512]{2,1,0:T(8,128)(2,1)S(1)}, bf16[2,160,512]{2,1,0:T(8,128)(2,1)S(1)}, u32[]{:S(2)}, u32[]{:S(2)}) collective-permute-start(bf16[2,160,512]{2,1,0:T(8,128)(2,1)S(1)} %pad_maximum_fusion.3), channel_id=1, source_target_pairs={{0,2},{1,3},{2,0},{3,1},{4,6},{5,7},{6,4},{7,5},{8,10},{9,11},{10,... | collective-permute-start | bytes 983048 | tf_op jit(solution)/shard_map/ppermute | solution.py:729
  106.5 6.5 %copy-start.2 = (f32[4,160,512]{2,1,0:T(8,128)S(1)}, f32[4,160,512]{2,1,0:T(8,128)}, u32[]{:S(2)}) copy-start(f32[4,160,512]{2,1,0:T(8,128)} %get-tuple-element.41) | copy-start | bytes 3932164
  106.6 10.6 %collective-permute-start.3 = (bf16[2,176,512]{2,1,0:T(8,128)(2,1)S(1)}, bf16[2,176,512]{2,1,0:T(8,128)(2,1)S(1)}, u32[]{:S(2)}, u32[]{:S(2)}) collective-permute-start(bf16[2,176,512]{2,1,0:T(8,128)(2,1)S(1)} %pad_maximum_fusion.1), channel_id=1, source_target_pairs={{0,6},{1,7},{2,4},{3,5},{4,2},{5,3},{6,0},{7,1},{8,14},{9,15},{10,... | collective-permute-start | bytes 1081352 | tf_op jit(solution)/shard_map/ppermute | solution.py:729
  109.6 11.4 %collective-permute-start.6 = (bf16[2,176,512]{2,1,0:T(8,128)(2,1)S(1)}, bf16[2,176,512]{2,1,0:T(8,128)(2,1)S(1)}, u32[]{:S(2)}, u32[]{:S(2)}) collective-permute-start(bf16[2,176,512]{2,1,0:T(8,128)(2,1)S(1)} %pad_maximum_fusion.2), channel_id=1, source_target_pairs={{0,1},{1,0},{2,3},{3,2},{4,5},{5,4},{6,7},{7,6},{8,9},{9,8},{10,11... | collective-permute-start | bytes 1081352 | tf_op jit(solution)/shard_map/ppermute | solution.py:729
  113.1 8.1 %collective-permute-start.10 = (bf16[1,160,512]{2,1,0:T(8,128)(2,1)S(1)}, bf16[1,160,512]{2,1,0:T(8,128)(2,1)S(1)}, u32[]{:S(2)}, u32[]{:S(2)}) collective-permute-start(bf16[1,160,512]{2,1,0:T(8,128)(2,1)S(1)} %add_convert_fusion.9), channel_id=1, source_target_pairs={{0,6},{1,7},{2,4},{3,5},{4,2},{5,3},{6,0},{7,1},{8,14},{9,15},{10,... | collective-permute-start | bytes 491528 | tf_op jit(solution)/shard_map/ppermute | solution.py:729
  117.3 7.2 %collective-permute-start.4 = (bf16[1,176,512]{2,1,0:T(8,128)(2,1)S(1)}, bf16[1,176,512]{2,1,0:T(8,128)(2,1)S(1)}, u32[]{:S(2)}, u32[]{:S(2)}) collective-permute-start(bf16[1,176,512]{2,1,0:T(8,128)(2,1)S(1)} %add_convert_fusion.5), channel_id=1, source_target_pairs={{0,1},{1,0},{2,3},{3,2},{4,5},{5,4},{6,7},{7,6},{8,9},{9,8},{10,11... | collective-permute-start | bytes 540680 | tf_op jit(solution)/shard_map/ppermute | solution.py:729
  121.1 5.6 %collective-permute-start.7 = (bf16[1,176,512]{2,1,0:T(8,128)(2,1)S(1)}, bf16[1,176,512]{2,1,0:T(8,128)(2,1)S(1)}, u32[]{:S(2)}, u32[]{:S(2)}) collective-permute-start(bf16[1,176,512]{2,1,0:T(8,128)(2,1)S(1)} %add_convert_fusion.1), channel_id=1, source_target_pairs={{0,2},{1,3},{2,0},{3,1},{4,6},{5,7},{6,4},{7,5},{8,10},{9,11},{10,... | collective-permute-start | bytes 540680 | tf_op jit(solution)/shard_map/ppermute | solution.py:729

commit v4 on v3

--- a/solution.py
+++ b/solution.py
@@ -14,6 +14,7 @@
 FLIP = 256
 ROWS = 64
 GRANT = 56
+OUTPUT_GRANT = 28
 BF16 = jnp.bfloat16
 F32 = jnp.float32
 NT = (((1,), (1,)), ((), ()))
@@ -24,6 +25,10 @@
     return pltpu.CompilerParams(
         dimension_semantics=("arbitrary",) * dims, vmem_limit_bytes=megabytes << 20
     )
+
+
+def streamed(*arrays):
+    return [pltpu.with_memory_space_constraint(x, pltpu.HBM) for x in arrays]
 
 
 def iota(shape, dim):
@@ -100,18 +105,19 @@
     squares[...] = jnp.broadcast_to(lax.rsqrt(mean + EPSILON), squares.shape)
 
 
-def scale_all(hid, before, after, gain, xs, squares):
+def scale_all(hid, gain, xs, squares, halo=None):
     tokens, depth = hid[0].shape
-    rows = tokens + 2 * HALO
+    rows = xs.shape[0] // 2
     for i in range(2):
         lanes = pl.ds(i * depth, depth)
-        halo = jnp.concatenate([before[i][...].astype(F32), after[i][...].astype(F32)], axis=0)
+        mirrored = pl.ds((1 - i) * depth, depth)
         own, other = gain[i][...], gain[1 - i][...]
         scale_rows(hid[i], 0, own, xs.at[:, lanes], squares)
-        scale_rows(halo, tokens, own, xs.at[:, lanes], squares)
-        lanes = pl.ds((1 - i) * depth, depth)
-        scale_mirrored(hid[i], rows, other, xs.at[:, lanes])
-        scale_mirrored(halo.astype(BF16), rows + tokens, other, xs.at[:, lanes])
+        scale_mirrored(hid[i], rows, other, xs.at[:, mirrored])
+        if halo:
+            beside = jnp.concatenate([half[i][...].astype(F32) for half in halo], axis=0)
+            scale_rows(beside, tokens, own, xs.at[:, lanes], squares)
+            scale_mirrored(beside.astype(BF16), rows + tokens, other, xs.at[:, mirrored])
 
 
 def placed(tokens):
@@ -119,58 +125,52 @@
     return spans + [(tokens, 0, HALO), (tokens + HALO, tokens + HALO, HALO)]
 
 
-def mix_step(hid, before, after, gain, wv, wb, wst, mix, steps, acc_v, acc_b, xs, squares, weights, last):
+def mix_step(hid, before, after, gain, wv, wbc, wst, mix, steps, acc_v, acc_b, acc_s, xs, squares, last):
     tokens, depth = hid[0].shape
     rows = tokens + 2 * HALO
-    inner = wv[0].shape[1]
-    heads = wst[0].shape[0]
-    state = wb[0].shape[1]
-    scale_all(hid, before, after, gain, xs, squares)
-    for i in range(2):
-        weights[i * depth : (i + 1) * depth, :state] = wb[i][...]
-        turned = jnp.concatenate(
-            [wst[i][...].astype(F32), jnp.zeros((TILE - heads, depth), F32)], axis=0
-        )
-        for c in range(0, depth, TILE):
-            weights[i * depth + c : i * depth + c + TILE, state:] = (
-                turned[:, c : c + TILE].T.astype(BF16)
-            )
+    inner, maps = acc_v.shape[1], acc_b.shape[1]
+    heads = acc_s.shape[1]
+    chunks = tokens // CHUNK
+    scale_all(hid, gain, xs, squares, (before, after))
     accumulate(xs, acc_v, wv, 3)
-    accumulate(xs, acc_b, (weights,), 3)
+    accumulate(xs, acc_b, wbc, 3)
+    for b in range(2):
+        at = slice(b * rows, b * rows + tokens)
+        total = lax.dot_general(wst[0][...], xs[at, :depth], NT, preferred_element_type=F32)
+        total = total + lax.dot_general(wst[1][...], xs[at, depth:], NT, preferred_element_type=F32)
+        acc_s[b] += total
 
     @pl.when(last)
     def _():
         finish_rms(squares, WIDTH)
+        spans = [slice(c * CHUNK, (c + 1) * CHUNK) for c in range(chunks)]
+        scale = jnp.concatenate([squares[at, :heads] for at in spans], axis=1)
         for b in range(2):
-            for r in range(0, tokens, CHUNK):
-                at = r // CHUNK * heads
-                steps[b, :, at : at + heads] = (
-                    acc_b[b * rows + r : b * rows + r + CHUNK, state : state + heads]
-                    * squares[r : r + CHUNK, :heads]
-                )
+            stack = [acc_s[b, :, at] for at in spans]
+            stack.append(jnp.zeros((TILE - chunks * heads, CHUNK), F32))
+            steps[b] = jnp.concatenate(stack, axis=0).T[:, : chunks * heads] * scale
             for r, out, size in placed(tokens):
                 here = slice(b * rows + r, b * rows + r + size)
-                scale = squares[r : r + size, :]
+                scales = squares[r : r + size, :]
                 for c in range(0, inner, TILE):
-                    mix[b, c // TILE, out : out + size, :] = acc_v[here, c : c + TILE] * scale
-                mix[b, inner // TILE, out : out + size, :] = acc_b[here, :state] * scale
+                    mix[b, c // TILE, out : out + size, :] = acc_v[here, c : c + TILE] * scales
+                for c in range(0, maps, TILE):
+                    mix[b, (inner + c) // TILE, out : out + size, :] = acc_b[here, c : c + TILE] * scales
 
 
 def gate_kernel(*refs):
-    hid, before, after, gain, wg, wc = (refs[2 * i : 2 * i + 2] for i in range(6))
-    taps_ref, gate_ref, maps_ref, acc_g, acc_c, xs, squares, padded = refs[12:]
+    hid, gain, wg = (refs[2 * i : 2 * i + 2] for i in range(3))
+    gate_ref, acc_g, xs, squares = refs[6:]
     k = pl.program_id(0)
     tokens = hid[0].shape[0]
-    rows = tokens + 2 * HALO
 
     @pl.when(k == 0)
     def _():
-        for acc in (acc_g, acc_c, squares):
+        for acc in (acc_g, squares):
             acc[...] = jnp.zeros_like(acc)
 
-    scale_all(hid, before, after, gain, xs, squares)
-    accumulate(xs, acc_g, wg, 3)
-    accumulate(xs, acc_c, wc, 3)
+    scale_all(hid, gain, xs, squares)
+    accumulate(xs, acc_g, wg, 2)
 
     @pl.when(k == pl.num_programs(0) - 1)
     def _():
@@ -180,16 +180,8 @@
                 scale = squares[r : r + TILE, :]
                 for c in range(0, gate_ref.shape[2], TILE):
                     gate_ref[b, r : r + TILE, c : c + TILE] = silu(
-                        acc_g[b * rows + r : b * rows + r + TILE, c : c + TILE] * scale
+                        acc_g[b * tokens + r : b * tokens + r + TILE, c : c + TILE] * scale
                     )
-            for r, out, size in placed(tokens):
-                padded[out : out + size, :] = (
-                    acc_c[b * rows + r : b * rows + r + size, :] * squares[r : r + size, :]
-                )
-            for r in range(0, tokens, ROWS):
-                forward, backward = convolved(padded, r, taps_ref[...])
-                maps_ref[b, 0, r : r + ROWS, :] = forward.astype(BF16)
-                maps_ref[b, 1, r : r + ROWS, :] = backward.astype(BF16)
 
 
 def convolved(source, row, taps):
@@ -219,50 +211,38 @@
     ]
 
 
-def token_specs(tokens):
-    across = lambda k: (0, k)
-    return (
-        paired((tokens, DEPTH), across)
-        + paired((HALO, DEPTH), across)
-        + paired((HALO, DEPTH), across)
-        + paired((1, DEPTH), across)
-    )
-
-
-def project_gate(hidden, before, after, norm_gain, w_gate, w_bc, taps):
+def across(k):
+    return (0, k)
+
+
+def downward(k):
+    return (k, 0)
+
+
+def project_gate(hidden, norm_gain, w_gate):
     tokens, width = hidden.shape
-    inner, state = w_gate.shape[1], w_bc.shape[1] // 2
-    rows = tokens + 2 * HALO
+    inner = w_gate.shape[1]
     return pl.pallas_call(
         gate_kernel,
         grid=(PAIRS,),
-        in_specs=token_specs(tokens)
-        + paired((DEPTH, inner), lambda k: (k, 0))
-        + paired((DEPTH, state), lambda k: (k, 1))
-        + [pl.BlockSpec((CONV, state), lambda k: (0, 1))],
-        out_specs=[
-            pl.BlockSpec((2, tokens, inner), lambda k: (0, 0, 0)),
-            pl.BlockSpec((2, 2, tokens, state), lambda k: (0, 0, 0, 0)),
-        ],
-        out_shape=[
-            jax.ShapeDtypeStruct((2, tokens, inner), F32),
-            jax.ShapeDtypeStruct((2, 2, tokens, state), BF16),
-        ],
+        in_specs=paired((tokens, DEPTH), across)
+        + paired((1, DEPTH), across)
+        + paired((DEPTH, inner), downward),
+        out_specs=pl.BlockSpec((2, tokens, inner), lambda k: (0, 0, 0)),
+        out_shape=jax.ShapeDtypeStruct((2, tokens, inner), F32),
         scratch_shapes=[
-            pltpu.VMEM((2 * rows, inner), F32),
-            pltpu.VMEM((2 * rows, state), F32),
-            pltpu.VMEM((2 * rows, 2 * DEPTH), BF16),
-            pltpu.VMEM((rows, TILE), F32),
-            pltpu.VMEM((rows, TILE), F32),
+            pltpu.VMEM((2 * tokens, inner), F32),
+            pltpu.VMEM((2 * tokens, 2 * DEPTH), BF16),
+            pltpu.VMEM((tokens, TILE), F32),
         ],
         compiler_params=params(GRANT),
         cost_estimate=pl.CostEstimate(
-            flops=4 * rows * width * (inner + state + FLIP),
+            flops=4 * tokens * width * (inner + FLIP),
             transcendentals=2 * tokens * inner,
-            bytes_accessed=14 << 20,
+            bytes_accessed=12 << 20,
         ),
         name="project_gate",
-    )(*twice(hidden, before, after, norm_gain[None], w_gate, w_bc), taps)
+    )(*twice(*streamed(hidden), norm_gain[None], *streamed(w_gate)))
 
 
 def twice(*arrays):
@@ -283,7 +263,7 @@
 
 def conv_step(
     mix, steps, base_ref, tapv_ref, tapb_ref, bias_ref, rate_ref, skip_ref,
-    direct_ref, xf_ref, xb_ref, maps_ref, cols_ref, rows_ref, enter_ref, final_ref,
+    direct_ref, xf_ref, xb_ref, maps_ref, cmaps_ref, cols_ref, rows_ref, enter_ref, final_ref,
     dt_sc, wf_sc, wb_sc, keep_sc, vf_sc, vb_sc, carry_sc,
 ):
     tokens, inner = direct_ref.shape[1:]
@@ -363,9 +343,11 @@
             xb_ref[0, here, lanes] = backward.astype(BF16)
             vf_sc[here, lanes] = (forward * wf_sc[here, lanes]).astype(BF16)
             vb_sc[here, lanes] = (backward * wb_sc[here, lanes]).astype(BF16)
-        forward, backward = convolved(mix.at[inner // TILE], r, tapb_ref[...])
-        maps_ref[0, 0, here, :] = forward.astype(BF16)
-        maps_ref[0, 1, here, :] = backward.astype(BF16)
+        for n, maps in enumerate((maps_ref, cmaps_ref)):
+            taps = tapb_ref[:, n * state : (n + 1) * state]
+            forward, backward = convolved(mix.at[inner // TILE + n], r, taps)
+            maps[0, 0, here, :] = forward.astype(BF16)
+            maps[0, 1, here, :] = backward.astype(BF16)
         return carry
 
     lax.fori_loop(0, tokens // ROWS, block, 0)
@@ -391,20 +373,20 @@
 
 
 def front_kernel(*refs):
-    hid, before, after, gain, wv, wb, wst = (refs[2 * i : 2 * i + 2] for i in range(7))
-    small, outs, scratch = refs[14:20], refs[20:28], refs[28:]
-    acc_v, acc_b, xs, squares, weights, mix, steps = scratch[:7]
+    hid, before, after, gain, wv, wbc, wst = (refs[2 * i : 2 * i + 2] for i in range(7))
+    small, outs, scratch = refs[14:20], refs[20:29], refs[29:]
+    acc_v, acc_b, acc_s, xs, squares, mix, steps = scratch[:7]
     i = pl.program_id(0)
 
     @pl.when(i == 0)
     def _():
-        for acc in (acc_v, acc_b, squares):
+        for acc in (acc_v, acc_b, acc_s, squares):
             acc[...] = jnp.zeros_like(acc)
 
     @pl.when(i < PAIRS)
     def _():
         mix_step(
-            hid, before, after, gain, wv, wb, wst, mix, steps, acc_v, acc_b, xs, squares, weights,
+            hid, before, after, gain, wv, wbc, wst, mix, steps, acc_v, acc_b, acc_s, xs, squares,
             i == PAIRS - 1,
         )
 
@@ -430,14 +412,17 @@
     return pl.pallas_call(
         front_kernel,
         grid=(PAIRS + 2,),
-        in_specs=token_specs(tokens)
-        + paired((DEPTH, inner), lambda k: (k, 0))
-        + paired((DEPTH, state), lambda k: (k, 0))
-        + paired((heads, DEPTH), lambda k: (0, k))
+        in_specs=paired((tokens, DEPTH), across)
+        + paired((HALO, DEPTH), across)
+        + paired((HALO, DEPTH), across)
+        + paired((1, DEPTH), across)
+        + paired((DEPTH, inner), downward)
+        + paired((DEPTH, 2 * state), downward)
+        + paired((heads, DEPTH), across)
         + [
             pl.BlockSpec((chunks, CHUNK), flat),
             pl.BlockSpec((CONV, inner), flat),
-            pl.BlockSpec((CONV, state), flat),
+            pl.BlockSpec((CONV, 2 * state), flat),
             pl.BlockSpec((1, heads), flat),
             pl.BlockSpec((1, heads), flat),
             pl.BlockSpec((1, heads), flat),
@@ -446,6 +431,7 @@
             pl.BlockSpec((1, tokens, inner), one),
             pl.BlockSpec((1, tokens, inner), one),
             pl.BlockSpec((1, tokens, inner), one),
+            pl.BlockSpec((1, 2, tokens, state), four),
             pl.BlockSpec((1, 2, tokens, state), four),
             pl.BlockSpec((1, chunks, CHUNK, COLUMNS * heads), four),
             pl.BlockSpec((1, chunks, 2, heads, CHUNK), five),
@@ -457,6 +443,7 @@
             jax.ShapeDtypeStruct((2, tokens, inner), BF16),
             jax.ShapeDtypeStruct((2, tokens, inner), BF16),
             jax.ShapeDtypeStruct((2, 2, tokens, state), BF16),
+            jax.ShapeDtypeStruct((2, 2, tokens, state), BF16),
             jax.ShapeDtypeStruct((2, chunks, CHUNK, COLUMNS * heads), F32),
             jax.ShapeDtypeStruct((2, chunks, 2, heads, CHUNK), F32),
             jax.ShapeDtypeStruct((2, 2, chunks, state, inner), BF16),
@@ -464,11 +451,11 @@
         ],
         scratch_shapes=[
             pltpu.VMEM((2 * rows, inner), F32),
-            pltpu.VMEM((2 * rows, state + TILE), F32),
+            pltpu.VMEM((2 * rows, 2 * state), F32),
+            pltpu.VMEM((2, heads, tokens), F32),
             pltpu.VMEM((2 * rows, 2 * DEPTH), BF16),
             pltpu.VMEM((rows, TILE), F32),
-            pltpu.VMEM((2 * DEPTH, state + TILE), BF16),
-            pltpu.VMEM((2, (inner + state) // TILE, rows, TILE), F32),
+            pltpu.VMEM((2, (inner + 2 * state) // TILE, rows, TILE), F32),
             pltpu.VMEM((2, CHUNK, heads * chunks), F32),
             pltpu.VMEM((tokens, inner), F32),
             pltpu.VMEM((tokens, inner), F32),
@@ -486,7 +473,7 @@
         ),
         name="front",
     )(
-        *twice(hidden, before, after, norm_gain[None], w_value, w_bc, w_step.T),
+        *twice(*streamed(hidden), before, after, norm_gain[None], *streamed(w_value, w_bc, w_step.T)),
         base_ids, conv_value, conv_bc, step_bias, decay_rate, skip_gain,
     )
 
@@ -626,15 +613,40 @@
         normed[b, pl.ds(pl.multiple_of(row, size), size), lanes] = y.astype(BF16)
 
 
-def output_kernel(
+def multiply_out(t, part, outs, normed, straight, mirrored):
+    slab = straight[0].shape[1]
+    flip = reversal(FLIP)
+    for n, block in enumerate((STEPS[t], PARTS - 1 - STEPS[t])):
+        mine = [g for g, order in enumerate(ORDERS) if block in slots(order)[part]]
+        if not mine:
+            continue
+        for c in range(0, slab, FLIP):
+            at = slab - FLIP - c
+            mirrored[:, c : c + FLIP] = dot(straight[1 - n][:, at : at + FLIP], flip).astype(BF16)
+        spans = []
+        for g in mine:
+            if spans and spans[-1][-1] == g - 1:
+                spans[-1].append(g)
+            else:
+                spans.append([g])
+        for span in spans:
+            begin = GROUPS[span[0]][0]
+            at = slice(begin, sum(GROUPS[span[-1]]))
+            product = dot(normed[0, at], straight[n][...]) + dot(normed[1, at], mirrored[...])
+            for g in span:
+                row, rows = GROUPS[g]
+                slot = slots(ORDERS[g])[part].index(block) % outs[g].shape[0]
+                outs[g][slot] = product[row - begin : row - begin + rows].astype(outs[g].dtype)
+
+
+def send_kernel(
     place_ref, local_ref, silu_ref, c_ref, cols_ref, incoming_ref, gain_ref, wout_ref, wmir_ref, *rest
 ):
-    outs, (normed, mirrored, product) = rest[:-3], rest[-3:]
+    outs, normed, mirrored = rest[:3], rest[3], rest[4]
     i = pl.program_id(0)
     size = local_ref.shape[1]
     halves = normed.shape[1] // size
     pre = 2 * halves
-    slab = wout_ref.shape[1]
 
     @pl.when(i < pre)
     def _():
@@ -643,53 +655,53 @@
             gain_ref, normed,
         )
 
-    @pl.when(i >= pre)
-    def _():
-        flip = reversal(FLIP)
-        straight = (wout_ref, wmir_ref)
-        for n in range(2):
-            source = straight[1 - n]
-            for c in range(0, slab, FLIP):
-                at = slab - FLIP - c
-                mirrored[:, c : c + FLIP] = dot(source[:, at : at + FLIP], flip).astype(BF16)
-            product[n] = dot(normed[0], straight[n][...]) + dot(normed[1], mirrored[...])
-
-    for t, step in enumerate(STEPS):
+    for t in range(len(STEPS)):
 
         @pl.when(i == pre + t)
         def _():
-            for g, (order, (row, rows)) in enumerate(zip(ORDERS, GROUPS)):
-                sent, kept = slots(order)
-                for n, block in enumerate((step, PARTS - 1 - step)):
-                    ref, held = (outs[2 * g], sent) if block in sent else (outs[2 * g + 1], kept)
-                    at = held.index(block) % ref.shape[0]
-                    ref[at] = product[n, row : row + rows, :].astype(ref.dtype)
+            multiply_out(t, 0, outs, normed, (wout_ref, wmir_ref), mirrored)
+
+
+def keep_kernel(place_ref, normed_ref, wout_ref, wmir_ref, *rest):
+    outs, mirrored = rest[:3], rest[3]
+    for t in range(len(STEPS)):
+
+        @pl.when(pl.program_id(0) == t)
+        def _():
+            multiply_out(t, 1, outs, normed_ref, (wout_ref, wmir_ref), mirrored)
+
+
+def group_outs(part, dtype, slab, late):
+    specs, shapes = [], []
+    for order, (_, rows) in zip(ORDERS, GROUPS):
+        given = slots(order)[part]
+        steps = [t for t, s in enumerate(STEPS) for r in (s, PARTS - 1 - s) if r in given]
+        if len(set(steps)) == len(steps):
+            spec = pl.BlockSpec((1, rows, slab), lambda i, n: (late(i), 0, 0))
+        else:
+            spec = pl.BlockSpec(
+                (2, rows, slab), lambda i, n, b=steps[0]: (jnp.clip(late(i) - b, 0, 1), 0, 0)
+            )
+        specs.append(spec)
+        shapes.append(jax.ShapeDtypeStruct((PARTS // 2, rows, slab), dtype))
+    return specs, shapes
 
 
 def output(local, gate, c_maps, cols, incoming, gain, w_out):
     tokens, inner = local.shape[1:]
     state = c_maps.shape[3]
-    chunks = tokens // CHUNK
     size = 2 * CHUNK
     halves = tokens // size
     pre = 2 * halves
     slab = w_out.shape[1] // PARTS
+    place = lax.axis_index("head")[None]
     held = lambda i: jnp.minimum(i, pre - 1)
+    late = lambda i: jnp.maximum(i - pre, 0)
     token = lambda i, n: (held(i) // halves, held(i) % halves, 0)
-    block = lambda i, n: n[0] ^ (jnp.maximum(i - pre, 0) ^ STEPS[0])
-    late = lambda i: jnp.maximum(i - pre, 0)
-    out_specs, out_shape = [], []
-    for order, (_, rows) in zip(ORDERS, GROUPS):
-        sent, _ = slots(order)
-        if {STEPS[0], PARTS - 1 - STEPS[0]} <= set(sent):
-            per, places = 2, (lambda i, n: (jnp.minimum(late(i), 1), 0, 0), lambda i, n: (jnp.maximum(late(i) - 2, 0), 0, 0))
-        else:
-            per, places = 1, (lambda i, n: (late(i), 0, 0),) * 2
-        for place, dtype in zip(places, (BF16, F32)):
-            out_specs.append(pl.BlockSpec((per, rows, slab), place))
-            out_shape.append(jax.ShapeDtypeStruct((PARTS // 2, rows, slab), dtype))
-    return pl.pallas_call(
-        output_kernel,
+    block = lambda t, n: n[0] ^ (t ^ STEPS[0])
+    specs, shapes = group_outs(0, BF16, slab, late)
+    *sends, normed = pl.pallas_call(
+        send_kernel,
         grid_spec=pltpu.PrefetchScalarGridSpec(
             num_scalar_prefetch=1,
             grid=(pre + len(STEPS),),
@@ -705,21 +717,39 @@
                     (2, 1, inner // TILE, state, TILE), lambda i, n: (0, held(i) // halves, 0, 0, 0)
                 ),
                 pl.BlockSpec((1, inner), lambda i, n: (0, 0)),
+                pl.BlockSpec((inner, slab), lambda i, n: (0, block(late(i), n))),
+                pl.BlockSpec((inner, slab), lambda i, n: (0, PARTS - 1 - block(late(i), n))),
+            ],
+            out_specs=specs + [pl.BlockSpec((2, tokens, inner), lambda i, n: (0, 0, 0))],
+            scratch_shapes=[pltpu.VMEM((inner, slab), BF16)],
+        ),
+        out_shape=shapes + [jax.ShapeDtypeStruct((2, tokens, inner), BF16)],
+        compiler_params=params(OUTPUT_GRANT),
+        cost_estimate=pl.CostEstimate(flops=3 << 30, transcendentals=1 << 20, bytes_accessed=14 << 20),
+        name="output_send",
+    )(
+        place, *streamed(local, gate, c_maps, cols), incoming, gain, *twice(*streamed(w_out))
+    )
+    specs, shapes = group_outs(1, F32, slab, lambda i: i)
+    keeps = pl.pallas_call(
+        keep_kernel,
+        grid_spec=pltpu.PrefetchScalarGridSpec(
+            num_scalar_prefetch=1,
+            grid=(len(STEPS),),
+            in_specs=[
+                pl.BlockSpec((2, tokens, inner), lambda i, n: (0, 0, 0)),
                 pl.BlockSpec((inner, slab), lambda i, n: (0, block(i, n))),
                 pl.BlockSpec((inner, slab), lambda i, n: (0, PARTS - 1 - block(i, n))),
             ],
-            out_specs=out_specs,
-            scratch_shapes=[
-                pltpu.VMEM((2, tokens, inner), BF16),
-                pltpu.VMEM((inner, slab), BF16),
-                pltpu.VMEM((2, tokens, slab), F32),
-            ],
+            out_specs=specs,
+            scratch_shapes=[pltpu.VMEM((inner, slab), BF16)],
         ),
-        out_shape=out_shape,
-        compiler_params=params(GRANT),
-        cost_estimate=pl.CostEstimate(flops=6 << 30, transcendentals=1 << 20, bytes_accessed=20 << 20),
-        name="output",
-    )(lax.axis_index("head")[None], local, gate, c_maps, cols, incoming, gain, w_out, w_out)
+        out_shape=shapes,
+        compiler_params=params(OUTPUT_GRANT),
+        cost_estimate=pl.CostEstimate(flops=3 << 30, transcendentals=0, bytes_accessed=10 << 20),
+        name="output_keep",
+    )(place, normed, *twice(*streamed(w_out)))
+    return sends, keeps
 
 
 def reduced(send, keep, order):
@@ -766,7 +796,7 @@
     down = [(j, i) for i, j in up]
     before = lax.ppermute(hidden[-HALO:], "ctx", up)
     after = lax.ppermute(hidden[:HALO], "ctx", down)
-    direct, xf, xb, b_maps, cols, rows, enter, final = front(
+    direct, xf, xb, b_maps, c_maps, cols, rows, enter, final = front(
         hidden, before, after, norm_gain, w_value, w_bc, w_step,
         base_ids.reshape(-1, CHUNK),
         conv_value,
@@ -777,15 +807,14 @@
     )
     state, tile = final.shape[3:]
     sent = lax.all_to_all(final.reshape(count, state, tile), "ctx", 0, 0)
-    gate, c_maps = project_gate(hidden, before, after, norm_gain, w_gate, w_bc, conv_bc)
-    sent, gate, c_maps = lax.optimization_barrier((sent, gate, c_maps))
-    incoming = lax.all_to_all(chain(sent), "ctx", 0, 0)
+    local = within(direct, xf, xb, b_maps, c_maps, cols, rows, enter)
+    sent, local = lax.optimization_barrier((sent, local))
+    chained, late_gain = lax.optimization_barrier((chain(sent), norm_gain))
+    incoming = lax.all_to_all(chained, "ctx", 0, 0)
     incoming = incoming.reshape(final.shape[:3] + incoming.shape[1:])
-    local = within(direct, xf, xb, b_maps, c_maps, cols, rows, enter)
-    outs = output(local, gate, c_maps, cols, incoming, out_gain[None], w_out)
-    return jnp.concatenate(
-        [reduced(outs[2 * g], outs[2 * g + 1], order) for g, order in enumerate(ORDERS)], axis=0
-    )
+    gate = project_gate(hidden, late_gain, w_gate)
+    sends, keeps = output(local, gate, c_maps, cols, incoming, out_gain[None], w_out)
+    return jnp.concatenate([reduced(*group) for group in zip(sends, keeps, ORDERS)], axis=0)
 
 
 def solution(mesh):

time: 128 us -> 121 us (0.945)
  starting transfers between devices: 38 us -> 33.1 us
    ppermute x9, starting transfers between devices: 20.1 us -> 17.3 us  [reduced(): arrived = lax.ppermute(send, 'head', pairs)]
    ppermute x9, waiting for transfers between devices: 19.3 us -> 16.6 us  [reduced(): arrived = lax.ppermute(send, 'head', pairs)]
    all_to_all x1, waiting for transfers between devices: 0.01 us -> 2.23 us  [shards(): sent = lax.all_to_all(final.reshape(count, state, tile), 'ctx', 0, 0)]
    all_to_all x1, starting transfers between devices: 5.68 us -> 3.57 us  [shards(): incoming = lax.all_to_all(chained, 'ctx', 0, 0)]
    pallas_call x3 -> x4, Pallas kernels: 49.5 us -> 49.7 us  [the longest x1 22.8 us: front(): pl.pallas_call(front_kernel, grid=(PAIRS + 2,), in_specs=paired((tokens,...]
  transfers between devices with their start and end apart: 13 -> 13, of which waited for: 8 -> 10; matrix products, arithmetic and copies ran while one was open for 1% -> 1% of each run, Pallas kernels for 18% -> 21%
where the time goes in v4:
time: 121 us; the launch traced here: 120 us
  Pallas kernels  60.1 us (50%)
  starting transfers between devices  33.1 us (27%)
  waiting for transfers between devices  23.6 us (20%)
  other arithmetic  1.72 us (1%)
  local copies, waits for them, and re-layouts  1.52 us (1%)
    pallas_call x1, Pallas kernels, front(): pl.pallas_call(front_kernel, grid=(PAIRS + 2,), in_specs=paired((tokens,...  22.8 us
    ppermute x9, starting transfers between devices, reduced(): arrived = lax.ppermute(send, 'head', pairs)  17.3 us
    ppermute x9, waiting for transfers between devices, reduced(): arrived = lax.ppermute(send, 'head', pairs)  16.6 us
    pallas_call x1, Pallas kernels, output(): pl.pallas_call(send_kernel, grid_spec=pltpu.PrefetchScalarGridSpec(num_sc...  11.1 us
    pallas_call x1, Pallas kernels, project_gate(): pl.pallas_call(gate_kernel, grid=(PAIRS,), in_specs=paired((tokens, DEPTH...  9.82 us
    all_to_all x1, starting transfers between devices, shards(): sent = lax.all_to_all(final.reshape(count, state, tile), 'ctx', 0, 0)  9.66 us
    pallas_call x1, Pallas kernels, within(): pl.pallas_call(within_kernel, grid=(2 * chunks,), in_specs=[pl.BlockSpec(...  9.37 us
    pallas_call x1, Pallas kernels, output(): pl.pallas_call(keep_kernel, grid_spec=pltpu.PrefetchScalarGridSpec(num_sc...  5.94 us
  transfers between devices with their start and end apart: 13, of which 10 were waited for; matrix products, arithmetic and copies ran while one was open for 1% of the time, Pallas kernels for 21%

profile of v4, /device:TPU:0, one launch (start us, length us, event | category | flops | bytes accessed | tf_op | source)
XLA Modules:
  0.0 120.1 jit_solution(548139874668369492)
XLA Ops:
  0.9 1.3 %collective-permute-start = (bf16[8,4096]{1,0:T(8,128)(2,1)S(1)}, bf16[8,4096]{1,0:T(8,128)(2,1)S(1)}, u32[]{:S(2)}, u32[]{:S(2)}) collective-permute-start(bf16[8,4096]{1,0:T(8,128)(2,1)S(1)} %get-tuple-element.46), channel_id=1, source_target_pairs={{0,8},{8,16},{16,24},{24,32},{32,40},{40,48},{48,56},{56,64},{64,7... | collective-permute-start | bytes 196616 | tf_op jit(solution)/shard_map/ppermute | solution.py:797
  2.2 1.3 %collective-permute-start.1 = (bf16[8,4096]{1,0:T(8,128)(2,1)S(1)}, bf16[8,4096]{1,0:T(8,128)(2,1)S(1)}, u32[]{:S(2)}, u32[]{:S(2)}) collective-permute-start(bf16[8,4096]{1,0:T(8,128)(2,1)S(1)} %get-tuple-element.45), channel_id=1, source_target_pairs={{8,0},{16,8},{24,16},{32,24},{40,32},{48,40},{56,48},{64,56},{72,6... | collective-permute-start | bytes 196616 | tf_op jit(solution)/shard_map/ppermute | solution.py:798
  3.5 3.7 %collective-permute-done.1.refs_4_.refs_5_ = bf16[8,4096]{1,0:T(8,128)(2,1)S(1)} collective-permute-done((bf16[8,4096]{1,0:T(8,128)(2,1)S(1)}, bf16[8,4096]{1,0:T(8,128)(2,1)S(1)}, u32[]{:S(2)}, u32[]{:S(2)}) %collective-permute-start.1) | collective-permute-done | bytes 65568 | tf_op jit(solution)/shard_map/ppermute | solution.py:798
  7.9 22.8 %front.1 = (f32[2,512,512]{2,1,0:T(8,128)}, bf16[2,512,512]{2,1,0:T(8,128)(2,1)}, bf16[2,512,512]{2,1,0:T(8,128)(2,1)}, bf16[2,2,512,128]{3,2,1,0:T(8,128)(2,1)}...) custom-call(bf16[512,4096]{1,0:T(8,128)(2,1)} %refs_1_.3, ...), custom_call_target="tpu_custom_call" | custom-call | flops 8858370048 | bytes 25165824 | tf_op jit(solution)/shard_map/front/pallas_call | solution.py:412
  30.7 9.7 %all-to-all-start = ((bf16[16,144,128]{2,1,0:T(8,128)(2,1)}), bf16[16,144,128]{2,1,0:T(8,128)(2,1)S(1)}, u32[]{:S(2)}, u32[]{:S(2)}) async-start(bf16[16,144,128]{2,1,0:T(8,128)(2,1)} %bitcast.19), calls=%async_computation | async-start | bytes 1179648 | tf_op jit(solution)/shard_map/all_to_all | solution.py:809
  40.4 9.4 %within.1.local_ref = f32[2,512,512]{2,1,0:T(8,128)} custom-call(f32[2,512,512]{2,1,0:T(8,128)} %get-tuple-element.26.direct_ref, bf16[2,512,512]{2,1,0:T(8,128)(2,1)} %get-tuple-element.27.xf_ref, bf16[2,512,512]{2,1,0:T(8,128)(2,1)} %get-tuple-element.28.xb_ref, bf16[2,2,512,128]{3,2,1,0:T(8,128)(2,1)} %get-tuple-element.29.b_ref, ...), custom_call_target="tpu_custom_call" | custom-call | flops 4294967296 | bytes 16777216 | tf_op jit(solution)/shard_map/within/pallas_call | solution.py:526
  49.8 2.2 %all-to-all-done.states_ref = bf16[16,144,128]{2,1,0:T(8,128)(2,1)S(1)} async-done(((bf16[16,144,128]{2,1,0:T(8,128)(2,1)}), bf16[16,144,128]{2,1,0:T(8,128)(2,1)S(1)}, u32[]{:S(2)}, u32[]{:S(2)}) %all-to-all-start) | async-done | bytes 589856 | tf_op jit(solution)/shard_map/all_to_all | solution.py:809
  52.9 3.6 %all-to-all-start.1 = ((bf16[16,128,128]{2,1,0:T(8,128)(2,1)}), bf16[16,128,128]{2,1,0:T(8,128)(2,1)S(1)}, u32[]{:S(2)}, u32[]{:S(2)}) async-start(bf16[16,128,128]{2,1,0:T(8,128)(2,1)} %chain.1), calls=%async_computation.1 | async-start | bytes 1048576 | tf_op jit(solution)/shard_map/all_to_all | solution.py:813
  56.5 9.8 %project_gate.1.silu_ref = f32[2,512,512]{2,1,0:T(8,128)} custom-call(bf16[512,4096]{1,0:T(8,128)(2,1)} %refs_1_.3, bf16[512,4096]{1,0:T(8,128)(2,1)} %refs_1_.3, f32[1,4096]{1,0:T(1,128)} %bitcast.24, f32[1,4096]{1,0:T(1,128)} %bitcast.25, bf16[4096,512]{1,0:T(8,128)(2,1)} %refs_5_.1, bf16[4096,512]{1,0:T(8,128)(2,1)} %refs_5_.1), custom_call_target="tpu_custom_call" | custom-call | flops 6442450944 | bytes 12582912 | tf_op jit(solution)/shard_map/project_gate/pallas_call | solution.py:225
  67.3 11.1 %output_send.1 = (bf16[4,176,512]{2,1,0:T(8,128)(2,1)S(1)}, bf16[4,176,512]{2,1,0:T(8,128)(2,1)S(1)}, bf16[4,160,512]{2,1,0:T(8,128)(2,1)S(1)}, bf16[2,512,512]{2,1,0:T(8,128)(2,1)S(1)}) custom-call(s32[1]{0:T(128)} %bitcast.place_ref, f32[2,512,512]{2,1,0:T(8,128)} %within.1.local_ref, f32[2,512,512]{2,1,0:T(8,128)} %project_gate.1.silu_ref, ...), custom_call_target="tpu_custom_call" | custom-call | flops 3221225472 | bytes 14680064 | tf_op jit(solution)/shard_map/output_send/pallas_call | solution.py:703
  78.5 3.3 %collective-permute-start.8 = (bf16[4,160,512]{2,1,0:T(8,128)(2,1)S(1)}, bf16[4,160,512]{2,1,0:T(8,128)(2,1)S(1)}, u32[]{:S(2)}, u32[]{:S(2)}) collective-permute-start(bf16[4,160,512]{2,1,0:T(8,128)(2,1)S(1)} %get-tuple-element.44), channel_id=1, source_target_pairs={{0,1},{1,0},{2,3},{3,2},{4,5},{5,4},{6,7},{7,6},{8,9},{9,8},{10,11... | collective-permute-start | bytes 1966088 | tf_op jit(solution)/shard_map/ppermute | solution.py:759
  81.8 1.5 %collective-permute-start.2 = (bf16[4,176,512]{2,1,0:T(8,128)(2,1)S(1)}, bf16[4,176,512]{2,1,0:T(8,128)(2,1)S(1)}, u32[]{:S(2)}, u32[]{:S(2)}) collective-permute-start(bf16[4,176,512]{2,1,0:T(8,128)(2,1)S(1)} %get-tuple-element.40), channel_id=1, source_target_pairs={{0,2},{1,3},{2,0},{3,1},{4,6},{5,7},{6,4},{7,5},{8,10},{9,11},{10,... | collective-permute-start | bytes 2162696 | tf_op jit(solution)/shard_map/ppermute | solution.py:759
  83.3 2.1 %collective-permute-start.5 = (bf16[4,176,512]{2,1,0:T(8,128)(2,1)S(1)}, bf16[4,176,512]{2,1,0:T(8,128)(2,1)S(1)}, u32[]{:S(2)}, u32[]{:S(2)}) collective-permute-start(bf16[4,176,512]{2,1,0:T(8,128)(2,1)S(1)} %get-tuple-element.42), channel_id=1, source_target_pairs={{0,6},{1,7},{2,4},{3,5},{4,2},{5,3},{6,0},{7,1},{8,14},{9,15},{10,... | collective-permute-start | bytes 2162696 | tf_op jit(solution)/shard_map/ppermute | solution.py:759
  85.3 5.9 %output_keep.1 = (f32[4,176,512]{2,1,0:T(8,128)S(1)}, f32[4,176,512]{2,1,0:T(8,128)S(1)}, f32[4,160,512]{2,1,0:T(8,128)S(1)}) custom-call(s32[1]{0:T(128)} %bitcast.place_ref, bf16[2,512,512]{2,1,0:T(8,128)(2,1)S(1)} %get-tuple-element.38.normed_ref, bf16[512,4096]{1,0:T(8,128)(2,1)} %wmir_ref.3, bf16[512,4096]{1,0:T(8,128)(2,1)} %wmir_ref.3), custom_call_target="tpu_custom_call" | custom-call | flops 3221225472 | bytes 10485760 | tf_op jit(solution)/shard_map/output_keep/pallas_call | solution.py:734
  91.3 4.8 %collective-permute-done.8 = bf16[4,160,512]{2,1,0:T(8,128)(2,1)S(1)} collective-permute-done((bf16[4,160,512]{2,1,0:T(8,128)(2,1)S(1)}, bf16[4,160,512]{2,1,0:T(8,128)(2,1)S(1)}, u32[]{:S(2)}, u32[]{:S(2)}) %collective-permute-start.8) | collective-permute-done | bytes 655392 | tf_op jit(solution)/shard_map/ppermute | solution.py:759
  96.2 1.6 %collective-permute-start.9 = (bf16[2,160,512]{2,1,0:T(8,128)(2,1)S(1)}, bf16[2,160,512]{2,1,0:T(8,128)(2,1)S(1)}, u32[]{:S(2)}, u32[]{:S(2)}) collective-permute-start(bf16[2,160,512]{2,1,0:T(8,128)(2,1)S(1)} %pad_maximum_fusion.3), channel_id=1, source_target_pairs={{0,2},{1,3},{2,0},{3,1},{4,6},{5,7},{6,4},{7,5},{8,10},{9,11},{10,... | collective-permute-start | bytes 983048 | tf_op jit(solution)/shard_map/ppermute | solution.py:759
  97.8 2.6 %collective-permute-done.2 = bf16[4,176,512]{2,1,0:T(8,128)(2,1)S(1)} collective-permute-done((bf16[4,176,512]{2,1,0:T(8,128)(2,1)S(1)}, bf16[4,176,512]{2,1,0:T(8,128)(2,1)S(1)}, u32[]{:S(2)}, u32[]{:S(2)}) %collective-permute-start.2) | collective-permute-done | bytes 720928 | tf_op jit(solution)/shard_map/ppermute | solution.py:759
  100.5 2.8 %collective-permute-start.3 = (bf16[2,176,512]{2,1,0:T(8,128)(2,1)S(1)}, bf16[2,176,512]{2,1,0:T(8,128)(2,1)S(1)}, u32[]{:S(2)}, u32[]{:S(2)}) collective-permute-start(bf16[2,176,512]{2,1,0:T(8,128)(2,1)S(1)} %pad_maximum_fusion.1), channel_id=1, source_target_pairs={{0,6},{1,7},{2,4},{3,5},{4,2},{5,3},{6,0},{7,1},{8,14},{9,15},{10,... | collective-permute-start | bytes 1081352 | tf_op jit(solution)/shard_map/ppermute | solution.py:759
  103.6 2.3 %collective-permute-done.9 = bf16[2,160,512]{2,1,0:T(8,128)(2,1)S(1)} collective-permute-done((bf16[2,160,512]{2,1,0:T(8,128)(2,1)S(1)}, bf16[2,160,512]{2,1,0:T(8,128)(2,1)S(1)}, u32[]{:S(2)}, u32[]{:S(2)}) %collective-permute-start.9) | collective-permute-done | bytes 327712 | tf_op jit(solution)/shard_map/ppermute | solution.py:759
  106.0 2.8 %collective-permute-start.10 = (bf16[1,160,512]{2,1,0:T(8,128)(2,1)S(1)}, bf16[1,160,512]{2,1,0:T(8,128)(2,1)S(1)}, u32[]{:S(2)}, u32[]{:S(2)}) collective-permute-start(bf16[1,160,512]{2,1,0:T(8,128)(2,1)S(1)} %add_convert_fusion.9), channel_id=1, source_target_pairs={{0,6},{1,7},{2,4},{3,5},{4,2},{5,3},{6,0},{7,1},{8,14},{9,15},{10,... | collective-permute-start | bytes 491528 | tf_op jit(solution)/shard_map/ppermute | solution.py:759
  108.8 1.1 collective-permute-done.3
  110.0 2.8 %collective-permute-start.4 = (bf16[1,176,512]{2,1,0:T(8,128)(2,1)S(1)}, bf16[1,176,512]{2,1,0:T(8,128)(2,1)S(1)}, u32[]{:S(2)}, u32[]{:S(2)}) collective-permute-start(bf16[1,176,512]{2,1,0:T(8,128)(2,1)S(1)} %add_convert_fusion.5), channel_id=1, source_target_pairs={{0,1},{1,0},{2,3},{3,2},{4,5},{5,4},{6,7},{7,6},{8,9},{9,8},{10,11... | collective-permute-start | bytes 540680 | tf_op jit(solution)/shard_map/ppermute | solution.py:759
  114.0 3.1 %collective-permute-done.4 = bf16[1,176,512]{2,1,0:T(8,128)(2,1)S(1)} collective-permute-done((bf16[1,176,512]{2,1,0:T(8,128)(2,1)S(1)}, bf16[1,176,512]{2,1,0:T(8,128)(2,1)S(1)}, u32[]{:S(2)}, u32[]{:S(2)}) %collective-permute-start.4) | collective-permute-done | bytes 180256 | tf_op jit(solution)/shard_map/ppermute | solution.py:759
  117.2 2.0 %collective-permute-done.7 = bf16[1,176,512]{2,1,0:T(8,128)(2,1)S(1)} collective-permute-done((bf16[1,176,512]{2,1,0:T(8,128)(2,1)S(1)}, bf16[1,176,512]{2,1,0:T(8,128)(2,1)S(1)}, u32[]{:S(2)}, u32[]{:S(2)}) %collective-permute-start.7) | collective-permute-done | bytes 180256 | tf_op jit(solution)/shard_map/ppermute | solution.py:759
  (28 shorter events, 6.3 us)
Async XLA Ops:
  0.9 2.6 %collective-permute-start = (bf16[8,4096]{1,0:T(8,128)(2,1)S(1)}, bf16[8,4096]{1,0:T(8,128)(2,1)S(1)}, u32[]{:S(2)}, u32[]{:S(2)}) collective-permute-start(bf16[8,4096]{1,0:T(8,128)(2,1)S(1)} %get-tuple-element.46), channel_id=1, source_target_pairs={{0,8},{8,16},{16,24},{24,32},{32,40},{40,48},{48,56},{56,64},{64,7... | collective-permute-start | bytes 196616 | tf_op jit(solution)/shard_map/ppermute | solution.py:797
  2.2 5.0 %collective-permute-start.1 = (bf16[8,4096]{1,0:T(8,128)(2,1)S(1)}, bf16[8,4096]{1,0:T(8,128)(2,1)S(1)}, u32[]{:S(2)}, u32[]{:S(2)}) collective-permute-start(bf16[8,4096]{1,0:T(8,128)(2,1)S(1)} %get-tuple-element.45), channel_id=1, source_target_pairs={{8,0},{16,8},{24,16},{32,24},{40,32},{48,40},{56,48},{64,56},{72,6... | collective-permute-start | bytes 196616 | tf_op jit(solution)/shard_map/ppermute | solution.py:798
  3.5 3.7 %copy-start.1 = (bf16[8,4096]{1,0:T(8,128)(2,1)}, bf16[8,4096]{1,0:T(8,128)(2,1)S(1)}, u32[]{:S(2)}) copy-start(bf16[8,4096]{1,0:T(8,128)(2,1)S(1)} %collective-permute-done.refs_2_.refs_3_) | copy-start | bytes 196612
  7.2 0.6 copy-start.2
  30.7 21.3 %all-to-all-start = ((bf16[16,144,128]{2,1,0:T(8,128)(2,1)}), bf16[16,144,128]{2,1,0:T(8,128)(2,1)S(1)}, u32[]{:S(2)}, u32[]{:S(2)}) async-start(bf16[16,144,128]{2,1,0:T(8,128)(2,1)} %bitcast.19), calls=%async_computation | async-start | bytes 1179648 | tf_op jit(solution)/shard_map/all_to_all | solution.py:809
  52.9 14.4 %all-to-all-start.1 = ((bf16[16,128,128]{2,1,0:T(8,128)(2,1)}), bf16[16,128,128]{2,1,0:T(8,128)(2,1)S(1)}, u32[]{:S(2)}, u32[]{:S(2)}) async-start(bf16[16,128,128]{2,1,0:T(8,128)(2,1)} %chain.1), calls=%async_computation.1 | async-start | bytes 1048576 | tf_op jit(solution)/shard_map/all_to_all | solution.py:813
  56.5 10.8 %copy-start = (f32[512]{0:T(512)S(1)}, f32[512]{0:T(512)}, u32[]{:S(2)}) copy-start(f32[512]{0:T(512)} %param.26) | copy-start | bytes 6148
  78.5 17.6 %collective-permute-start.8 = (bf16[4,160,512]{2,1,0:T(8,128)(2,1)S(1)}, bf16[4,160,512]{2,1,0:T(8,128)(2,1)S(1)}, u32[]{:S(2)}, u32[]{:S(2)}) collective-permute-start(bf16[4,160,512]{2,1,0:T(8,128)(2,1)S(1)} %get-tuple-element.44), channel_id=1, source_target_pairs={{0,1},{1,0},{2,3},{3,2},{4,5},{5,4},{6,7},{7,6},{8,9},{9,8},{10,11... | collective-permute-start | bytes 1966088 | tf_op jit(solution)/shard_map/ppermute | solution.py:759
  81.8 18.6 %collective-permute-start.2 = (bf16[4,176,512]{2,1,0:T(8,128)(2,1)S(1)}, bf16[4,176,512]{2,1,0:T(8,128)(2,1)S(1)}, u32[]{:S(2)}, u32[]{:S(2)}) collective-permute-start(bf16[4,176,512]{2,1,0:T(8,128)(2,1)S(1)} %get-tuple-element.40), channel_id=1, source_target_pairs={{0,2},{1,3},{2,0},{3,1},{4,6},{5,7},{6,4},{7,5},{8,10},{9,11},{10,... | collective-permute-start | bytes 2162696 | tf_op jit(solution)/shard_map/ppermute | solution.py:759
  83.3 20.1 %collective-permute-start.5 = (bf16[4,176,512]{2,1,0:T(8,128)(2,1)S(1)}, bf16[4,176,512]{2,1,0:T(8,128)(2,1)S(1)}, u32[]{:S(2)}, u32[]{:S(2)}) collective-permute-start(bf16[4,176,512]{2,1,0:T(8,128)(2,1)S(1)} %get-tuple-element.42), channel_id=1, source_target_pairs={{0,6},{1,7},{2,4},{3,5},{4,2},{5,3},{6,0},{7,1},{8,14},{9,15},{10,... | collective-permute-start | bytes 2162696 | tf_op jit(solution)/shard_map/ppermute | solution.py:759
  96.2 9.7 %collective-permute-start.9 = (bf16[2,160,512]{2,1,0:T(8,128)(2,1)S(1)}, bf16[2,160,512]{2,1,0:T(8,128)(2,1)S(1)}, u32[]{:S(2)}, u32[]{:S(2)}) collective-permute-start(bf16[2,160,512]{2,1,0:T(8,128)(2,1)S(1)} %pad_maximum_fusion.3), channel_id=1, source_target_pairs={{0,2},{1,3},{2,0},{3,1},{4,6},{5,7},{6,4},{7,5},{8,10},{9,11},{10,... | collective-permute-start | bytes 983048 | tf_op jit(solution)/shard_map/ppermute | solution.py:759
  100.5 9.4 %collective-permute-start.3 = (bf16[2,176,512]{2,1,0:T(8,128)(2,1)S(1)}, bf16[2,176,512]{2,1,0:T(8,128)(2,1)S(1)}, u32[]{:S(2)}, u32[]{:S(2)}) collective-permute-start(bf16[2,176,512]{2,1,0:T(8,128)(2,1)S(1)} %pad_maximum_fusion.1), channel_id=1, source_target_pairs={{0,6},{1,7},{2,4},{3,5},{4,2},{5,3},{6,0},{7,1},{8,14},{9,15},{10,... | collective-permute-start | bytes 1081352 | tf_op jit(solution)/shard_map/ppermute | solution.py:759
  103.5 10.0 %collective-permute-start.6 = (bf16[2,176,512]{2,1,0:T(8,128)(2,1)S(1)}, bf16[2,176,512]{2,1,0:T(8,128)(2,1)S(1)}, u32[]{:S(2)}, u32[]{:S(2)}) collective-permute-start(bf16[2,176,512]{2,1,0:T(8,128)(2,1)S(1)} %pad_maximum_fusion.2), channel_id=1, source_target_pairs={{0,1},{1,0},{2,3},{3,2},{4,5},{5,4},{6,7},{7,6},{8,9},{9,8},{10,11... | collective-permute-start | bytes 1081352 | tf_op jit(solution)/shard_map/ppermute | solution.py:759
  106.0 7.9 %collective-permute-start.10 = (bf16[1,160,512]{2,1,0:T(8,128)(2,1)S(1)}, bf16[1,160,512]{2,1,0:T(8,128)(2,1)S(1)}, u32[]{:S(2)}, u32[]{:S(2)}) collective-permute-start(bf16[1,160,512]{2,1,0:T(8,128)(2,1)S(1)} %add_convert_fusion.9), channel_id=1, source_target_pairs={{0,6},{1,7},{2,4},{3,5},{4,2},{5,3},{6,0},{7,1},{8,14},{9,15},{10,... | collective-permute-start | bytes 491528 | tf_op jit(solution)/shard_map/ppermute | solution.py:759
  110.0 7.1 %collective-permute-start.4 = (bf16[1,176,512]{2,1,0:T(8,128)(2,1)S(1)}, bf16[1,176,512]{2,1,0:T(8,128)(2,1)S(1)}, u32[]{:S(2)}, u32[]{:S(2)}) collective-permute-start(bf16[1,176,512]{2,1,0:T(8,128)(2,1)S(1)} %add_convert_fusion.5), channel_id=1, source_target_pairs={{0,1},{1,0},{2,3},{3,2},{4,5},{5,4},{6,7},{7,6},{8,9},{9,8},{10,11... | collective-permute-start | bytes 540680 | tf_op jit(solution)/shard_map/ppermute | solution.py:759
  113.6 5.6 %collective-permute-start.7 = (bf16[1,176,512]{2,1,0:T(8,128)(2,1)S(1)}, bf16[1,176,512]{2,1,0:T(8,128)(2,1)S(1)}, u32[]{:S(2)}, u32[]{:S(2)}) collective-permute-start(bf16[1,176,512]{2,1,0:T(8,128)(2,1)S(1)} %add_convert_fusion.1), channel_id=1, source_target_pairs={{0,2},{1,3},{2,0},{3,1},{4,6},{5,7},{6,4},{7,5},{8,10},{9,11},{10,... | collective-permute-start | bytes 540680 | tf_op jit(solution)/shard_map/ppermute | solution.py:759

commit v5 on v4

--- a/solution.py
+++ b/solution.py
@@ -68,7 +68,7 @@
 
 def scale_rows(source, begin, gain, xs, squares):
     depth = source.shape[1]
-    step = min(source.shape[0], TILE)
+    step = min(source.shape[0], 32)
     for r in range(0, source.shape[0], step):
         x = source[r : r + step, :].astype(F32)
         xs[begin + r : begin + r + step, :] = (x * gain).astype(BF16)
@@ -82,14 +82,16 @@
 def scale_mirrored(source, begin, gain, xs):
     size, depth = source.shape
     flip = reversal(FLIP)
+    step = min(size, 512)
     for i in range(depth // FLIP):
         at = depth - (i + 1) * FLIP
         lanes = slice(i * FLIP, (i + 1) * FLIP)
-        x = dot(source[:, at : at + FLIP], flip)
-        xs[begin : begin + size, lanes] = (x * gain[:, lanes]).astype(BF16)
-
-
-def accumulate(xs, acc, weights, splits):
+        for r in range(0, size, step):
+            x = dot(source[r : r + step, at : at + FLIP], flip)
+            xs[begin + r : begin + r + step, lanes] = (x * gain[:, lanes]).astype(BF16)
+
+
+def accumulate(xs, acc, weights, splits, first=False):
     part = xs.shape[0] // splits
     depth = weights[0].shape[0]
     for i in range(splits):
@@ -97,7 +99,7 @@
         total = dot(xs[at, :depth], weights[0][...])
         for j in range(1, len(weights)):
             total = total + dot(xs[at, j * depth : (j + 1) * depth], weights[j][...])
-        acc[at, :] += total
+        acc[at, :] = total if first else acc[at, :] + total
 
 
 def finish_rms(squares, width):
@@ -125,37 +127,43 @@
     return spans + [(tokens, 0, HALO), (tokens + HALO, tokens + HALO, HALO)]
 
 
-def mix_step(hid, before, after, gain, wv, wbc, wst, mix, steps, acc_v, acc_b, acc_s, xs, squares, last):
-    tokens, depth = hid[0].shape
+def multiply_mix(scaled, halo, lanes, wv, wbc, wst, acc_v, acc_b, acc_s, first):
+    tokens = scaled.shape[1]
+    rows = halo.shape[1] + tokens
+    for b in range(2):
+        totals = [0.0, 0.0, 0.0]
+        for i in range(2):
+            x = jnp.concatenate([scaled[b, :, lanes[i]], halo[b, :, lanes[i]]], axis=0)
+            totals[0] += dot(x, wv[i][...])
+            totals[1] += dot(x, wbc[i][...])
+            totals[2] += lax.dot_general(
+                wst[i][...], scaled[b, :, lanes[i]], NT, preferred_element_type=F32
+            )
+        at = slice(b * rows, (b + 1) * rows)
+        acc_v[at, :] = totals[0] if first else acc_v[at, :] + totals[0]
+        acc_b[at, :] = totals[1] if first else acc_b[at, :] + totals[1]
+        acc_s[b] = totals[2] if first else acc_s[b] + totals[2]
+
+
+def finish_mix(mix, steps, acc_v, acc_b, acc_s, squares):
+    heads, tokens = acc_s.shape[1:]
     rows = tokens + 2 * HALO
     inner, maps = acc_v.shape[1], acc_b.shape[1]
-    heads = acc_s.shape[1]
     chunks = tokens // CHUNK
-    scale_all(hid, gain, xs, squares, (before, after))
-    accumulate(xs, acc_v, wv, 3)
-    accumulate(xs, acc_b, wbc, 3)
+    finish_rms(squares, WIDTH)
+    spans = [slice(c * CHUNK, (c + 1) * CHUNK) for c in range(chunks)]
+    scale = jnp.concatenate([squares[at, :heads] for at in spans], axis=1)
     for b in range(2):
-        at = slice(b * rows, b * rows + tokens)
-        total = lax.dot_general(wst[0][...], xs[at, :depth], NT, preferred_element_type=F32)
-        total = total + lax.dot_general(wst[1][...], xs[at, depth:], NT, preferred_element_type=F32)
-        acc_s[b] += total
-
-    @pl.when(last)
-    def _():
-        finish_rms(squares, WIDTH)
-        spans = [slice(c * CHUNK, (c + 1) * CHUNK) for c in range(chunks)]
-        scale = jnp.concatenate([squares[at, :heads] for at in spans], axis=1)
-        for b in range(2):
-            stack = [acc_s[b, :, at] for at in spans]
-            stack.append(jnp.zeros((TILE - chunks * heads, CHUNK), F32))
-            steps[b] = jnp.concatenate(stack, axis=0).T[:, : chunks * heads] * scale
-            for r, out, size in placed(tokens):
-                here = slice(b * rows + r, b * rows + r + size)
-                scales = squares[r : r + size, :]
-                for c in range(0, inner, TILE):
-                    mix[b, c // TILE, out : out + size, :] = acc_v[here, c : c + TILE] * scales
-                for c in range(0, maps, TILE):
-                    mix[b, (inner + c) // TILE, out : out + size, :] = acc_b[here, c : c + TILE] * scales
+        stack = [acc_s[b, :, at] for at in spans]
+        stack.append(jnp.zeros((TILE - chunks * heads, CHUNK), F32))
+        steps[b] = jnp.concatenate(stack, axis=0).T[:, : chunks * heads] * scale
+        for r, out, size in placed(tokens):
+            here = slice(b * rows + r, b * rows + r + size)
+            scales = squares[r : r + size, :]
+            for c in range(0, inner, TILE):
+                mix[b, c // TILE, out : out + size, :] = acc_v[here, c : c + TILE] * scales
+            for c in range(0, maps, TILE):
+                mix[b, (inner + c) // TILE, out : out + size, :] = acc_b[here, c : c + TILE] * scales
 
 
 def gate_kernel(*refs):
@@ -181,7 +189,7 @@
                 for c in range(0, gate_ref.shape[2], TILE):
                     gate_ref[b, r : r + TILE, c : c + TILE] = silu(
                         acc_g[b * tokens + r : b * tokens + r + TILE, c : c + TILE] * scale
-                    )
+                    ).astype(BF16)
 
 
 def convolved(source, row, taps):
@@ -229,7 +237,7 @@
         + paired((1, DEPTH), across)
         + paired((DEPTH, inner), downward),
         out_specs=pl.BlockSpec((2, tokens, inner), lambda k: (0, 0, 0)),
-        out_shape=jax.ShapeDtypeStruct((2, tokens, inner), F32),
+        out_shape=jax.ShapeDtypeStruct((2, tokens, inner), BF16),
         scratch_shapes=[
             pltpu.VMEM((2 * tokens, inner), F32),
             pltpu.VMEM((2 * tokens, 2 * DEPTH), BF16),
@@ -372,28 +380,109 @@
 COLUMNS = 6
 
 
-def front_kernel(*refs):
-    hid, before, after, gain, wv, wbc, wst = (refs[2 * i : 2 * i + 2] for i in range(7))
-    small, outs, scratch = refs[14:20], refs[20:29], refs[29:]
-    acc_v, acc_b, acc_s, xs, squares, mix, steps = scratch[:7]
-    i = pl.program_id(0)
-
-    @pl.when(i == 0)
-    def _():
-        for acc in (acc_v, acc_b, acc_s, squares):
-            acc[...] = jnp.zeros_like(acc)
-
-    @pl.when(i < PAIRS)
-    def _():
-        mix_step(
-            hid, before, after, gain, wv, wbc, wst, mix, steps, acc_v, acc_b, acc_s, xs, squares,
-            i == PAIRS - 1,
+SMALL = 8
+OUTS = 9
+
+
+def front_kernel(scaled_ref, square_ref, before_ref, after_ref, *rest):
+    far, rest = rest[: SMALL + 2], rest[SMALL + 2 :]
+    far_outs, rest = rest[:OUTS], rest[OUTS:]
+    near, rest = rest[: SMALL + 2], rest[SMALL + 2 :]
+    outs, rest = rest[:OUTS], rest[OUTS:]
+    small_sem, weight_sem, out_sem, acc_v, acc_b, acc_s, halo, squares, mix, steps = rest[:10]
+    gain, wst = near[:2]
+    wv, wbc = near[SMALL:]
+
+    fetches = [pltpu.make_async_copy(far[i], near[i], small_sem.at[i]) for i in range(SMALL)]
+    blocks = [[pl.ds(j * DEPTH, DEPTH) for j in (p, 2 * PAIRS - 1 - p)] for p in range(PAIRS)]
+    loads = [
+        [
+            pltpu.make_async_copy(
+                far[SMALL + n].at[rows, :], near[SMALL + n].at[rows, :], weight_sem.at[p, h, n]
+            )
+            for h, rows in enumerate(blocks[p])
+            for n in range(2)
+        ]
+        for p in range(PAIRS)
+    ]
+    for copy in fetches[:2] + [copy for load in loads for copy in load] + fetches[2:]:
+        copy.start()
+    tokens = scaled_ref.shape[1]
+    squares[:tokens] = square_ref[...]
+    squares[tokens:] = jnp.zeros_like(squares[tokens:])
+    for copy in fetches[:2]:
+        copy.wait()
+    beside = jnp.concatenate([before_ref[...].astype(F32), after_ref[...].astype(F32)], axis=0)
+    scale_rows(beside, 0, gain[...], halo.at[0], squares.at[pl.ds(tokens, 2 * HALO)])
+    scale_mirrored(beside.astype(BF16), 0, gain[...], halo.at[1])
+    for p in range(PAIRS):
+        lanes = blocks[p]
+        for copy in loads[p]:
+            copy.wait()
+        multiply_mix(
+            scaled_ref,
+            halo,
+            lanes,
+            [wv.at[at, :] for at in lanes],
+            [wbc.at[at, :] for at in lanes],
+            [wst.at[:, at] for at in lanes],
+            acc_v, acc_b, acc_s, p == 0,
         )
-
-    @pl.when(i >= PAIRS)
-    def _():
-        b = i - PAIRS
-        conv_step(mix.at[b], steps.at[b], *small, *outs, *scratch[7:])
+    finish_mix(mix, steps, acc_v, acc_b, acc_s, squares)
+    for copy in fetches[2:]:
+        copy.wait()
+    stores = []
+    for b in range(2):
+        views = [out.at[b : b + 1] for out in outs[:-1]] + [outs[-1].at[:, b : b + 1]]
+        conv_step(mix.at[b], steps.at[b], *near[2:SMALL], *views, *rest[10:])
+        for n, (out, far_out) in enumerate(zip(outs, far_outs)):
+            at = (slice(None), b) if n == OUTS - 1 else (b,)
+            stores.append(pltpu.make_async_copy(out.at[at], far_out.at[at], out_sem.at[b, n]))
+            stores[-1].start()
+    for copy in stores:
+        copy.wait()
+
+
+def scale_kernel(far_ref, far_gain_ref, scaled_ref, square_ref, hid, gain, hid_sem, gain_sem):
+    blocks = [pl.ds(j * DEPTH, DEPTH) for p in range(PAIRS) for j in (p, 2 * PAIRS - 1 - p)]
+    fetch = pltpu.make_async_copy(far_gain_ref, gain, gain_sem)
+    fetch.start()
+    loads = [
+        pltpu.make_async_copy(far_ref.at[:, at], hid.at[:, at], hid_sem.at[i])
+        for i, at in enumerate(blocks)
+    ]
+    for copy in loads:
+        copy.start()
+    square_ref[...] = jnp.zeros_like(square_ref)
+    fetch.wait()
+    for p in range(PAIRS):
+        pair = blocks[2 * p : 2 * p + 2]
+        for i in range(2):
+            loads[2 * p + i].wait()
+            scale_rows(hid.at[:, pair[i]], 0, gain[:, pair[i]], scaled_ref.at[0, :, pair[i]], square_ref)
+            scale_mirrored(
+                hid.at[:, pair[i]], 0, gain[:, pair[1 - i]], scaled_ref.at[1, :, pair[1 - i]]
+            )
+
+
+def scale(hidden, gain):
+    tokens, width = hidden.shape
+    outs = pl.pallas_call(
+        scale_kernel,
+        in_specs=[pl.BlockSpec(memory_space=pltpu.HBM)] * 2,
+        out_specs=[pl.BlockSpec(memory_space=pltpu.VMEM)] * 2,
+        out_shape=[pltpu.VMEM((2, tokens, width), BF16), pltpu.VMEM((tokens, TILE), F32)],
+        scratch_shapes=[
+            pltpu.VMEM((tokens, width), BF16),
+            pltpu.VMEM((1, width), F32),
+            pltpu.SemaphoreType.DMA((2 * PAIRS,)),
+            pltpu.SemaphoreType.DMA,
+        ],
+        compiler_params=pltpu.CompilerParams(vmem_limit_bytes=20 << 20),
+        cost_estimate=pl.CostEstimate(flops=2 << 30, transcendentals=0, bytes_accessed=8 << 20),
+        name="scale",
+    )(*streamed(hidden, gain))
+    return [pltpu.with_memory_space_constraint(x, pltpu.VMEM) for x in outs]
 
 
 def front(
@@ -401,59 +490,42 @@
     base_ids, conv_value, conv_bc, step_bias, decay_rate, skip_gain,
 ):
     tokens, width = hidden.shape
+    scaled, squares = scale(hidden, norm_gain[None])
     inner, state, heads = w_value.shape[1], w_bc.shape[1] // 2, w_step.shape[1]
     rows = tokens + 2 * HALO
     chunks = tokens // CHUNK
-    branch = lambda k: jnp.maximum(k - PAIRS, 0)
-    one = lambda k: (branch(k), 0, 0)
-    flat = lambda k: (0, 0)
-    four = lambda k: (branch(k), 0, 0, 0)
-    five = lambda k: (branch(k), 0, 0, 0, 0)
+    far = (
+        norm_gain[None], w_step.T, base_ids, conv_value, conv_bc, step_bias, decay_rate, skip_gain,
+        w_value, w_bc,
+    )
+    outs = (
+        ((2, tokens, inner), F32),
+        ((2, tokens, inner), BF16),
+        ((2, tokens, inner), BF16),
+        ((2, 2, tokens, state), BF16),
+        ((2, 2, tokens, state), BF16),
+        ((2, chunks, CHUNK, COLUMNS * heads), F32),
+        ((2, chunks, 2, heads, CHUNK), F32),
+        ((2, 2, chunks, state, inner), BF16),
+        ((2, 2, inner // TILE, state + 16, TILE), BF16),
+    )
+    here = pl.BlockSpec(memory_space=pltpu.VMEM)
+    there = pl.BlockSpec(memory_space=pltpu.HBM)
     return pl.pallas_call(
         front_kernel,
-        grid=(PAIRS + 2,),
-        in_specs=paired((tokens, DEPTH), across)
-        + paired((HALO, DEPTH), across)
-        + paired((HALO, DEPTH), across)
-        + paired((1, DEPTH), across)
-        + paired((DEPTH, inner), downward)
-        + paired((DEPTH, 2 * state), downward)
-        + paired((heads, DEPTH), across)
+        in_specs=[here] * 4 + [there] * len(far),
+        out_specs=[there] * OUTS,
+        out_shape=[pltpu.HBM(*out) for out in outs],
+        scratch_shapes=[pltpu.VMEM(x.shape, x.dtype) for x in far]
+        + [pltpu.VMEM(*out) for out in outs]
         + [
-            pl.BlockSpec((chunks, CHUNK), flat),
-            pl.BlockSpec((CONV, inner), flat),
-            pl.BlockSpec((CONV, 2 * state), flat),
-            pl.BlockSpec((1, heads), flat),
-            pl.BlockSpec((1, heads), flat),
-            pl.BlockSpec((1, heads), flat),
-        ],
-        out_specs=[
-            pl.BlockSpec((1, tokens, inner), one),
-            pl.BlockSpec((1, tokens, inner), one),
-            pl.BlockSpec((1, tokens, inner), one),
-            pl.BlockSpec((1, 2, tokens, state), four),
-            pl.BlockSpec((1, 2, tokens, state), four),
-            pl.BlockSpec((1, chunks, CHUNK, COLUMNS * heads), four),
-            pl.BlockSpec((1, chunks, 2, heads, CHUNK), five),
-            pl.BlockSpec((1, 2, chunks, state, inner), five),
-            pl.BlockSpec((2, 1, inner // TILE, state + 16, TILE), lambda k: (0, branch(k), 0, 0, 0)),
-        ],
-        out_shape=[
-            jax.ShapeDtypeStruct((2, tokens, inner), F32),
-            jax.ShapeDtypeStruct((2, tokens, inner), BF16),
-            jax.ShapeDtypeStruct((2, tokens, inner), BF16),
-            jax.ShapeDtypeStruct((2, 2, tokens, state), BF16),
-            jax.ShapeDtypeStruct((2, 2, tokens, state), BF16),
-            jax.ShapeDtypeStruct((2, chunks, CHUNK, COLUMNS * heads), F32),
-            jax.ShapeDtypeStruct((2, chunks, 2, heads, CHUNK), F32),
-            jax.ShapeDtypeStruct((2, 2, chunks, state, inner), BF16),
-            jax.ShapeDtypeStruct((2, 2, inner // TILE, state + 16, TILE), BF16),
-        ],
-        scratch_shapes=[
+            pltpu.SemaphoreType.DMA((SMALL,)),
+            pltpu.SemaphoreType.DMA((PAIRS, 2, 2)),
+            pltpu.SemaphoreType.DMA((2, OUTS)),
             pltpu.VMEM((2 * rows, inner), F32),
             pltpu.VMEM((2 * rows, 2 * state), F32),
             pltpu.VMEM((2, heads, tokens), F32),
-            pltpu.VMEM((2 * rows, 2 * DEPTH), BF16),
+            pltpu.VMEM((2, 2 * HALO, width), BF16),
             pltpu.VMEM((rows, TILE), F32),
             pltpu.VMEM((2, (inner + 2 * state) // TILE, rows, TILE), F32),
             pltpu.VMEM((2, CHUNK, heads * chunks), F32),
@@ -465,17 +537,14 @@
             pltpu.VMEM((tokens, inner), BF16),
             pltpu.VMEM((state, inner), F32),
         ],
-        compiler_params=params(GRANT),
+        compiler_params=pltpu.CompilerParams(vmem_limit_bytes=44 << 20),
         cost_estimate=pl.CostEstimate(
             flops=4 * rows * width * (inner + 2 * state + FLIP),
             transcendentals=1 << 22,
             bytes_accessed=24 << 20,
         ),
         name="front",
-    )(
-        *twice(*streamed(hidden), before, after, norm_gain[None], *streamed(w_value, w_bc, w_step.T)),
-        base_ids, conv_value, conv_bc, step_bias, decay_rate, skip_gain,
-    )
+    )(scaled, squares, before, after, *streamed(*far))
 
 
 def within_kernel(direct_ref, xf_ref, xb_ref, b_ref, c_ref, cols_ref, rows_ref, enter_ref, local_ref):
@@ -604,7 +673,7 @@
         y = local_ref[0, :, lanes]
         y = y + scale_f[:, lanes] * dot(c_ref[0, 0], into_f)
         y = y + scale_b[:, lanes] * dot(c_ref[0, 1], into_b)
-        y = y * silu_ref[0, :, lanes]
+        y = y * silu_ref[0, :, lanes].astype(F32)
         square = y * y
         high = square.astype(BF16)
         low = (square - high.astype(F32)).astype(BF16)
@@ -814,7 +883,11 @@
     incoming = incoming.reshape(final.shape[:3] + incoming.shape[1:])
     gate = project_gate(hidden, late_gain, w_gate)
     sends, keeps = output(local, gate, c_maps, cols, incoming, out_gain[None], w_out)
-    return jnp.concatenate([reduced(*group) for group in zip(sends, keeps, ORDERS)], axis=0)
+    groups = [reduced(*group) for group in zip(sends, keeps, ORDERS)]
+    mixed = jnp.zeros((sum(GROUPS[-1]), groups[0].shape[1]), BF16)
+    for (row, _), group in zip(GROUPS, groups):
+        mixed = lax.dynamic_update_slice(mixed, group, (row, 0))
+    return mixed
 
 
 def solution(mesh):

time: 121 us -> 120 us (level)
  waiting for transfers between devices: 23.6 us -> 19.7 us
  Pallas kernels: 60.1 us -> 62.8 us
    ppermute x1, waiting for transfers between devices: 3.72 us -> 0.01 us  [shards(): after = lax.ppermute(hidden[:HALO], 'ctx', down)]
    pallas_call x1 -> x2, Pallas kernels: 22.8 us -> 26 us  [the longest x1 20.7 us: front(): pl.pallas_call(front_kernel, in_specs=[here] * 4 + [there] * len(far), ou...]
  transfers between devices with their start and end apart: 13 -> 13, of which waited for: 10 -> 9; matrix products, arithmetic and copies ran while one was open for 1% -> 1% of each run, Pallas kernels for 21% -> 25%
where the time goes in v5:
time: 120 us; the launch traced here: 119 us
  Pallas kernels  62.8 us (52%)
  starting transfers between devices  33.2 us (28%)
  waiting for transfers between devices  19.7 us (16%)
  local copies, waits for them, and re-layouts  1.7 us (1%)
  other arithmetic  1.52 us (1%)
    pallas_call x1, Pallas kernels, front(): pl.pallas_call(front_kernel, in_specs=[here] * 4 + [there] * len(far), ou...  20.7 us
    ppermute x9, starting transfers between devices, reduced(): arrived = lax.ppermute(send, 'head', pairs)  17.5 us
    ppermute x9, waiting for transfers between devices, reduced(): arrived = lax.ppermute(send, 'head', pairs)  16.2 us
    pallas_call x1, Pallas kernels, output(): pl.pallas_call(send_kernel, grid_spec=pltpu.PrefetchScalarGridSpec(num_sc...  11 us
    pallas_call x1, Pallas kernels, project_gate(): pl.pallas_call(gate_kernel, grid=(PAIRS,), in_specs=paired((tokens, DEPTH...  9.53 us
    all_to_all x1, starting transfers between devices, shards(): sent = lax.all_to_all(final.reshape(count, state, tile), 'ctx', 0, 0)  9.52 us
    pallas_call x1, Pallas kernels, within(): pl.pallas_call(within_kernel, grid=(2 * chunks,), in_specs=[pl.BlockSpec(...  9.37 us
    pallas_call x1, Pallas kernels, output(): pl.pallas_call(keep_kernel, grid_spec=pltpu.PrefetchScalarGridSpec(num_sc...  5.93 us
  transfers between devices with their start and end apart: 13, of which 9 were waited for; matrix products, arithmetic and copies ran while one was open for 1% of the time, Pallas kernels for 25%

profile of v5, /device:TPU:0, one launch (start us, length us, event | category | flops | bytes accessed | tf_op | source)
XLA Modules:
  0.0 119.1 jit_solution(16116550064102719356)
XLA Ops:
  0.9 1.3 %collective-permute-start = (bf16[8,4096]{1,0:T(8,128)(2,1)S(1)}, bf16[8,4096]{1,0:T(8,128)(2,1)S(1)}, u32[]{:S(2)}, u32[]{:S(2)}) collective-permute-start(bf16[8,4096]{1,0:T(8,128)(2,1)S(1)} %get-tuple-element.50), channel_id=1, source_target_pairs={{0,8},{8,16},{16,24},{24,32},{32,40},{40,48},{48,56},{56,64},{64,7... | collective-permute-start | bytes 196616 | tf_op jit(solution)/shard_map/ppermute | solution.py:866
  2.2 1.3 %collective-permute-start.1 = (bf16[8,4096]{1,0:T(8,128)(2,1)S(1)}, bf16[8,4096]{1,0:T(8,128)(2,1)S(1)}, u32[]{:S(2)}, u32[]{:S(2)}) collective-permute-start(bf16[8,4096]{1,0:T(8,128)(2,1)S(1)} %get-tuple-element.49), channel_id=1, source_target_pairs={{8,0},{16,8},{24,16},{32,24},{40,32},{48,40},{56,48},{64,56},{72,6... | collective-permute-start | bytes 196616 | tf_op jit(solution)/shard_map/ppermute | solution.py:867
  3.5 5.4 %scale.1 = (bf16[2,512,4096]{2,1,0:T(8,128)(2,1)S(1)}, f32[512,128]{1,0:T(8,128)S(1)}) custom-call(bf16[512,4096]{1,0:T(8,128)(2,1)} %refs_1_.1, f32[1,4096]{1,0:T(1,128)} %bitcast.25), custom_call_target="tpu_custom_call" | custom-call | flops 2147483648 | bytes 8388608 | tf_op jit(solution)/shard_map/scale/pallas_call | solution.py:470
  8.9 20.7 %front.1 = (f32[2,512,512]{2,1,0:T(8,128)}, bf16[2,512,512]{2,1,0:T(8,128)(2,1)}, bf16[2,512,512]{2,1,0:T(8,128)(2,1)}, bf16[2,2,512,128]{3,2,1,0:T(8,128)(2,1)}...) custom-call(bf16[2,512,4096]{2,1,0:T(8,128)(2,1)S(1)} %get-tuple-ele, ...), custom_call_target="tpu_custom_call" | custom-call | flops 8858370048 | bytes 25165824 | tf_op jit(solution)/shard_map/front/pallas_call | solution.py:514
  29.5 9.5 %all-to-all-start = ((bf16[16,144,128]{2,1,0:T(8,128)(2,1)}), bf16[16,144,128]{2,1,0:T(8,128)(2,1)S(1)}, u32[]{:S(2)}, u32[]{:S(2)}) async-start(bf16[16,144,128]{2,1,0:T(8,128)(2,1)} %bitcast.23), calls=%async_computation | async-start | bytes 1179648 | tf_op jit(solution)/shard_map/all_to_all | solution.py:878
  39.1 9.4 %within.1.local_ref = f32[2,512,512]{2,1,0:T(8,128)} custom-call(f32[2,512,512]{2,1,0:T(8,128)} %get-tuple-element.30.direct_ref, bf16[2,512,512]{2,1,0:T(8,128)(2,1)} %get-tuple-element.31.xf_ref, bf16[2,512,512]{2,1,0:T(8,128)(2,1)} %get-tuple-element.32.xb_ref, bf16[2,2,512,128]{3,2,1,0:T(8,128)(2,1)} %get-tuple-element.33.b_ref, ...), custom_call_target="tpu_custom_call" | custom-call | flops 4294967296 | bytes 16777216 | tf_op jit(solution)/shard_map/within/pallas_call | solution.py:595
  48.4 2.2 %all-to-all-done.states_ref = bf16[16,144,128]{2,1,0:T(8,128)(2,1)S(1)} async-done(((bf16[16,144,128]{2,1,0:T(8,128)(2,1)}), bf16[16,144,128]{2,1,0:T(8,128)(2,1)S(1)}, u32[]{:S(2)}, u32[]{:S(2)}) %all-to-all-start) | async-done | bytes 589856 | tf_op jit(solution)/shard_map/all_to_all | solution.py:878
  51.6 3.6 %all-to-all-start.1 = ((bf16[16,128,128]{2,1,0:T(8,128)(2,1)}), bf16[16,128,128]{2,1,0:T(8,128)(2,1)S(1)}, u32[]{:S(2)}, u32[]{:S(2)}) async-start(bf16[16,128,128]{2,1,0:T(8,128)(2,1)} %chain.1), calls=%async_computation.1 | async-start | bytes 1048576 | tf_op jit(solution)/shard_map/all_to_all | solution.py:882
  55.2 9.5 %project_gate.1.silu_ref = bf16[2,512,512]{2,1,0:T(8,128)(2,1)} custom-call(bf16[512,4096]{1,0:T(8,128)(2,1)} %refs_1_.1, bf16[512,4096]{1,0:T(8,128)(2,1)} %refs_1_.1, f32[1,4096]{1,0:T(1,128)} %bitcast.27, f32[1,4096]{1,0:T(1,128)} %bitcast.28, bf16[4096,512]{1,0:T(8,128)(2,1)} %refs_5_.1, bf16[4096,512]{1,0:T(8,128)(2,1)} %refs_5_.1), custom_call_target="tpu_custom_call" | custom-call | flops 6442450944 | bytes 12582912 | tf_op jit(solution)/shard_map/project_gate/pallas_call | solution.py:233
  64.7 1.3 %all-to-all-done.1 = bf16[16,128,128]{2,1,0:T(8,128)(2,1)S(1)} async-done(((bf16[16,128,128]{2,1,0:T(8,128)(2,1)}), bf16[16,128,128]{2,1,0:T(8,128)(2,1)S(1)}, u32[]{:S(2)}, u32[]{:S(2)}) %all-to-all-start.1) | async-done | bytes 524320 | tf_op jit(solution)/shard_map/all_to_all | solution.py:882
  66.0 11.0 %output_send.1 = (bf16[4,176,512]{2,1,0:T(8,128)(2,1)S(1)}, bf16[4,176,512]{2,1,0:T(8,128)(2,1)S(1)}, bf16[4,160,512]{2,1,0:T(8,128)(2,1)S(1)}, bf16[2,512,512]{2,1,0:T(8,128)(2,1)S(1)}) custom-call(s32[1]{0:T(128)} %bitcast.place_ref, f32[2,512,512]{2,1,0:T(8,128)} %within.1.local_ref, bf16[2,512,512]{2,1,0:T(8,128)(2,1)} %project_gate.1.silu_ref, ...), custom_call_target="tpu_custom_call" | custom-call | flops 3221225472 | bytes 14680064 | tf_op jit(solution)/shard_map/output_send/pallas_call | solution.py:772
  77.0 3.1 %collective-permute-start.8 = (bf16[4,160,512]{2,1,0:T(8,128)(2,1)S(1)}, bf16[4,160,512]{2,1,0:T(8,128)(2,1)S(1)}, u32[]{:S(2)}, u32[]{:S(2)}) collective-permute-start(bf16[4,160,512]{2,1,0:T(8,128)(2,1)S(1)} %get-tuple-element.48), channel_id=1, source_target_pairs={{0,1},{1,0},{2,3},{3,2},{4,5},{5,4},{6,7},{7,6},{8,9},{9,8},{10,11... | collective-permute-start | bytes 1966088 | tf_op jit(solution)/shard_map/ppermute | solution.py:828
  80.2 1.5 %collective-permute-start.2 = (bf16[4,176,512]{2,1,0:T(8,128)(2,1)S(1)}, bf16[4,176,512]{2,1,0:T(8,128)(2,1)S(1)}, u32[]{:S(2)}, u32[]{:S(2)}) collective-permute-start(bf16[4,176,512]{2,1,0:T(8,128)(2,1)S(1)} %get-tuple-element.44), channel_id=1, source_target_pairs={{0,2},{1,3},{2,0},{3,1},{4,6},{5,7},{6,4},{7,5},{8,10},{9,11},{10,... | collective-permute-start | bytes 2162696 | tf_op jit(solution)/shard_map/ppermute | solution.py:828
  81.7 2.1 %collective-permute-start.5 = (bf16[4,176,512]{2,1,0:T(8,128)(2,1)S(1)}, bf16[4,176,512]{2,1,0:T(8,128)(2,1)S(1)}, u32[]{:S(2)}, u32[]{:S(2)}) collective-permute-start(bf16[4,176,512]{2,1,0:T(8,128)(2,1)S(1)} %get-tuple-element.46), channel_id=1, source_target_pairs={{0,6},{1,7},{2,4},{3,5},{4,2},{5,3},{6,0},{7,1},{8,14},{9,15},{10,... | collective-permute-start | bytes 2162696 | tf_op jit(solution)/shard_map/ppermute | solution.py:828
  83.8 5.9 %output_keep.1 = (f32[4,176,512]{2,1,0:T(8,128)S(1)}, f32[4,176,512]{2,1,0:T(8,128)S(1)}, f32[4,160,512]{2,1,0:T(8,128)S(1)}) custom-call(s32[1]{0:T(128)} %bitcast.place_ref, bf16[2,512,512]{2,1,0:T(8,128)(2,1)S(1)} %get-tuple-element.42.normed_ref, bf16[512,4096]{1,0:T(8,128)(2,1)} %wmir_ref.3, bf16[512,4096]{1,0:T(8,128)(2,1)} %wmir_ref.3), custom_call_target="tpu_custom_call" | custom-call | flops 3221225472 | bytes 10485760 | tf_op jit(solution)/shard_map/output_keep/pallas_call | solution.py:803
  89.7 4.9 %collective-permute-done.8 = bf16[4,160,512]{2,1,0:T(8,128)(2,1)S(1)} collective-permute-done((bf16[4,160,512]{2,1,0:T(8,128)(2,1)S(1)}, bf16[4,160,512]{2,1,0:T(8,128)(2,1)S(1)}, u32[]{:S(2)}, u32[]{:S(2)}) %collective-permute-start.8) | collective-permute-done | bytes 655392 | tf_op jit(solution)/shard_map/ppermute | solution.py:828
  94.7 1.6 %collective-permute-start.9 = (bf16[2,160,512]{2,1,0:T(8,128)(2,1)S(1)}, bf16[2,160,512]{2,1,0:T(8,128)(2,1)S(1)}, u32[]{:S(2)}, u32[]{:S(2)}) collective-permute-start(bf16[2,160,512]{2,1,0:T(8,128)(2,1)S(1)} %pad_maximum_fusion.2), channel_id=1, source_target_pairs={{0,2},{1,3},{2,0},{3,1},{4,6},{5,7},{6,4},{7,5},{8,10},{9,11},{10,... | collective-permute-start | bytes 983048 | tf_op jit(solution)/shard_map/ppermute | solution.py:828
  96.3 2.4 %collective-permute-done.2 = bf16[4,176,512]{2,1,0:T(8,128)(2,1)S(1)} collective-permute-done((bf16[4,176,512]{2,1,0:T(8,128)(2,1)S(1)}, bf16[4,176,512]{2,1,0:T(8,128)(2,1)S(1)}, u32[]{:S(2)}, u32[]{:S(2)}) %collective-permute-start.2) | collective-permute-done | bytes 720928 | tf_op jit(solution)/shard_map/ppermute | solution.py:828
  98.8 2.9 %collective-permute-start.3 = (bf16[2,176,512]{2,1,0:T(8,128)(2,1)S(1)}, bf16[2,176,512]{2,1,0:T(8,128)(2,1)S(1)}, u32[]{:S(2)}, u32[]{:S(2)}) collective-permute-start(bf16[2,176,512]{2,1,0:T(8,128)(2,1)S(1)} %pad_maximum_fusion), channel_id=1, source_target_pairs={{0,6},{1,7},{2,4},{3,5},{4,2},{5,3},{6,0},{7,1},{8,14},{9,15},{10,... | collective-permute-start | bytes 1081352 | tf_op jit(solution)/shard_map/ppermute | solution.py:828
  101.9 2.4 %collective-permute-done.9 = bf16[2,160,512]{2,1,0:T(8,128)(2,1)S(1)} collective-permute-done((bf16[2,160,512]{2,1,0:T(8,128)(2,1)S(1)}, bf16[2,160,512]{2,1,0:T(8,128)(2,1)S(1)}, u32[]{:S(2)}, u32[]{:S(2)}) %collective-permute-start.9) | collective-permute-done | bytes 327712 | tf_op jit(solution)/shard_map/ppermute | solution.py:828
  104.4 2.8 %collective-permute-start.10 = (bf16[1,160,512]{2,1,0:T(8,128)(2,1)S(1)}, bf16[1,160,512]{2,1,0:T(8,128)(2,1)S(1)}, u32[]{:S(2)}, u32[]{:S(2)}) collective-permute-start(bf16[1,160,512]{2,1,0:T(8,128)(2,1)S(1)} %add_convert_fusion.9), channel_id=1, source_target_pairs={{0,6},{1,7},{2,4},{3,5},{4,2},{5,3},{6,0},{7,1},{8,14},{9,15},{10,... | collective-permute-start | bytes 491528 | tf_op jit(solution)/shard_map/ppermute | solution.py:828
  108.1 3.1 %collective-permute-start.4 = (bf16[1,176,512]{2,1,0:T(8,128)(2,1)S(1)}, bf16[1,176,512]{2,1,0:T(8,128)(2,1)S(1)}, u32[]{:S(2)}, u32[]{:S(2)}) collective-permute-start(bf16[1,176,512]{2,1,0:T(8,128)(2,1)S(1)} %add_convert_fusion.5), channel_id=1, source_target_pairs={{0,1},{1,0},{2,3},{3,2},{4,5},{5,4},{6,7},{7,6},{8,9},{9,8},{10,11... | collective-permute-start | bytes 540680 | tf_op jit(solution)/shard_map/ppermute | solution.py:828
  112.1 3.0 %collective-permute-done.4 = bf16[1,176,512]{2,1,0:T(8,128)(2,1)S(1)} collective-permute-done((bf16[1,176,512]{2,1,0:T(8,128)(2,1)S(1)}, bf16[1,176,512]{2,1,0:T(8,128)(2,1)S(1)}, u32[]{:S(2)}, u32[]{:S(2)}) %collective-permute-start.4) | collective-permute-done | bytes 180256 | tf_op jit(solution)/shard_map/ppermute | solution.py:828
  115.3 2.2 %collective-permute-done.7 = bf16[1,176,512]{2,1,0:T(8,128)(2,1)S(1)} collective-permute-done((bf16[1,176,512]{2,1,0:T(8,128)(2,1)S(1)}, bf16[1,176,512]{2,1,0:T(8,128)(2,1)S(1)}, u32[]{:S(2)}, u32[]{:S(2)}) %collective-permute-start.7) | collective-permute-done | bytes 180256 | tf_op jit(solution)/shard_map/ppermute | solution.py:828
  (27 shorter events, 5.9 us)
Async XLA Ops:
  0.9 8.0 %collective-permute-start = (bf16[8,4096]{1,0:T(8,128)(2,1)S(1)}, bf16[8,4096]{1,0:T(8,128)(2,1)S(1)}, u32[]{:S(2)}, u32[]{:S(2)}) collective-permute-start(bf16[8,4096]{1,0:T(8,128)(2,1)S(1)} %get-tuple-element.50), channel_id=1, source_target_pairs={{0,8},{8,16},{16,24},{24,32},{32,40},{40,48},{48,56},{56,64},{64,7... | collective-permute-start | bytes 196616 | tf_op jit(solution)/shard_map/ppermute | solution.py:866
  2.2 6.7 %collective-permute-start.1 = (bf16[8,4096]{1,0:T(8,128)(2,1)S(1)}, bf16[8,4096]{1,0:T(8,128)(2,1)S(1)}, u32[]{:S(2)}, u32[]{:S(2)}) collective-permute-start(bf16[8,4096]{1,0:T(8,128)(2,1)S(1)} %get-tuple-element.49), channel_id=1, source_target_pairs={{8,0},{16,8},{24,16},{32,24},{40,32},{48,40},{56,48},{64,56},{72,6... | collective-permute-start | bytes 196616 | tf_op jit(solution)/shard_map/ppermute | solution.py:867
  29.5 21.1 %all-to-all-start = ((bf16[16,144,128]{2,1,0:T(8,128)(2,1)}), bf16[16,144,128]{2,1,0:T(8,128)(2,1)S(1)}, u32[]{:S(2)}, u32[]{:S(2)}) async-start(bf16[16,144,128]{2,1,0:T(8,128)(2,1)} %bitcast.23), calls=%async_computation | async-start | bytes 1179648 | tf_op jit(solution)/shard_map/all_to_all | solution.py:878
  51.6 14.4 %all-to-all-start.1 = ((bf16[16,128,128]{2,1,0:T(8,128)(2,1)}), bf16[16,128,128]{2,1,0:T(8,128)(2,1)S(1)}, u32[]{:S(2)}, u32[]{:S(2)}) async-start(bf16[16,128,128]{2,1,0:T(8,128)(2,1)} %chain.1), calls=%async_computation.1 | async-start | bytes 1048576 | tf_op jit(solution)/shard_map/all_to_all | solution.py:882
  55.2 10.8 %copy-start = (f32[512]{0:T(512)S(1)}, f32[512]{0:T(512)}, u32[]{:S(2)}) copy-start(f32[512]{0:T(512)} %param.26) | copy-start | bytes 6148
  77.0 17.6 %collective-permute-start.8 = (bf16[4,160,512]{2,1,0:T(8,128)(2,1)S(1)}, bf16[4,160,512]{2,1,0:T(8,128)(2,1)S(1)}, u32[]{:S(2)}, u32[]{:S(2)}) collective-permute-start(bf16[4,160,512]{2,1,0:T(8,128)(2,1)S(1)} %get-tuple-element.48), channel_id=1, source_target_pairs={{0,1},{1,0},{2,3},{3,2},{4,5},{5,4},{6,7},{7,6},{8,9},{9,8},{10,11... | collective-permute-start | bytes 1966088 | tf_op jit(solution)/shard_map/ppermute | solution.py:828
  80.2 18.5 %collective-permute-start.2 = (bf16[4,176,512]{2,1,0:T(8,128)(2,1)S(1)}, bf16[4,176,512]{2,1,0:T(8,128)(2,1)S(1)}, u32[]{:S(2)}, u32[]{:S(2)}) collective-permute-start(bf16[4,176,512]{2,1,0:T(8,128)(2,1)S(1)} %get-tuple-element.44), channel_id=1, source_target_pairs={{0,2},{1,3},{2,0},{3,1},{4,6},{5,7},{6,4},{7,5},{8,10},{9,11},{10,... | collective-permute-start | bytes 2162696 | tf_op jit(solution)/shard_map/ppermute | solution.py:828
  81.7 20.0 %collective-permute-start.5 = (bf16[4,176,512]{2,1,0:T(8,128)(2,1)S(1)}, bf16[4,176,512]{2,1,0:T(8,128)(2,1)S(1)}, u32[]{:S(2)}, u32[]{:S(2)}) collective-permute-start(bf16[4,176,512]{2,1,0:T(8,128)(2,1)S(1)} %get-tuple-element.46), channel_id=1, source_target_pairs={{0,6},{1,7},{2,4},{3,5},{4,2},{5,3},{6,0},{7,1},{8,14},{9,15},{10,... | collective-permute-start | bytes 2162696 | tf_op jit(solution)/shard_map/ppermute | solution.py:828
  94.7 9.6 %collective-permute-start.9 = (bf16[2,160,512]{2,1,0:T(8,128)(2,1)S(1)}, bf16[2,160,512]{2,1,0:T(8,128)(2,1)S(1)}, u32[]{:S(2)}, u32[]{:S(2)}) collective-permute-start(bf16[2,160,512]{2,1,0:T(8,128)(2,1)S(1)} %pad_maximum_fusion.2), channel_id=1, source_target_pairs={{0,2},{1,3},{2,0},{3,1},{4,6},{5,7},{6,4},{7,5},{8,10},{9,11},{10,... | collective-permute-start | bytes 983048 | tf_op jit(solution)/shard_map/ppermute | solution.py:828
  98.8 9.2 %collective-permute-start.3 = (bf16[2,176,512]{2,1,0:T(8,128)(2,1)S(1)}, bf16[2,176,512]{2,1,0:T(8,128)(2,1)S(1)}, u32[]{:S(2)}, u32[]{:S(2)}) collective-permute-start(bf16[2,176,512]{2,1,0:T(8,128)(2,1)S(1)} %pad_maximum_fusion), channel_id=1, source_target_pairs={{0,6},{1,7},{2,4},{3,5},{4,2},{5,3},{6,0},{7,1},{8,14},{9,15},{10,... | collective-permute-start | bytes 1081352 | tf_op jit(solution)/shard_map/ppermute | solution.py:828
  101.8 9.9 %collective-permute-start.6 = (bf16[2,176,512]{2,1,0:T(8,128)(2,1)S(1)}, bf16[2,176,512]{2,1,0:T(8,128)(2,1)S(1)}, u32[]{:S(2)}, u32[]{:S(2)}) collective-permute-start(bf16[2,176,512]{2,1,0:T(8,128)(2,1)S(1)} %pad_maximum_fusion.1), channel_id=1, source_target_pairs={{0,1},{1,0},{2,3},{3,2},{4,5},{5,4},{6,7},{7,6},{8,9},{9,8},{10,11... | collective-permute-start | bytes 1081352 | tf_op jit(solution)/shard_map/ppermute | solution.py:828
  104.4 13.2 %collective-permute-start.10 = (bf16[1,160,512]{2,1,0:T(8,128)(2,1)S(1)}, bf16[1,160,512]{2,1,0:T(8,128)(2,1)S(1)}, u32[]{:S(2)}, u32[]{:S(2)}) collective-permute-start(bf16[1,160,512]{2,1,0:T(8,128)(2,1)S(1)} %add_convert_fusion.9), channel_id=1, source_target_pairs={{0,6},{1,7},{2,4},{3,5},{4,2},{5,3},{6,0},{7,1},{8,14},{9,15},{10,... | collective-permute-start | bytes 491528 | tf_op jit(solution)/shard_map/ppermute | solution.py:828
  108.1 7.1 %collective-permute-start.4 = (bf16[1,176,512]{2,1,0:T(8,128)(2,1)S(1)}, bf16[1,176,512]{2,1,0:T(8,128)(2,1)S(1)}, u32[]{:S(2)}, u32[]{:S(2)}) collective-permute-start(bf16[1,176,512]{2,1,0:T(8,128)(2,1)S(1)} %add_convert_fusion.5), channel_id=1, source_target_pairs={{0,1},{1,0},{2,3},{3,2},{4,5},{5,4},{6,7},{7,6},{8,9},{9,8},{10,11... | collective-permute-start | bytes 540680 | tf_op jit(solution)/shard_map/ppermute | solution.py:828
  111.9 5.6 %collective-permute-start.7 = (bf16[1,176,512]{2,1,0:T(8,128)(2,1)S(1)}, bf16[1,176,512]{2,1,0:T(8,128)(2,1)S(1)}, u32[]{:S(2)}, u32[]{:S(2)}) collective-permute-start(bf16[1,176,512]{2,1,0:T(8,128)(2,1)S(1)} %add_convert_fusion.1), channel_id=1, source_target_pairs={{0,2},{1,3},{2,0},{3,1},{4,6},{5,7},{6,4},{7,5},{8,10},{9,11},{10,... | collective-permute-start | bytes 540680 | tf_op jit(solution)/shard_map/ppermute | solution.py:828
  117.5 0.8 copy-start.1

commit v6 on v5

--- a/solution.py
+++ b/solution.py
@@ -189,7 +189,7 @@
                 for c in range(0, gate_ref.shape[2], TILE):
                     gate_ref[b, r : r + TILE, c : c + TILE] = silu(
                         acc_g[b * tokens + r : b * tokens + r + TILE, c : c + TILE] * scale
-                    ).astype(BF16)
+                    )
 
 
 def convolved(source, row, taps):
@@ -237,7 +237,7 @@
         + paired((1, DEPTH), across)
         + paired((DEPTH, inner), downward),
         out_specs=pl.BlockSpec((2, tokens, inner), lambda k: (0, 0, 0)),
-        out_shape=jax.ShapeDtypeStruct((2, tokens, inner), BF16),
+        out_shape=jax.ShapeDtypeStruct((2, tokens, inner), F32),
         scratch_shapes=[
             pltpu.VMEM((2 * tokens, inner), F32),
             pltpu.VMEM((2 * tokens, 2 * DEPTH), BF16),
@@ -272,7 +272,7 @@
 def conv_step(
     mix, steps, base_ref, tapv_ref, tapb_ref, bias_ref, rate_ref, skip_ref,
     direct_ref, xf_ref, xb_ref, maps_ref, cmaps_ref, cols_ref, rows_ref, enter_ref, final_ref,
-    dt_sc, wf_sc, wb_sc, keep_sc, vf_sc, vb_sc, carry_sc,
+    dt_sc, wf_sc, wb_sc, keep_sc, vf_sc, vb_sc, carry_sc, flush,
 ):
     tokens, inner = direct_ref.shape[1:]
     heads = bias_ref.shape[1]
@@ -359,6 +359,7 @@
         return carry
 
     lax.fori_loop(0, tokens // ROWS, block, 0)
+    flush()
 
     for direction, moved, order in ((0, vf_sc, range(chunks)), (1, vb_sc, range(chunks - 1, -1, -1))):
         for n, c in enumerate(order):
@@ -432,13 +433,21 @@
     for copy in fetches[2:]:
         copy.wait()
     stores = []
+
+    def store(b, which):
+        for n in which:
+            at = (slice(None), b) if n == OUTS - 1 else (b,)
+            copy = pltpu.make_async_copy(outs[n].at[at], far_outs[n].at[at], out_sem.at[b, n])
+            copy.start()
+            stores.append(copy)
+
     for b in range(2):
         views = [out.at[b : b + 1] for out in outs[:-1]] + [outs[-1].at[:, b : b + 1]]
-        conv_step(mix.at[b], steps.at[b], *near[2:SMALL], *views, *rest[10:])
-        for n, (out, far_out) in enumerate(zip(outs, far_outs)):
-            at = (slice(None), b) if n == OUTS - 1 else (b,)
-            stores.append(pltpu.make_async_copy(out.at[at], far_out.at[at], out_sem.at[b, n]))
-            stores[-1].start()
+        conv_step(
+            mix.at[b], steps.at[b], *near[2:SMALL], *views, *rest[10:],
+            functools.partial(store, b, range(OUTS - 2)),
+        )
+        store(b, range(OUTS - 2, OUTS))
     for copy in stores:
         copy.wait()
 
@@ -673,7 +682,7 @@
         y = local_ref[0, :, lanes]
         y = y + scale_f[:, lanes] * dot(c_ref[0, 0], into_f)
         y = y + scale_b[:, lanes] * dot(c_ref[0, 1], into_b)
-        y = y * silu_ref[0, :, lanes].astype(F32)
+        y = y * silu_ref[0, :, lanes]
         square = y * y
         high = square.astype(BF16)
         low = (square - high.astype(F32)).astype(BF16)
@@ -883,11 +892,7 @@
     incoming = incoming.reshape(final.shape[:3] + incoming.shape[1:])
     gate = project_gate(hidden, late_gain, w_gate)
     sends, keeps = output(local, gate, c_maps, cols, incoming, out_gain[None], w_out)
-    groups = [reduced(*group) for group in zip(sends, keeps, ORDERS)]
-    mixed = jnp.zeros((sum(GROUPS[-1]), groups[0].shape[1]), BF16)
-    for (row, _), group in zip(GROUPS, groups):
-        mixed = lax.dynamic_update_slice(mixed, group, (row, 0))
-    return mixed
+    return jnp.concatenate([reduced(*group) for group in zip(sends, keeps, ORDERS)], axis=0)
 
 
 def solution(mesh):

time: 120 us -> 119 us (level)
  transfers between devices with their start and end apart: 13 -> 13, of which waited for: 9 -> 9; matrix products, arithmetic and copies ran while one was open for 1% -> 1% of each run, Pallas kernels for 25% -> 26%
where the time goes in v6:
time: 119 us; the launch traced here: 118 us
  Pallas kernels  63.2 us (53%)
  starting transfers between devices  33.2 us (28%)
  waiting for transfers between devices  19.1 us (16%)
  other arithmetic  1.68 us (1%)
    pallas_call x1, Pallas kernels, front(): pl.pallas_call(front_kernel, in_specs=[here] * 4 + [there] * len(far), ou...  20.7 us
    ppermute x9, starting transfers between devices, reduced(): arrived = lax.ppermute(send, 'head', pairs)  17.6 us
    ppermute x9, waiting for transfers between devices, reduced(): arrived = lax.ppermute(send, 'head', pairs)  15.9 us
    pallas_call x1, Pallas kernels, output(): pl.pallas_call(send_kernel, grid_spec=pltpu.PrefetchScalarGridSpec(num_sc...  11.1 us
    pallas_call x1, Pallas kernels, project_gate(): pl.pallas_call(gate_kernel, grid=(PAIRS,), in_specs=paired((tokens, DEPTH...  9.8 us
    all_to_all x1, starting transfers between devices, shards(): sent = lax.all_to_all(final.reshape(count, state, tile), 'ctx', 0, 0)  9.52 us
    pallas_call x1, Pallas kernels, within(): pl.pallas_call(within_kernel, grid=(2 * chunks,), in_specs=[pl.BlockSpec(...  9.38 us
    pallas_call x1, Pallas kernels, output(): pl.pallas_call(keep_kernel, grid_spec=pltpu.PrefetchScalarGridSpec(num_sc...  5.93 us
  transfers between devices with their start and end apart: 13, of which 9 were waited for; matrix products, arithmetic and copies ran while one was open for 1% of the time, Pallas kernels for 26%

profile of v6, /device:TPU:0, one launch (start us, length us, event | category | flops | bytes accessed | tf_op | source)
XLA Modules:
  0.0 118.3 jit_solution(3491630533273120360)
XLA Ops:
  0.9 1.3 %collective-permute-start = (bf16[8,4096]{1,0:T(8,128)(2,1)S(1)}, bf16[8,4096]{1,0:T(8,128)(2,1)S(1)}, u32[]{:S(2)}, u32[]{:S(2)}) collective-permute-start(bf16[8,4096]{1,0:T(8,128)(2,1)S(1)} %get-tuple-element.50), channel_id=1, source_target_pairs={{0,8},{8,16},{16,24},{24,32},{32,40},{40,48},{48,56},{56,64},{64,7... | collective-permute-start | bytes 196616 | tf_op jit(solution)/shard_map/ppermute | solution.py:875
  2.2 1.3 %collective-permute-start.1 = (bf16[8,4096]{1,0:T(8,128)(2,1)S(1)}, bf16[8,4096]{1,0:T(8,128)(2,1)S(1)}, u32[]{:S(2)}, u32[]{:S(2)}) collective-permute-start(bf16[8,4096]{1,0:T(8,128)(2,1)S(1)} %get-tuple-element.49), channel_id=1, source_target_pairs={{8,0},{16,8},{24,16},{32,24},{40,32},{48,40},{56,48},{64,56},{72,6... | collective-permute-start | bytes 196616 | tf_op jit(solution)/shard_map/ppermute | solution.py:876
  3.5 5.4 %scale.1 = (bf16[2,512,4096]{2,1,0:T(8,128)(2,1)S(1)}, f32[512,128]{1,0:T(8,128)S(1)}) custom-call(bf16[512,4096]{1,0:T(8,128)(2,1)} %refs_1_.1, f32[1,4096]{1,0:T(1,128)} %bitcast.21), custom_call_target="tpu_custom_call" | custom-call | flops 2147483648 | bytes 8388608 | tf_op jit(solution)/shard_map/scale/pallas_call | solution.py:479
  8.9 20.7 %front.1 = (f32[2,512,512]{2,1,0:T(8,128)}, bf16[2,512,512]{2,1,0:T(8,128)(2,1)}, bf16[2,512,512]{2,1,0:T(8,128)(2,1)}, bf16[2,2,512,128]{3,2,1,0:T(8,128)(2,1)}...) custom-call(bf16[2,512,4096]{2,1,0:T(8,128)(2,1)S(1)} %get-tuple-ele, ...), custom_call_target="tpu_custom_call" | custom-call | flops 8858370048 | bytes 25165824 | tf_op jit(solution)/shard_map/front/pallas_call | solution.py:523
  29.6 9.5 %all-to-all-start = ((bf16[16,144,128]{2,1,0:T(8,128)(2,1)}), bf16[16,144,128]{2,1,0:T(8,128)(2,1)S(1)}, u32[]{:S(2)}, u32[]{:S(2)}) async-start(bf16[16,144,128]{2,1,0:T(8,128)(2,1)} %bitcast.19), calls=%async_computation | async-start | bytes 1179648 | tf_op jit(solution)/shard_map/all_to_all | solution.py:887
  39.1 9.4 %within.1.local_ref = f32[2,512,512]{2,1,0:T(8,128)} custom-call(f32[2,512,512]{2,1,0:T(8,128)} %get-tuple-element.30.direct_ref, bf16[2,512,512]{2,1,0:T(8,128)(2,1)} %get-tuple-element.31.xf_ref, bf16[2,512,512]{2,1,0:T(8,128)(2,1)} %get-tuple-element.32.xb_ref, bf16[2,2,512,128]{3,2,1,0:T(8,128)(2,1)} %get-tuple-element.33.b_ref, ...), custom_call_target="tpu_custom_call" | custom-call | flops 4294967296 | bytes 16777216 | tf_op jit(solution)/shard_map/within/pallas_call | solution.py:604
  48.5 2.2 %all-to-all-done.states_ref = bf16[16,144,128]{2,1,0:T(8,128)(2,1)S(1)} async-done(((bf16[16,144,128]{2,1,0:T(8,128)(2,1)}), bf16[16,144,128]{2,1,0:T(8,128)(2,1)S(1)}, u32[]{:S(2)}, u32[]{:S(2)}) %all-to-all-start) | async-done | bytes 589856 | tf_op jit(solution)/shard_map/all_to_all | solution.py:887
  51.6 3.6 %all-to-all-start.1 = ((bf16[16,128,128]{2,1,0:T(8,128)(2,1)}), bf16[16,128,128]{2,1,0:T(8,128)(2,1)S(1)}, u32[]{:S(2)}, u32[]{:S(2)}) async-start(bf16[16,128,128]{2,1,0:T(8,128)(2,1)} %chain.1), calls=%async_computation.1 | async-start | bytes 1048576 | tf_op jit(solution)/shard_map/all_to_all | solution.py:891
  55.2 9.8 %project_gate.1.silu_ref = f32[2,512,512]{2,1,0:T(8,128)} custom-call(bf16[512,4096]{1,0:T(8,128)(2,1)} %refs_1_.1, bf16[512,4096]{1,0:T(8,128)(2,1)} %refs_1_.1, f32[1,4096]{1,0:T(1,128)} %bitcast.23, f32[1,4096]{1,0:T(1,128)} %bitcast.24, bf16[4096,512]{1,0:T(8,128)(2,1)} %refs_5_.1, bf16[4096,512]{1,0:T(8,128)(2,1)} %refs_5_.1), custom_call_target="tpu_custom_call" | custom-call | flops 6442450944 | bytes 12582912 | tf_op jit(solution)/shard_map/project_gate/pallas_call | solution.py:233
  65.0 1.0 all-to-all-done.1
  66.0 11.1 %output_send.1 = (bf16[4,176,512]{2,1,0:T(8,128)(2,1)S(1)}, bf16[4,176,512]{2,1,0:T(8,128)(2,1)S(1)}, bf16[4,160,512]{2,1,0:T(8,128)(2,1)S(1)}, bf16[2,512,512]{2,1,0:T(8,128)(2,1)S(1)}) custom-call(s32[1]{0:T(128)} %bitcast.place_ref, f32[2,512,512]{2,1,0:T(8,128)} %within.1.local_ref, f32[2,512,512]{2,1,0:T(8,128)} %project_gate.1.silu_ref, ...), custom_call_target="tpu_custom_call" | custom-call | flops 3221225472 | bytes 14680064 | tf_op jit(solution)/shard_map/output_send/pallas_call | solution.py:781
  77.2 3.1 %collective-permute-start.8 = (bf16[4,160,512]{2,1,0:T(8,128)(2,1)S(1)}, bf16[4,160,512]{2,1,0:T(8,128)(2,1)S(1)}, u32[]{:S(2)}, u32[]{:S(2)}) collective-permute-start(bf16[4,160,512]{2,1,0:T(8,128)(2,1)S(1)} %get-tuple-element.48), channel_id=1, source_target_pairs={{0,1},{1,0},{2,3},{3,2},{4,5},{5,4},{6,7},{7,6},{8,9},{9,8},{10,11... | collective-permute-start | bytes 1966088 | tf_op jit(solution)/shard_map/ppermute | solution.py:837
  80.3 1.5 %collective-permute-start.2 = (bf16[4,176,512]{2,1,0:T(8,128)(2,1)S(1)}, bf16[4,176,512]{2,1,0:T(8,128)(2,1)S(1)}, u32[]{:S(2)}, u32[]{:S(2)}) collective-permute-start(bf16[4,176,512]{2,1,0:T(8,128)(2,1)S(1)} %get-tuple-element.44), channel_id=1, source_target_pairs={{0,2},{1,3},{2,0},{3,1},{4,6},{5,7},{6,4},{7,5},{8,10},{9,11},{10,... | collective-permute-start | bytes 2162696 | tf_op jit(solution)/shard_map/ppermute | solution.py:837
  81.8 2.1 %collective-permute-start.5 = (bf16[4,176,512]{2,1,0:T(8,128)(2,1)S(1)}, bf16[4,176,512]{2,1,0:T(8,128)(2,1)S(1)}, u32[]{:S(2)}, u32[]{:S(2)}) collective-permute-start(bf16[4,176,512]{2,1,0:T(8,128)(2,1)S(1)} %get-tuple-element.46), channel_id=1, source_target_pairs={{0,6},{1,7},{2,4},{3,5},{4,2},{5,3},{6,0},{7,1},{8,14},{9,15},{10,... | collective-permute-start | bytes 2162696 | tf_op jit(solution)/shard_map/ppermute | solution.py:837
  83.9 5.9 %output_keep.1 = (f32[4,176,512]{2,1,0:T(8,128)S(1)}, f32[4,176,512]{2,1,0:T(8,128)S(1)}, f32[4,160,512]{2,1,0:T(8,128)S(1)}) custom-call(s32[1]{0:T(128)} %bitcast.place_ref, bf16[2,512,512]{2,1,0:T(8,128)(2,1)S(1)} %get-tuple-element.42.normed_ref, bf16[512,4096]{1,0:T(8,128)(2,1)} %wmir_ref.3, bf16[512,4096]{1,0:T(8,128)(2,1)} %wmir_ref.3), custom_call_target="tpu_custom_call" | custom-call | flops 3221225472 | bytes 10485760 | tf_op jit(solution)/shard_map/output_keep/pallas_call | solution.py:812
  89.9 4.9 %collective-permute-done.8 = bf16[4,160,512]{2,1,0:T(8,128)(2,1)S(1)} collective-permute-done((bf16[4,160,512]{2,1,0:T(8,128)(2,1)S(1)}, bf16[4,160,512]{2,1,0:T(8,128)(2,1)S(1)}, u32[]{:S(2)}, u32[]{:S(2)}) %collective-permute-start.8) | collective-permute-done | bytes 655392 | tf_op jit(solution)/shard_map/ppermute | solution.py:837
  94.9 1.6 %collective-permute-start.9 = (bf16[2,160,512]{2,1,0:T(8,128)(2,1)S(1)}, bf16[2,160,512]{2,1,0:T(8,128)(2,1)S(1)}, u32[]{:S(2)}, u32[]{:S(2)}) collective-permute-start(bf16[2,160,512]{2,1,0:T(8,128)(2,1)S(1)} %pad_maximum_fusion.3), channel_id=1, source_target_pairs={{0,2},{1,3},{2,0},{3,1},{4,6},{5,7},{6,4},{7,5},{8,10},{9,11},{10,... | collective-permute-start | bytes 983048 | tf_op jit(solution)/shard_map/ppermute | solution.py:837
  96.5 2.4 %collective-permute-done.2 = bf16[4,176,512]{2,1,0:T(8,128)(2,1)S(1)} collective-permute-done((bf16[4,176,512]{2,1,0:T(8,128)(2,1)S(1)}, bf16[4,176,512]{2,1,0:T(8,128)(2,1)S(1)}, u32[]{:S(2)}, u32[]{:S(2)}) %collective-permute-start.2) | collective-permute-done | bytes 720928 | tf_op jit(solution)/shard_map/ppermute | solution.py:837
  99.0 2.8 %collective-permute-start.3 = (bf16[2,176,512]{2,1,0:T(8,128)(2,1)S(1)}, bf16[2,176,512]{2,1,0:T(8,128)(2,1)S(1)}, u32[]{:S(2)}, u32[]{:S(2)}) collective-permute-start(bf16[2,176,512]{2,1,0:T(8,128)(2,1)S(1)} %pad_maximum_fusion.1), channel_id=1, source_target_pairs={{0,6},{1,7},{2,4},{3,5},{4,2},{5,3},{6,0},{7,1},{8,14},{9,15},{10,... | collective-permute-start | bytes 1081352 | tf_op jit(solution)/shard_map/ppermute | solution.py:837
  102.1 2.4 %collective-permute-done.9 = bf16[2,160,512]{2,1,0:T(8,128)(2,1)S(1)} collective-permute-done((bf16[2,160,512]{2,1,0:T(8,128)(2,1)S(1)}, bf16[2,160,512]{2,1,0:T(8,128)(2,1)S(1)}, u32[]{:S(2)}, u32[]{:S(2)}) %collective-permute-start.9) | collective-permute-done | bytes 327712 | tf_op jit(solution)/shard_map/ppermute | solution.py:837
  104.5 2.8 %collective-permute-start.10 = (bf16[1,160,512]{2,1,0:T(8,128)(2,1)S(1)}, bf16[1,160,512]{2,1,0:T(8,128)(2,1)S(1)}, u32[]{:S(2)}, u32[]{:S(2)}) collective-permute-start(bf16[1,160,512]{2,1,0:T(8,128)(2,1)S(1)} %add_convert_fusion.9), channel_id=1, source_target_pairs={{0,6},{1,7},{2,4},{3,5},{4,2},{5,3},{6,0},{7,1},{8,14},{9,15},{10,... | collective-permute-start | bytes 491528 | tf_op jit(solution)/shard_map/ppermute | solution.py:837
  108.2 3.1 %collective-permute-start.4 = (bf16[1,176,512]{2,1,0:T(8,128)(2,1)S(1)}, bf16[1,176,512]{2,1,0:T(8,128)(2,1)S(1)}, u32[]{:S(2)}, u32[]{:S(2)}) collective-permute-start(bf16[1,176,512]{2,1,0:T(8,128)(2,1)S(1)} %add_convert_fusion.5), channel_id=1, source_target_pairs={{0,1},{1,0},{2,3},{3,2},{4,5},{5,4},{6,7},{7,6},{8,9},{9,8},{10,11... | collective-permute-start | bytes 540680 | tf_op jit(solution)/shard_map/ppermute | solution.py:837
  112.2 3.1 %collective-permute-done.4 = bf16[1,176,512]{2,1,0:T(8,128)(2,1)S(1)} collective-permute-done((bf16[1,176,512]{2,1,0:T(8,128)(2,1)S(1)}, bf16[1,176,512]{2,1,0:T(8,128)(2,1)S(1)}, u32[]{:S(2)}, u32[]{:S(2)}) %collective-permute-start.4) | collective-permute-done | bytes 180256 | tf_op jit(solution)/shard_map/ppermute | solution.py:837
  115.4 2.0 %collective-permute-done.7 = bf16[1,176,512]{2,1,0:T(8,128)(2,1)S(1)} collective-permute-done((bf16[1,176,512]{2,1,0:T(8,128)(2,1)S(1)}, bf16[1,176,512]{2,1,0:T(8,128)(2,1)S(1)}, u32[]{:S(2)}, u32[]{:S(2)}) %collective-permute-start.7) | collective-permute-done | bytes 180256 | tf_op jit(solution)/shard_map/ppermute | solution.py:837
  (25 shorter events, 5.1 us)
Async XLA Ops:
  0.9 8.0 %collective-permute-start = (bf16[8,4096]{1,0:T(8,128)(2,1)S(1)}, bf16[8,4096]{1,0:T(8,128)(2,1)S(1)}, u32[]{:S(2)}, u32[]{:S(2)}) collective-permute-start(bf16[8,4096]{1,0:T(8,128)(2,1)S(1)} %get-tuple-element.50), channel_id=1, source_target_pairs={{0,8},{8,16},{16,24},{24,32},{32,40},{40,48},{48,56},{56,64},{64,7... | collective-permute-start | bytes 196616 | tf_op jit(solution)/shard_map/ppermute | solution.py:875
  2.2 6.7 %collective-permute-start.1 = (bf16[8,4096]{1,0:T(8,128)(2,1)S(1)}, bf16[8,4096]{1,0:T(8,128)(2,1)S(1)}, u32[]{:S(2)}, u32[]{:S(2)}) collective-permute-start(bf16[8,4096]{1,0:T(8,128)(2,1)S(1)} %get-tuple-element.49), channel_id=1, source_target_pairs={{8,0},{16,8},{24,16},{32,24},{40,32},{48,40},{56,48},{64,56},{72,6... | collective-permute-start | bytes 196616 | tf_op jit(solution)/shard_map/ppermute | solution.py:876
  29.6 21.1 %all-to-all-start = ((bf16[16,144,128]{2,1,0:T(8,128)(2,1)}), bf16[16,144,128]{2,1,0:T(8,128)(2,1)S(1)}, u32[]{:S(2)}, u32[]{:S(2)}) async-start(bf16[16,144,128]{2,1,0:T(8,128)(2,1)} %bitcast.19), calls=%async_computation | async-start | bytes 1179648 | tf_op jit(solution)/shard_map/all_to_all | solution.py:887
  51.6 14.4 %all-to-all-start.1 = ((bf16[16,128,128]{2,1,0:T(8,128)(2,1)}), bf16[16,128,128]{2,1,0:T(8,128)(2,1)S(1)}, u32[]{:S(2)}, u32[]{:S(2)}) async-start(bf16[16,128,128]{2,1,0:T(8,128)(2,1)} %chain.1), calls=%async_computation.1 | async-start | bytes 1048576 | tf_op jit(solution)/shard_map/all_to_all | solution.py:891
  55.2 10.8 %copy-start = (f32[512]{0:T(512)S(1)}, f32[512]{0:T(512)}, u32[]{:S(2)}) copy-start(f32[512]{0:T(512)} %param.26) | copy-start | bytes 6148
  77.2 17.6 %collective-permute-start.8 = (bf16[4,160,512]{2,1,0:T(8,128)(2,1)S(1)}, bf16[4,160,512]{2,1,0:T(8,128)(2,1)S(1)}, u32[]{:S(2)}, u32[]{:S(2)}) collective-permute-start(bf16[4,160,512]{2,1,0:T(8,128)(2,1)S(1)} %get-tuple-element.48), channel_id=1, source_target_pairs={{0,1},{1,0},{2,3},{3,2},{4,5},{5,4},{6,7},{7,6},{8,9},{9,8},{10,11... | collective-permute-start | bytes 1966088 | tf_op jit(solution)/shard_map/ppermute | solution.py:837
  80.3 18.5 %collective-permute-start.2 = (bf16[4,176,512]{2,1,0:T(8,128)(2,1)S(1)}, bf16[4,176,512]{2,1,0:T(8,128)(2,1)S(1)}, u32[]{:S(2)}, u32[]{:S(2)}) collective-permute-start(bf16[4,176,512]{2,1,0:T(8,128)(2,1)S(1)} %get-tuple-element.44), channel_id=1, source_target_pairs={{0,2},{1,3},{2,0},{3,1},{4,6},{5,7},{6,4},{7,5},{8,10},{9,11},{10,... | collective-permute-start | bytes 2162696 | tf_op jit(solution)/shard_map/ppermute | solution.py:837
  81.8 20.0 %collective-permute-start.5 = (bf16[4,176,512]{2,1,0:T(8,128)(2,1)S(1)}, bf16[4,176,512]{2,1,0:T(8,128)(2,1)S(1)}, u32[]{:S(2)}, u32[]{:S(2)}) collective-permute-start(bf16[4,176,512]{2,1,0:T(8,128)(2,1)S(1)} %get-tuple-element.46), channel_id=1, source_target_pairs={{0,6},{1,7},{2,4},{3,5},{4,2},{5,3},{6,0},{7,1},{8,14},{9,15},{10,... | collective-permute-start | bytes 2162696 | tf_op jit(solution)/shard_map/ppermute | solution.py:837
  94.9 9.6 %collective-permute-start.9 = (bf16[2,160,512]{2,1,0:T(8,128)(2,1)S(1)}, bf16[2,160,512]{2,1,0:T(8,128)(2,1)S(1)}, u32[]{:S(2)}, u32[]{:S(2)}) collective-permute-start(bf16[2,160,512]{2,1,0:T(8,128)(2,1)S(1)} %pad_maximum_fusion.3), channel_id=1, source_target_pairs={{0,2},{1,3},{2,0},{3,1},{4,6},{5,7},{6,4},{7,5},{8,10},{9,11},{10,... | collective-permute-start | bytes 983048 | tf_op jit(solution)/shard_map/ppermute | solution.py:837
  99.0 9.2 %collective-permute-start.3 = (bf16[2,176,512]{2,1,0:T(8,128)(2,1)S(1)}, bf16[2,176,512]{2,1,0:T(8,128)(2,1)S(1)}, u32[]{:S(2)}, u32[]{:S(2)}) collective-permute-start(bf16[2,176,512]{2,1,0:T(8,128)(2,1)S(1)} %pad_maximum_fusion.1), channel_id=1, source_target_pairs={{0,6},{1,7},{2,4},{3,5},{4,2},{5,3},{6,0},{7,1},{8,14},{9,15},{10,... | collective-permute-start | bytes 1081352 | tf_op jit(solution)/shard_map/ppermute | solution.py:837
  102.0 9.8 %collective-permute-start.6 = (bf16[2,176,512]{2,1,0:T(8,128)(2,1)S(1)}, bf16[2,176,512]{2,1,0:T(8,128)(2,1)S(1)}, u32[]{:S(2)}, u32[]{:S(2)}) collective-permute-start(bf16[2,176,512]{2,1,0:T(8,128)(2,1)S(1)} %pad_maximum_fusion.2), channel_id=1, source_target_pairs={{0,1},{1,0},{2,3},{3,2},{4,5},{5,4},{6,7},{7,6},{8,9},{9,8},{10,11... | collective-permute-start | bytes 1081352 | tf_op jit(solution)/shard_map/ppermute | solution.py:837
  104.5 7.6 %collective-permute-start.10 = (bf16[1,160,512]{2,1,0:T(8,128)(2,1)S(1)}, bf16[1,160,512]{2,1,0:T(8,128)(2,1)S(1)}, u32[]{:S(2)}, u32[]{:S(2)}) collective-permute-start(bf16[1,160,512]{2,1,0:T(8,128)(2,1)S(1)} %add_convert_fusion.9), channel_id=1, source_target_pairs={{0,6},{1,7},{2,4},{3,5},{4,2},{5,3},{6,0},{7,1},{8,14},{9,15},{10,... | collective-permute-start | bytes 491528 | tf_op jit(solution)/shard_map/ppermute | solution.py:837
  108.2 7.1 %collective-permute-start.4 = (bf16[1,176,512]{2,1,0:T(8,128)(2,1)S(1)}, bf16[1,176,512]{2,1,0:T(8,128)(2,1)S(1)}, u32[]{:S(2)}, u32[]{:S(2)}) collective-permute-start(bf16[1,176,512]{2,1,0:T(8,128)(2,1)S(1)} %add_convert_fusion.5), channel_id=1, source_target_pairs={{0,1},{1,0},{2,3},{3,2},{4,5},{5,4},{6,7},{7,6},{8,9},{9,8},{10,11... | collective-permute-start | bytes 540680 | tf_op jit(solution)/shard_map/ppermute | solution.py:837
  111.8 5.6 %collective-permute-start.7 = (bf16[1,176,512]{2,1,0:T(8,128)(2,1)S(1)}, bf16[1,176,512]{2,1,0:T(8,128)(2,1)S(1)}, u32[]{:S(2)}, u32[]{:S(2)}) collective-permute-start(bf16[1,176,512]{2,1,0:T(8,128)(2,1)S(1)} %add_convert_fusion.1), channel_id=1, source_target_pairs={{0,2},{1,3},{2,0},{3,1},{4,6},{5,7},{6,4},{7,5},{8,10},{9,11},{10,... | collective-permute-start | bytes 540680 | tf_op jit(solution)/shard_map/ppermute | solution.py:837

commit v7 on v6

--- a/solution.py
+++ b/solution.py
@@ -768,7 +768,7 @@
 def output(local, gate, c_maps, cols, incoming, gain, w_out):
     tokens, inner = local.shape[1:]
     state = c_maps.shape[3]
-    size = 2 * CHUNK
+    size = 4 * CHUNK
     halves = tokens // size
     pre = 2 * halves
     slab = w_out.shape[1] // PARTS

time: 119 us -> 118 us (level)
  no operation moved by 1% of the time
where the time goes in v7:
time: 118 us
  Pallas kernels  62.6 us (53%)
  starting transfers between devices  33.3 us (28%)
  waiting for transfers between devices  19.2 us (16%)
  other arithmetic  1.68 us (1%)
    pallas_call x1, Pallas kernels, front(): pl.pallas_call(front_kernel, in_specs=[here] * 4 + [there] * len(far), ou...  20.7 us
    ppermute x9, starting transfers between devices, reduced(): arrived = lax.ppermute(send, 'head', pairs)  17.6 us
    ppermute x9, waiting for transfers between devices, reduced(): arrived = lax.ppermute(send, 'head', pairs)  15.9 us
    pallas_call x1, Pallas kernels, output(): pl.pallas_call(send_kernel, grid_spec=pltpu.PrefetchScalarGridSpec(num_sc...  10.5 us
    pallas_call x1, Pallas kernels, project_gate(): pl.pallas_call(gate_kernel, grid=(PAIRS,), in_specs=paired((tokens, DEPTH...  9.8 us
    all_to_all x1, starting transfers between devices, shards(): sent = lax.all_to_all(final.reshape(count, state, tile), 'ctx', 0, 0)  9.52 us
    pallas_call x1, Pallas kernels, within(): pl.pallas_call(within_kernel, grid=(2 * chunks,), in_specs=[pl.BlockSpec(...  9.38 us
    pallas_call x1, Pallas kernels, output(): pl.pallas_call(keep_kernel, grid_spec=pltpu.PrefetchScalarGridSpec(num_sc...  5.91 us
  transfers between devices with their start and end apart: 13, of which 9 were waited for; matrix products, arithmetic and copies ran while one was open for 1% of the time, Pallas kernels for 26%

profile of v7, /device:TPU:0, one launch (start us, length us, event | category | flops | bytes accessed | tf_op | source)
XLA Modules:
  0.0 117.8 jit_solution(7508285195164267914)
XLA Ops:
  0.9 1.3 %collective-permute-start = (bf16[8,4096]{1,0:T(8,128)(2,1)S(1)}, bf16[8,4096]{1,0:T(8,128)(2,1)S(1)}, u32[]{:S(2)}, u32[]{:S(2)}) collective-permute-start(bf16[8,4096]{1,0:T(8,128)(2,1)S(1)} %get-tuple-element.50), channel_id=1, source_target_pairs={{0,8},{8,16},{16,24},{24,32},{32,40},{40,48},{48,56},{56,64},{64,7... | collective-permute-start | bytes 196616 | tf_op jit(solution)/shard_map/ppermute | solution.py:875
  2.2 1.3 %collective-permute-start.1 = (bf16[8,4096]{1,0:T(8,128)(2,1)S(1)}, bf16[8,4096]{1,0:T(8,128)(2,1)S(1)}, u32[]{:S(2)}, u32[]{:S(2)}) collective-permute-start(bf16[8,4096]{1,0:T(8,128)(2,1)S(1)} %get-tuple-element.49), channel_id=1, source_target_pairs={{8,0},{16,8},{24,16},{32,24},{40,32},{48,40},{56,48},{64,56},{72,6... | collective-permute-start | bytes 196616 | tf_op jit(solution)/shard_map/ppermute | solution.py:876
  3.5 5.4 %scale.1 = (bf16[2,512,4096]{2,1,0:T(8,128)(2,1)S(1)}, f32[512,128]{1,0:T(8,128)S(1)}) custom-call(bf16[512,4096]{1,0:T(8,128)(2,1)} %refs_1_.1, f32[1,4096]{1,0:T(1,128)} %bitcast.21), custom_call_target="tpu_custom_call" | custom-call | flops 2147483648 | bytes 8388608 | tf_op jit(solution)/shard_map/scale/pallas_call | solution.py:479
  8.9 20.7 %front.1 = (f32[2,512,512]{2,1,0:T(8,128)}, bf16[2,512,512]{2,1,0:T(8,128)(2,1)}, bf16[2,512,512]{2,1,0:T(8,128)(2,1)}, bf16[2,2,512,128]{3,2,1,0:T(8,128)(2,1)}...) custom-call(bf16[2,512,4096]{2,1,0:T(8,128)(2,1)S(1)} %get-tuple-ele, ...), custom_call_target="tpu_custom_call" | custom-call | flops 8858370048 | bytes 25165824 | tf_op jit(solution)/shard_map/front/pallas_call | solution.py:523
  29.6 9.5 %all-to-all-start = ((bf16[16,144,128]{2,1,0:T(8,128)(2,1)}), bf16[16,144,128]{2,1,0:T(8,128)(2,1)S(1)}, u32[]{:S(2)}, u32[]{:S(2)}) async-start(bf16[16,144,128]{2,1,0:T(8,128)(2,1)} %bitcast.19), calls=%async_computation | async-start | bytes 1179648 | tf_op jit(solution)/shard_map/all_to_all | solution.py:887
  39.1 9.4 %within.1.local_ref = f32[2,512,512]{2,1,0:T(8,128)} custom-call(f32[2,512,512]{2,1,0:T(8,128)} %get-tuple-element.30.direct_ref, bf16[2,512,512]{2,1,0:T(8,128)(2,1)} %get-tuple-element.31.xf_ref, bf16[2,512,512]{2,1,0:T(8,128)(2,1)} %get-tuple-element.32.xb_ref, bf16[2,2,512,128]{3,2,1,0:T(8,128)(2,1)} %get-tuple-element.33.b_ref, ...), custom_call_target="tpu_custom_call" | custom-call | flops 4294967296 | bytes 16777216 | tf_op jit(solution)/shard_map/within/pallas_call | solution.py:604
  48.5 2.2 %all-to-all-done.states_ref = bf16[16,144,128]{2,1,0:T(8,128)(2,1)S(1)} async-done(((bf16[16,144,128]{2,1,0:T(8,128)(2,1)}), bf16[16,144,128]{2,1,0:T(8,128)(2,1)S(1)}, u32[]{:S(2)}, u32[]{:S(2)}) %all-to-all-start) | async-done | bytes 589856 | tf_op jit(solution)/shard_map/all_to_all | solution.py:887
  51.6 3.6 %all-to-all-start.1 = ((bf16[16,128,128]{2,1,0:T(8,128)(2,1)}), bf16[16,128,128]{2,1,0:T(8,128)(2,1)S(1)}, u32[]{:S(2)}, u32[]{:S(2)}) async-start(bf16[16,128,128]{2,1,0:T(8,128)(2,1)} %chain.1), calls=%async_computation.1 | async-start | bytes 1048576 | tf_op jit(solution)/shard_map/all_to_all | solution.py:891
  55.2 9.8 %project_gate.1.silu_ref = f32[2,512,512]{2,1,0:T(8,128)} custom-call(bf16[512,4096]{1,0:T(8,128)(2,1)} %refs_1_.1, bf16[512,4096]{1,0:T(8,128)(2,1)} %refs_1_.1, f32[1,4096]{1,0:T(1,128)} %bitcast.23, f32[1,4096]{1,0:T(1,128)} %bitcast.24, bf16[4096,512]{1,0:T(8,128)(2,1)} %refs_5_.1, bf16[4096,512]{1,0:T(8,128)(2,1)} %refs_5_.1), custom_call_target="tpu_custom_call" | custom-call | flops 6442450944 | bytes 12582912 | tf_op jit(solution)/shard_map/project_gate/pallas_call | solution.py:233
  65.0 1.0 all-to-all-done.1
  66.0 10.5 %output_send.1 = (bf16[4,176,512]{2,1,0:T(8,128)(2,1)S(1)}, bf16[4,176,512]{2,1,0:T(8,128)(2,1)S(1)}, bf16[4,160,512]{2,1,0:T(8,128)(2,1)S(1)}, bf16[2,512,512]{2,1,0:T(8,128)(2,1)S(1)}) custom-call(s32[1]{0:T(128)} %bitcast.place_ref, f32[2,512,512]{2,1,0:T(8,128)} %within.1.local_ref, f32[2,512,512]{2,1,0:T(8,128)} %project_gate.1.silu_ref, ...), custom_call_target="tpu_custom_call" | custom-call | flops 3221225472 | bytes 14680064 | tf_op jit(solution)/shard_map/output_send/pallas_call | solution.py:781
  76.6 3.1 %collective-permute-start.8 = (bf16[4,160,512]{2,1,0:T(8,128)(2,1)S(1)}, bf16[4,160,512]{2,1,0:T(8,128)(2,1)S(1)}, u32[]{:S(2)}, u32[]{:S(2)}) collective-permute-start(bf16[4,160,512]{2,1,0:T(8,128)(2,1)S(1)} %get-tuple-element.48), channel_id=1, source_target_pairs={{0,1},{1,0},{2,3},{3,2},{4,5},{5,4},{6,7},{7,6},{8,9},{9,8},{10,11... | collective-permute-start | bytes 1966088 | tf_op jit(solution)/shard_map/ppermute | solution.py:837
  79.7 1.5 %collective-permute-start.2 = (bf16[4,176,512]{2,1,0:T(8,128)(2,1)S(1)}, bf16[4,176,512]{2,1,0:T(8,128)(2,1)S(1)}, u32[]{:S(2)}, u32[]{:S(2)}) collective-permute-start(bf16[4,176,512]{2,1,0:T(8,128)(2,1)S(1)} %get-tuple-element.44), channel_id=1, source_target_pairs={{0,2},{1,3},{2,0},{3,1},{4,6},{5,7},{6,4},{7,5},{8,10},{9,11},{10,... | collective-permute-start | bytes 2162696 | tf_op jit(solution)/shard_map/ppermute | solution.py:837
  81.2 2.1 %collective-permute-start.5 = (bf16[4,176,512]{2,1,0:T(8,128)(2,1)S(1)}, bf16[4,176,512]{2,1,0:T(8,128)(2,1)S(1)}, u32[]{:S(2)}, u32[]{:S(2)}) collective-permute-start(bf16[4,176,512]{2,1,0:T(8,128)(2,1)S(1)} %get-tuple-element.46), channel_id=1, source_target_pairs={{0,6},{1,7},{2,4},{3,5},{4,2},{5,3},{6,0},{7,1},{8,14},{9,15},{10,... | collective-permute-start | bytes 2162696 | tf_op jit(solution)/shard_map/ppermute | solution.py:837
  83.3 5.9 %output_keep.1 = (f32[4,176,512]{2,1,0:T(8,128)S(1)}, f32[4,176,512]{2,1,0:T(8,128)S(1)}, f32[4,160,512]{2,1,0:T(8,128)S(1)}) custom-call(s32[1]{0:T(128)} %bitcast.place_ref, bf16[2,512,512]{2,1,0:T(8,128)(2,1)S(1)} %get-tuple-element.42.normed_ref, bf16[512,4096]{1,0:T(8,128)(2,1)} %wmir_ref.3, bf16[512,4096]{1,0:T(8,128)(2,1)} %wmir_ref.3), custom_call_target="tpu_custom_call" | custom-call | flops 3221225472 | bytes 10485760 | tf_op jit(solution)/shard_map/output_keep/pallas_call | solution.py:812
  89.2 4.9 %collective-permute-done.8 = bf16[4,160,512]{2,1,0:T(8,128)(2,1)S(1)} collective-permute-done((bf16[4,160,512]{2,1,0:T(8,128)(2,1)S(1)}, bf16[4,160,512]{2,1,0:T(8,128)(2,1)S(1)}, u32[]{:S(2)}, u32[]{:S(2)}) %collective-permute-start.8) | collective-permute-done | bytes 655392 | tf_op jit(solution)/shard_map/ppermute | solution.py:837
  94.3 1.6 %collective-permute-start.9 = (bf16[2,160,512]{2,1,0:T(8,128)(2,1)S(1)}, bf16[2,160,512]{2,1,0:T(8,128)(2,1)S(1)}, u32[]{:S(2)}, u32[]{:S(2)}) collective-permute-start(bf16[2,160,512]{2,1,0:T(8,128)(2,1)S(1)} %pad_maximum_fusion.3), channel_id=1, source_target_pairs={{0,2},{1,3},{2,0},{3,1},{4,6},{5,7},{6,4},{7,5},{8,10},{9,11},{10,... | collective-permute-start | bytes 983048 | tf_op jit(solution)/shard_map/ppermute | solution.py:837
  95.9 2.3 %collective-permute-done.2 = bf16[4,176,512]{2,1,0:T(8,128)(2,1)S(1)} collective-permute-done((bf16[4,176,512]{2,1,0:T(8,128)(2,1)S(1)}, bf16[4,176,512]{2,1,0:T(8,128)(2,1)S(1)}, u32[]{:S(2)}, u32[]{:S(2)}) %collective-permute-start.2) | collective-permute-done | bytes 720928 | tf_op jit(solution)/shard_map/ppermute | solution.py:837
  98.3 2.9 %collective-permute-start.3 = (bf16[2,176,512]{2,1,0:T(8,128)(2,1)S(1)}, bf16[2,176,512]{2,1,0:T(8,128)(2,1)S(1)}, u32[]{:S(2)}, u32[]{:S(2)}) collective-permute-start(bf16[2,176,512]{2,1,0:T(8,128)(2,1)S(1)} %pad_maximum_fusion.1), channel_id=1, source_target_pairs={{0,6},{1,7},{2,4},{3,5},{4,2},{5,3},{6,0},{7,1},{8,14},{9,15},{10,... | collective-permute-start | bytes 1081352 | tf_op jit(solution)/shard_map/ppermute | solution.py:837
  101.5 2.4 %collective-permute-done.9 = bf16[2,160,512]{2,1,0:T(8,128)(2,1)S(1)} collective-permute-done((bf16[2,160,512]{2,1,0:T(8,128)(2,1)S(1)}, bf16[2,160,512]{2,1,0:T(8,128)(2,1)S(1)}, u32[]{:S(2)}, u32[]{:S(2)}) %collective-permute-start.9) | collective-permute-done | bytes 327712 | tf_op jit(solution)/shard_map/ppermute | solution.py:837
  103.9 2.8 %collective-permute-start.10 = (bf16[1,160,512]{2,1,0:T(8,128)(2,1)S(1)}, bf16[1,160,512]{2,1,0:T(8,128)(2,1)S(1)}, u32[]{:S(2)}, u32[]{:S(2)}) collective-permute-start(bf16[1,160,512]{2,1,0:T(8,128)(2,1)S(1)} %add_convert_fusion.9), channel_id=1, source_target_pairs={{0,6},{1,7},{2,4},{3,5},{4,2},{5,3},{6,0},{7,1},{8,14},{9,15},{10,... | collective-permute-start | bytes 491528 | tf_op jit(solution)/shard_map/ppermute | solution.py:837
  107.6 3.2 %collective-permute-start.4 = (bf16[1,176,512]{2,1,0:T(8,128)(2,1)S(1)}, bf16[1,176,512]{2,1,0:T(8,128)(2,1)S(1)}, u32[]{:S(2)}, u32[]{:S(2)}) collective-permute-start(bf16[1,176,512]{2,1,0:T(8,128)(2,1)S(1)} %add_convert_fusion.5), channel_id=1, source_target_pairs={{0,1},{1,0},{2,3},{3,2},{4,5},{5,4},{6,7},{7,6},{8,9},{9,8},{10,11... | collective-permute-start | bytes 540680 | tf_op jit(solution)/shard_map/ppermute | solution.py:837
  111.7 3.0 %collective-permute-done.4 = bf16[1,176,512]{2,1,0:T(8,128)(2,1)S(1)} collective-permute-done((bf16[1,176,512]{2,1,0:T(8,128)(2,1)S(1)}, bf16[1,176,512]{2,1,0:T(8,128)(2,1)S(1)}, u32[]{:S(2)}, u32[]{:S(2)}) %collective-permute-start.4) | collective-permute-done | bytes 180256 | tf_op jit(solution)/shard_map/ppermute | solution.py:837
  114.7 2.1 %collective-permute-done.7 = bf16[1,176,512]{2,1,0:T(8,128)(2,1)S(1)} collective-permute-done((bf16[1,176,512]{2,1,0:T(8,128)(2,1)S(1)}, bf16[1,176,512]{2,1,0:T(8,128)(2,1)S(1)}, u32[]{:S(2)}, u32[]{:S(2)}) %collective-permute-start.7) | collective-permute-done | bytes 180256 | tf_op jit(solution)/shard_map/ppermute | solution.py:837
  (25 shorter events, 5.1 us)
Async XLA Ops:
  0.9 8.0 %collective-permute-start = (bf16[8,4096]{1,0:T(8,128)(2,1)S(1)}, bf16[8,4096]{1,0:T(8,128)(2,1)S(1)}, u32[]{:S(2)}, u32[]{:S(2)}) collective-permute-start(bf16[8,4096]{1,0:T(8,128)(2,1)S(1)} %get-tuple-element.50), channel_id=1, source_target_pairs={{0,8},{8,16},{16,24},{24,32},{32,40},{40,48},{48,56},{56,64},{64,7... | collective-permute-start | bytes 196616 | tf_op jit(solution)/shard_map/ppermute | solution.py:875
  2.2 6.7 %collective-permute-start.1 = (bf16[8,4096]{1,0:T(8,128)(2,1)S(1)}, bf16[8,4096]{1,0:T(8,128)(2,1)S(1)}, u32[]{:S(2)}, u32[]{:S(2)}) collective-permute-start(bf16[8,4096]{1,0:T(8,128)(2,1)S(1)} %get-tuple-element.49), channel_id=1, source_target_pairs={{8,0},{16,8},{24,16},{32,24},{40,32},{48,40},{56,48},{64,56},{72,6... | collective-permute-start | bytes 196616 | tf_op jit(solution)/shard_map/ppermute | solution.py:876
  29.6 21.1 %all-to-all-start = ((bf16[16,144,128]{2,1,0:T(8,128)(2,1)}), bf16[16,144,128]{2,1,0:T(8,128)(2,1)S(1)}, u32[]{:S(2)}, u32[]{:S(2)}) async-start(bf16[16,144,128]{2,1,0:T(8,128)(2,1)} %bitcast.19), calls=%async_computation | async-start | bytes 1179648 | tf_op jit(solution)/shard_map/all_to_all | solution.py:887
  51.6 14.4 %all-to-all-start.1 = ((bf16[16,128,128]{2,1,0:T(8,128)(2,1)}), bf16[16,128,128]{2,1,0:T(8,128)(2,1)S(1)}, u32[]{:S(2)}, u32[]{:S(2)}) async-start(bf16[16,128,128]{2,1,0:T(8,128)(2,1)} %chain.1), calls=%async_computation.1 | async-start | bytes 1048576 | tf_op jit(solution)/shard_map/all_to_all | solution.py:891
  55.2 10.8 %copy-start = (f32[512]{0:T(512)S(1)}, f32[512]{0:T(512)}, u32[]{:S(2)}) copy-start(f32[512]{0:T(512)} %param.26) | copy-start | bytes 6148
  76.6 17.6 %collective-permute-start.8 = (bf16[4,160,512]{2,1,0:T(8,128)(2,1)S(1)}, bf16[4,160,512]{2,1,0:T(8,128)(2,1)S(1)}, u32[]{:S(2)}, u32[]{:S(2)}) collective-permute-start(bf16[4,160,512]{2,1,0:T(8,128)(2,1)S(1)} %get-tuple-element.48), channel_id=1, source_target_pairs={{0,1},{1,0},{2,3},{3,2},{4,5},{5,4},{6,7},{7,6},{8,9},{9,8},{10,11... | collective-permute-start | bytes 1966088 | tf_op jit(solution)/shard_map/ppermute | solution.py:837
  79.7 18.5 %collective-permute-start.2 = (bf16[4,176,512]{2,1,0:T(8,128)(2,1)S(1)}, bf16[4,176,512]{2,1,0:T(8,128)(2,1)S(1)}, u32[]{:S(2)}, u32[]{:S(2)}) collective-permute-start(bf16[4,176,512]{2,1,0:T(8,128)(2,1)S(1)} %get-tuple-element.44), channel_id=1, source_target_pairs={{0,2},{1,3},{2,0},{3,1},{4,6},{5,7},{6,4},{7,5},{8,10},{9,11},{10,... | collective-permute-start | bytes 2162696 | tf_op jit(solution)/shard_map/ppermute | solution.py:837
  81.2 20.0 %collective-permute-start.5 = (bf16[4,176,512]{2,1,0:T(8,128)(2,1)S(1)}, bf16[4,176,512]{2,1,0:T(8,128)(2,1)S(1)}, u32[]{:S(2)}, u32[]{:S(2)}) collective-permute-start(bf16[4,176,512]{2,1,0:T(8,128)(2,1)S(1)} %get-tuple-element.46), channel_id=1, source_target_pairs={{0,6},{1,7},{2,4},{3,5},{4,2},{5,3},{6,0},{7,1},{8,14},{9,15},{10,... | collective-permute-start | bytes 2162696 | tf_op jit(solution)/shard_map/ppermute | solution.py:837
  94.3 9.6 %collective-permute-start.9 = (bf16[2,160,512]{2,1,0:T(8,128)(2,1)S(1)}, bf16[2,160,512]{2,1,0:T(8,128)(2,1)S(1)}, u32[]{:S(2)}, u32[]{:S(2)}) collective-permute-start(bf16[2,160,512]{2,1,0:T(8,128)(2,1)S(1)} %pad_maximum_fusion.3), channel_id=1, source_target_pairs={{0,2},{1,3},{2,0},{3,1},{4,6},{5,7},{6,4},{7,5},{8,10},{9,11},{10,... | collective-permute-start | bytes 983048 | tf_op jit(solution)/shard_map/ppermute | solution.py:837
  98.3 9.1 %collective-permute-start.3 = (bf16[2,176,512]{2,1,0:T(8,128)(2,1)S(1)}, bf16[2,176,512]{2,1,0:T(8,128)(2,1)S(1)}, u32[]{:S(2)}, u32[]{:S(2)}) collective-permute-start(bf16[2,176,512]{2,1,0:T(8,128)(2,1)S(1)} %pad_maximum_fusion.1), channel_id=1, source_target_pairs={{0,6},{1,7},{2,4},{3,5},{4,2},{5,3},{6,0},{7,1},{8,14},{9,15},{10,... | collective-permute-start | bytes 1081352 | tf_op jit(solution)/shard_map/ppermute | solution.py:837
  101.4 9.9 %collective-permute-start.6 = (bf16[2,176,512]{2,1,0:T(8,128)(2,1)S(1)}, bf16[2,176,512]{2,1,0:T(8,128)(2,1)S(1)}, u32[]{:S(2)}, u32[]{:S(2)}) collective-permute-start(bf16[2,176,512]{2,1,0:T(8,128)(2,1)S(1)} %pad_maximum_fusion.2), channel_id=1, source_target_pairs={{0,1},{1,0},{2,3},{3,2},{4,5},{5,4},{6,7},{7,6},{8,9},{9,8},{10,11... | collective-permute-start | bytes 1081352 | tf_op jit(solution)/shard_map/ppermute | solution.py:837
  103.9 7.7 %collective-permute-start.10 = (bf16[1,160,512]{2,1,0:T(8,128)(2,1)S(1)}, bf16[1,160,512]{2,1,0:T(8,128)(2,1)S(1)}, u32[]{:S(2)}, u32[]{:S(2)}) collective-permute-start(bf16[1,160,512]{2,1,0:T(8,128)(2,1)S(1)} %add_convert_fusion.9), channel_id=1, source_target_pairs={{0,6},{1,7},{2,4},{3,5},{4,2},{5,3},{6,0},{7,1},{8,14},{9,15},{10,... | collective-permute-start | bytes 491528 | tf_op jit(solution)/shard_map/ppermute | solution.py:837
  107.6 7.1 %collective-permute-start.4 = (bf16[1,176,512]{2,1,0:T(8,128)(2,1)S(1)}, bf16[1,176,512]{2,1,0:T(8,128)(2,1)S(1)}, u32[]{:S(2)}, u32[]{:S(2)}) collective-permute-start(bf16[1,176,512]{2,1,0:T(8,128)(2,1)S(1)} %add_convert_fusion.5), channel_id=1, source_target_pairs={{0,1},{1,0},{2,3},{3,2},{4,5},{5,4},{6,7},{7,6},{8,9},{9,8},{10,11... | collective-permute-start | bytes 540680 | tf_op jit(solution)/shard_map/ppermute | solution.py:837
  111.3 5.6 %collective-permute-start.7 = (bf16[1,176,512]{2,1,0:T(8,128)(2,1)S(1)}, bf16[1,176,512]{2,1,0:T(8,128)(2,1)S(1)}, u32[]{:S(2)}, u32[]{:S(2)}) collective-permute-start(bf16[1,176,512]{2,1,0:T(8,128)(2,1)S(1)} %add_convert_fusion.1), channel_id=1, source_target_pairs={{0,2},{1,3},{2,0},{3,1},{4,6},{5,7},{6,4},{7,5},{8,10},{9,11},{10,... | collective-permute-start | bytes 540680 | tf_op jit(solution)/shard_map/ppermute | solution.py:837
